TPU v7x, 32 devices: a whole 2x2x4 slice. The times are simulated.
32 devices in a mesh: cols: 16 (over z, y, core), fsdp: 2 (over x).
Axes of the slice: x: 2, y: 2, z: 4, core: 2. Of those that a mesh axis runs over, the one named last changes fastest.
Arguments:
- alignment: bfloat16 [2, 2, 4, 1024, 768], P(None, 'fsdp', None, 'cols'), may hold values from -6 to 6
- cotangent: bfloat16 [2, 2, 4, 1024, 768], P(None, 'fsdp', None, 'cols'), may hold values from -6 to 6
- row_counts: int32 [2, 2], P(None, 'fsdp'), may hold values from 1 to 4, as said below
- band_reach: int32 [2, 2, 2, 1024], P(None, 'fsdp', None, 'cols'), may hold values from 0 to 32
- master_weights: float32 [12288, 768], P(('cols', 'fsdp'))
- weight_moment: float32 [12288, 768], P(('cols', 'fsdp'))
- weight_square: float32 [12288, 768], P(('cols', 'fsdp')), as said below
- norm_gains: float32 [2304], P(('cols', 'fsdp')), may hold values from 0.5 to 1.5
- gain_moment: float32 [2304], P(('cols', 'fsdp'))
- gain_square: float32 [2304], P(('cols', 'fsdp')), as said below
Outputs:
- block_output: bfloat16 [2, 2, 4, 1024, 768], P(None, 'fsdp', None, 'cols')
- input_grad: bfloat16 [2, 2, 4, 1024, 768], P(None, 'fsdp', None, 'cols')
- new_weights: float32 [12288, 768], P(('cols', 'fsdp'))
- new_moment: float32 [12288, 768], P(('cols', 'fsdp'))
- new_square: float32 [12288, 768], P(('cols', 'fsdp'))
- weight_copies: bfloat16 [12288, 768], P(('cols', 'fsdp'))
- new_gains: float32 [2304], P(('cols', 'fsdp'))
- new_gain_moment: float32 [2304], P(('cols', 'fsdp'))
- new_gain_square: float32 [2304], P(('cols', 'fsdp'))
Inputs may be any that keep to these rules, and one draw needn't show every extreme that they name: `row_counts`: every alignment holds at least one live sequence. `weight_square`: positive. `gain_square`: positive.
All inputs are finite; a program needn't handle non-finite values.
Results may differ from a plain program's by a relative error of at most 0.017.
Values may be sent and summed in bfloat16 or wider, within the bound.
No kernel may reach another device: no remote copies, remote signals or barrier semaphores. Data moves between devices by JAX's collectives and lax.ppermute only.
A program may use at most 240 MiB of HBM per device.

v0:
```python
from functools import partial

import jax
import jax.numpy as jnp
from jax import lax
from jax.sharding import PartitionSpec as P

D = 768
H = 12
DH = 64
FF = 3072
NMAT = 16
ROWS = 4
CB = 64
HALO = 32
MB = 2


EPS = 1e-05
BETA_ONE = 0.9
BETA_TWO = 0.999
ADAM_EPS = 1e-08
DECAY = 0.01
RATE_GAIN = 0.3
STEP_NUMBER = 10.0
MASKED = -1e30


def extended(block, sides, width):
    for axis, dim in sides:
        count = lax.axis_size(axis)
        forward = [(i, i + 1) for i in range(count - 1)]
        backward = [(target, source) for source, target in forward]
        low = lax.ppermute(
            lax.slice_in_dim(block, block.shape[dim] - width, None, axis=dim), axis, forward
        )
        high = lax.ppermute(lax.slice_in_dim(block, 0, width, axis=dim), axis, backward)
        block = jnp.concatenate([low, block, high], axis=dim)
    return block


def norm_forward(values, norm_gain):
    center = values - jnp.mean(values, axis=-1, keepdims=True)
    spread = lax.rsqrt(jnp.mean(center * center, axis=-1, keepdims=True) + EPS)
    scaled = center * spread
    return (scaled * norm_gain, scaled, spread)


def norm_backward(upward, scaled, spread, norm_gain):
    weighted = upward * norm_gain
    gain_grad = jnp.sum(upward * scaled, axis=(0, 1))
    result = spread * (
        weighted
        - jnp.mean(weighted, axis=-1, keepdims=True)
        - scaled * jnp.mean(weighted * scaled, axis=-1, keepdims=True)
    )
    return (result, gain_grad)


def soft_stats(scores):
    row_top = jnp.max(scores, axis=-1, keepdims=True)
    return row_top + jnp.log(jnp.sum(jnp.exp(scores - row_top), axis=-1, keepdims=True))


def adamw(master, moment, square, grad_total, rate, decay, steps_done):
    moment_new = BETA_ONE * moment + (1.0 - BETA_ONE) * grad_total
    square_new = BETA_TWO * square + (1.0 - BETA_TWO) * grad_total * grad_total
    moment_fix = 1.0 - BETA_ONE**steps_done
    square_fix = 1.0 - BETA_TWO**steps_done
    update = moment_new / moment_fix / (jnp.sqrt(square_new / square_fix) + ADAM_EPS)
    return (master - rate * (update + decay * master), moment_new, square_new)


def micro_pass(
    block_input, block_cot, present_count, reach_bounds, weight_matrices, norm_gain_values
):
    f32 = jnp.float32
    low_type = jnp.bfloat16
    rounded = weight_matrices.reshape(NMAT, D, D)
    gain_rows = norm_gain_values.astype(f32).reshape(3, D)
    block_input = block_input.astype(f32)
    present_mask = (jnp.arange(ROWS, dtype=jnp.int32) < present_count).astype(f32)
    live_rows = present_mask[:, None, None]
    col_live = present_mask > 0
    row_scale = DH ** (-0.5) * lax.rsqrt(present_count.astype(f32))
    col_scale = DH ** (-0.5)
    extent = CB + 2 * HALO
    col_total = CB * lax.axis_size("cols")
    first_col = lax.axis_index("cols") * CB
    query_pos = first_col + jnp.arange(CB, dtype=jnp.int32)
    key_pos = first_col - HALO + jnp.arange(extent, dtype=jnp.int32)
    lowest = query_pos - reach_bounds[0]
    highest = query_pos + reach_bounds[1]
    allowed = (key_pos[None, :] >= lowest[:, None]) & (key_pos[None, :] <= highest[:, None])
    allowed = allowed & (key_pos[None, :] >= 0) & (key_pos[None, :] < col_total)
    normed_one, scaled_one, spread_one = norm_forward(block_input, gain_rows[0])
    normed_one = normed_one.astype(low_type)
    queries = jnp.einsum("rcd,de->rce", normed_one, rounded[0], preferred_element_type=f32).astype(
        low_type
    )
    queries = queries * live_rows.astype(low_type)
    pair_low = jnp.einsum(
        "rcd,jde->jrce", normed_one, rounded[1:3], preferred_element_type=f32
    ).astype(low_type)
    pair_ext = extended(pair_low, (("cols", 2),), HALO)
    query_heads = queries.reshape(ROWS, CB, H, DH)
    key_heads = pair_ext[0].reshape(ROWS, extent, H, DH)
    value_heads = pair_ext[1].reshape(ROWS, extent, H, DH)

    def row_scores():
        raw_scores = (
            jnp.einsum("rchd,rkhd->hck", query_heads, key_heads, preferred_element_type=f32)
            * row_scale
        )
        return jnp.where(allowed[None], raw_scores, MASKED)

    scores_one = row_scores()
    log_one = soft_stats(scores_one)
    attn_one = jnp.exp(scores_one - log_one)
    mixed_one = jnp.einsum(
        "hck,rkhd->rchd", attn_one.astype(low_type), value_heads, preferred_element_type=f32
    )
    mixed_one = mixed_one.reshape(ROWS, CB, D).astype(low_type)
    after_rows = block_input + jnp.einsum(
        "rcd,de->rce", mixed_one, rounded[3], preferred_element_type=f32
    )
    normed_two, scaled_two, spread_two = norm_forward(after_rows, gain_rows[1])
    normed_two = normed_two.astype(low_type)
    col_proj = jnp.einsum(
        "rcd,jde->jrce", normed_two, rounded[4:7], preferred_element_type=f32
    ).astype(low_type)
    col_heads = col_proj.reshape(3, ROWS, CB, H, DH)

    def col_scores():
        raw_scores = (
            jnp.einsum("rchd,schd->chrs", col_heads[0], col_heads[1], preferred_element_type=f32)
            * col_scale
        )
        return jnp.where(col_live[None, None, None, :], raw_scores, MASKED)

    scores_two = col_scores()
    log_two = soft_stats(scores_two)
    attn_two = jnp.exp(scores_two - log_two)
    mixed_two = jnp.einsum(
        "chrs,schd->rchd", attn_two.astype(low_type), col_heads[2], preferred_element_type=f32
    )
    mixed_two = mixed_two.reshape(ROWS, CB, D).astype(low_type)
    after_cols = after_rows + jnp.einsum(
        "rcd,de->rce", mixed_two, rounded[7], preferred_element_type=f32
    )
    normed_three, scaled_three, spread_three = norm_forward(after_cols, gain_rows[2])
    normed_three = normed_three.astype(low_type)
    fold_count = FF // D
    up_blocks = rounded[8 : 8 + fold_count]
    down_matrix = rounded[8 + fold_count :].reshape(FF, D)
    hidden = jnp.einsum(
        "rcd,jde->rcje", normed_three, up_blocks, preferred_element_type=f32
    ).reshape(ROWS, CB, FF)
    active, gelu_pull = jax.vjp(partial(jax.nn.gelu, approximate=False), hidden)
    active_low = active.astype(low_type)
    result = after_cols + jnp.einsum(
        "rcf,fe->rce", active_low, down_matrix, preferred_element_type=f32
    )
    block_out = (result * live_rows).astype(low_type)
    grad_three = block_cot.astype(f32) * live_rows
    grad_low = grad_three.astype(low_type)
    down_grad = jnp.einsum("rcf,rce->fe", active_low, grad_low, preferred_element_type=f32)
    active_grad = jnp.einsum("rce,fe->rcf", grad_low, down_matrix, preferred_element_type=f32)
    hidden_grad = gelu_pull(active_grad)[0].astype(low_type).reshape(ROWS, CB, fold_count, D)
    up_grad = jnp.einsum("rcd,rcje->jde", normed_three, hidden_grad, preferred_element_type=f32)
    normed_grad = jnp.einsum("rcje,jde->rcd", hidden_grad, up_blocks, preferred_element_type=f32)
    norm_part, gain_three = norm_backward(normed_grad, scaled_three, spread_three, gain_rows[2])
    grad_two = grad_three + norm_part
    grad_low = grad_two.astype(low_type)
    out_two_grad = jnp.einsum("rcd,rce->de", mixed_two, grad_low, preferred_element_type=f32)
    mixed_grad = jnp.einsum("rce,de->rcd", grad_low, rounded[7], preferred_element_type=f32).astype(
        low_type
    )
    mixed_grad = mixed_grad.reshape(ROWS, CB, H, DH)
    attn_two = jnp.exp(col_scores() - log_two)
    attn_grad = jnp.einsum("rchd,schd->chrs", mixed_grad, col_heads[2], preferred_element_type=f32)
    value_grad = jnp.einsum(
        "chrs,rchd->schd", attn_two.astype(low_type), mixed_grad, preferred_element_type=f32
    )
    score_grad = (
        attn_two * (attn_grad - jnp.sum(attn_two * attn_grad, axis=-1, keepdims=True))
    ).astype(low_type)
    query_grad = (
        jnp.einsum("chrs,schd->rchd", score_grad, col_heads[1], preferred_element_type=f32)
        * col_scale
    )
    key_grad = (
        jnp.einsum("chrs,rchd->schd", score_grad, col_heads[0], preferred_element_type=f32)
        * col_scale
    )
    col_grads = (
        jnp.stack([query_grad, key_grad, value_grad]).astype(low_type).reshape(3, ROWS, CB, D)
    )
    col_proj_grad = jnp.einsum("rcd,jrce->jde", normed_two, col_grads, preferred_element_type=f32)
    normed_grad = jnp.einsum("jrce,jde->rcd", col_grads, rounded[4:7], preferred_element_type=f32)
    norm_part, gain_two = norm_backward(normed_grad, scaled_two, spread_two, gain_rows[1])
    grad_one = grad_two + norm_part
    grad_low = grad_one.astype(low_type)
    out_one_grad = jnp.einsum("rcd,rce->de", mixed_one, grad_low, preferred_element_type=f32)
    mixed_grad = jnp.einsum("rce,de->rcd", grad_low, rounded[3], preferred_element_type=f32).astype(
        low_type
    )
    mixed_grad = mixed_grad.reshape(ROWS, CB, H, DH)
    attn_one = jnp.exp(row_scores() - log_one)
    attn_grad = jnp.einsum("rchd,rkhd->hck", mixed_grad, value_heads, preferred_element_type=f32)
    value_ext_grad = jnp.einsum(
        "hck,rchd->rkhd", attn_one.astype(low_type), mixed_grad, preferred_element_type=f32
    )
    score_grad = (
        attn_one * (attn_grad - jnp.sum(attn_one * attn_grad, axis=-1, keepdims=True))
    ).astype(low_type)
    query_grad = (
        jnp.einsum("hck,rkhd->rchd", score_grad, key_heads, preferred_element_type=f32) * row_scale
    )
    query_grad = (query_grad.reshape(ROWS, CB, D) * live_rows).astype(low_type)
    key_ext_grad = (
        jnp.einsum("hck,rchd->rkhd", score_grad, query_heads, preferred_element_type=f32)
        * row_scale
    )
    ext_grads = jnp.stack([key_ext_grad, value_ext_grad]).reshape(2, ROWS, extent, D)
    rim_grads = jnp.concatenate([ext_grads[:, :, :HALO], ext_grads[:, :, HALO + CB :]], axis=2)
    arrived = extended(rim_grads.astype(jnp.bfloat16), (("cols", 2),), HALO).astype(rim_grads.dtype)
    own_part = ext_grads[:, :, HALO : HALO + CB]
    own_part = own_part + jnp.pad(arrived[:, :, :HALO], ((0, 0), (0, 0), (0, CB - HALO), (0, 0)))
    own_part = own_part + jnp.pad(
        arrived[:, :, 3 * HALO :], ((0, 0), (0, 0), (CB - HALO, 0), (0, 0))
    )
    row_grads = jnp.concatenate([query_grad[None], own_part.astype(low_type)], axis=0)
    row_proj_grad = jnp.einsum("rcd,jrce->jde", normed_one, row_grads, preferred_element_type=f32)
    normed_grad = jnp.einsum("jrce,jde->rcd", row_grads, rounded[0:3], preferred_element_type=f32)
    norm_part, gain_one = norm_backward(normed_grad, scaled_one, spread_one, gain_rows[0])
    block_grad = (grad_one + norm_part).astype(low_type)
    weight_grad = jnp.concatenate(
        [
            row_proj_grad,
            out_one_grad[None],
            col_proj_grad,
            out_two_grad[None],
            up_grad,
            down_grad.reshape(fold_count, D, D),
        ],
        axis=0,
    )
    gain_grad = jnp.concatenate([gain_one, gain_two, gain_three])
    return (block_out, block_grad, weight_grad.reshape(NMAT * D, D), gain_grad)


def per_device(
    alignment,
    cotangent,
    row_counts,
    band_reach,
    master_weights,
    weight_moment,
    weight_square,
    norm_gains,
    gain_moment,
    gain_square,
):
    weight_low = master_weights.astype(jnp.bfloat16)
    gain_low = norm_gains.astype(jnp.bfloat16)
    weight_total = jnp.zeros((NMAT * D, D), jnp.float32)
    gain_total = jnp.zeros((3 * D,), jnp.float32)
    outputs = []
    input_grads = []
    for micro_step in range(MB):
        full_pair = (
            lax.all_gather(weight_low, ("cols", "fsdp"), axis=0, tiled=True),
            lax.all_gather(gain_low, ("cols", "fsdp"), axis=0, tiled=True),
        )
        block_out, block_grad, weight_grad, gain_grad = micro_pass(
            alignment[micro_step, 0],
            cotangent[micro_step, 0],
            row_counts[micro_step, 0],
            band_reach[micro_step, 0],
            full_pair[0],
            full_pair[1],
        )
        weight_total = weight_total + weight_grad
        gain_total = gain_total + gain_grad
        outputs.append(block_out)
        input_grads.append(block_grad)
    weight_total, gain_total = (
        lax.psum_scatter(weight_total, ("cols", "fsdp"), scatter_dimension=0, tiled=True),
        lax.psum_scatter(gain_total, ("cols", "fsdp"), scatter_dimension=0, tiled=True),
    )
    rate_matrix = D ** (-0.5)
    new_weights, new_moment, new_square = adamw(
        master_weights, weight_moment, weight_square, weight_total, rate_matrix, DECAY, STEP_NUMBER
    )
    new_gains, new_gain_moment, new_gain_square = adamw(
        norm_gains, gain_moment, gain_square, gain_total, RATE_GAIN, 0.0, STEP_NUMBER
    )
    block_output = jnp.stack(outputs)[:, None]
    input_grad = jnp.stack(input_grads)[:, None]
    return (
        block_output,
        input_grad,
        new_weights,
        new_moment,
        new_square,
        new_weights.astype(jnp.bfloat16),
        new_gains,
        new_gain_moment,
        new_gain_square,
    )


def solution(mesh):
    in_specs = (
        P(None, "fsdp", None, "cols", None),
        P(None, "fsdp", None, "cols", None),
        P(None, "fsdp"),
        P(None, "fsdp", None, "cols"),
        P(("cols", "fsdp"), None),
        P(("cols", "fsdp"), None),
        P(("cols", "fsdp"), None),
        P(("cols", "fsdp")),
        P(("cols", "fsdp")),
        P(("cols", "fsdp")),
    )
    out_specs = (
        P(None, "fsdp", None, "cols", None),
        P(None, "fsdp", None, "cols", None),
        P(("cols", "fsdp"), None),
        P(("cols", "fsdp"), None),
        P(("cols", "fsdp"), None),
        P(("cols", "fsdp"), None),
        P(("cols", "fsdp")),
        P(("cols", "fsdp")),
        P(("cols", "fsdp")),
    )
    return jax.shard_map(
        per_device, mesh=mesh, in_specs=in_specs, out_specs=out_specs, check_vma=False
    )
```

profile of v0, /device:TPU:0, one launch (start us, length us, event | category | flops | bytes accessed | tf_op | source)
XLA Modules:
  0.0 933.2 jit_solution(3368442752547443402)
XLA Ops:
  13.2 43.0 %all-reduce.2 = bf16[2304]{0:T(1024)(128)(2,1)S(1)} all-reduce(bf16[2304]{0:T(1024)(128)(2,1)S(1)} %dynamic-update-slice), channel_id=1, replica_groups=mesh['cols'=16,'fsdp'=2] {'cols','fsdp'}, use_global_device_ids=true, to_apply=%add.2 | all-reduce | flops 2304 | bytes 9216
  62.8 77.2 %all-gather.2.cloned.1.call-done = bf16[12288,768]{1,0:T(8,128)(2,1)} async-done(((bf16[384,768]{1,0:T(8,128)(2,1)}), bf16[12288,768]{1,0:T(8,128)(2,1)}) %all-gather.2.cloned.1.call-update) | async-done | bytes 18874384 | tf_op jit(solution)/shard_map/all_gather | solution.py:273
  153.5 6.5 fusion.289
  171.2 4.8 slice.277
  176.0 6.7 copy.163
  242.6 4.5 fusion.166
  247.2 6.3 fusion.165
  253.5 7.9 fusion.11
  261.4 7.5 fusion.8
  268.9 6.8 fusion.5
  275.8 4.5 add_convert_fusion
  280.3 5.2 fusion.91
  285.5 7.7 fusion.4
  366.1 4.6 multiply_reduce_fusion.5
  387.7 6.7 multiply_bitcast_fusion.1
  394.4 6.7 multiply_bitcast_fusion
  414.3 6.4 multiply_bitcast_fusion.3
  420.8 6.5 multiply_bitcast_fusion.2
  469.4 4.3 collective-permute-start.6
  480.0 4.2 bitcast_dynamic-update-slice_fusion.5
  486.3 4.2 bitcast_dynamic-update-slice_fusion.4
  492.5 5.1 bitcast_dynamic-update-slice_fusion
  497.6 4.1 bitcast_dynamic-update-slice_fusion.7
  503.8 4.2 bitcast_dynamic-update-slice_fusion.6
  510.0 5.1 bitcast_dynamic-update-slice_fusion.1
  515.1 5.3 bitcast_dynamic-update-slice_fusion.2
  520.4 5.1 bitcast_dynamic-update-slice_fusion.3
  525.6 37.8 %add.261 = f32[16,768,768]{2,1,0:T(8,128)} add(f32[16,768,768]{2,1,0:T(8,128)} %bitcast_dynamic-update-slice_fusion.3, f32[16,768,768]{2,1,0:T(8,128)} %bitcast_dynamic-update-slice_fusion.2) | non-fusion elementwise | flops 9437184 | bytes 113246208 | tf_op jit(solution)/shard_map/add | solution.py:284
  563.4 6.0 fusion.108
  578.8 51.0 %all-reduce.3 = f32[2304]{0:T(1024)} all-reduce(f32[2304]{0:T(1024)S(1)} %maximum_add_fusion), channel_id=3, replica_groups=mesh['cols'=16,'fsdp'=2] {'cols','fsdp'}, use_global_device_ids=true, to_apply=%region_43.44.clone | all-reduce | flops 2304 | bytes 18432
  636.8 284.5 %reduce-scatter.2.cloned.1.call-done = f32[384,768]{1,0:T(8,128)} async-done(((f32[12288,768]{1,0:T(8,128)}), f32[384,768]{1,0:T(8,128)}) %reduce-scatter.2.cloned.1.call-update) | async-done | bytes 1179664 | tf_op jit(solution)/shard_map/reduce_scatter | solution.py:289
  921.4 4.5 fusion.287
  (516 shorter events, 270.0 us)
Async XLA Ops:
  7.2 54.5 %copy-start.11 = (bf16[2,1,4,64,768]{4,3,2,1,0:T(8,128)(2,1)S(1)}, bf16[2,1,4,64,768]{4,3,2,1,0:T(8,128)(2,1)}, u32[]{:S(2)}) copy-start(bf16[2,1,4,64,768]{4,3,2,1,0:T(8,128)(2,1)} %param.10) | copy-start | bytes 2359300
  7.2 54.9 %copy-start.143 = (s32[2,1,2,64]{3,2,1,0:T(2,128)S(1)}, s32[2,1,2,64]{3,2,1,0:T(2,128)}, u32[]{:S(2)}) copy-start(s32[2,1,2,64]{3,2,1,0:T(2,128)} %param.13) | copy-start | bytes 3076
  7.2 132.8 %all-gather.2.cloned.1.call-start = ((), (), s32[]{:S(2)}) async-start(), calls=%async_computation.1 | async-start | bytes 19464192 | tf_op jit(solution)/shard_map/all_gather | solution.py:273
  9.5 911.9 %reduce-scatter.2.cloned.1.call-start = ((), (), s32[]{:S(2)}) async-start(), calls=%async_computation.2 | async-start | bytes 38928384 | tf_op jit(solution)/shard_map/reduce_scatter | solution.py:289
  61.7 98.4 %copy-start.105 = (f32[4,64]{1,0:T(4,128)}, f32[4,64]{1,0:T(4,128)S(1)}, u32[]{:S(2)}) copy-start(f32[4,64]{1,0:T(4,128)S(1)} %get-tuple-element.141) | copy-start | bytes 3076
  61.7 101.7 %copy-start.103 = (f32[4,64]{1,0:T(4,128)}, f32[4,64]{1,0:T(4,128)S(1)}, u32[]{:S(2)}) copy-start(f32[4,64]{1,0:T(4,128)S(1)} %get-tuple-element.140) | copy-start | bytes 3076
  62.1 97.9 %copy-start.112 = (f32[4,64]{1,0:T(4,128)}, f32[4,64]{1,0:T(4,128)S(1)}, u32[]{:S(2)}) copy-start(f32[4,64]{1,0:T(4,128)S(1)} %add_rsqrt_fusion.5) | copy-start | bytes 3076
  62.1 101.2 %copy-start.114 = (f32[4,64]{1,0:T(4,128)}, f32[4,64]{1,0:T(4,128)S(1)}, u32[]{:S(2)}) copy-start(f32[4,64]{1,0:T(4,128)S(1)} %add_rsqrt_fusion.2) | copy-start | bytes 3076
  62.7 100.6 %copy-start.101 = (f32[768]{0:T(1024)}, f32[768]{0:T(1024)S(1)}, u32[]{:S(2)}) copy-start(f32[768]{0:T(1024)S(1)} %get-tuple-element.97) | copy-start | bytes 9220
  144.5 38.2 %collective-permute-start = (bf16[2,4,32,768]{3,2,0,1:T(8,128)(2,1)}, bf16[2,4,32,768]{3,2,0,1:T(8,128)(2,1)}, u32[]{:S(2)}, u32[]{:S(2)}) collective-permute-start(bf16[2,4,32,768]{3,2,0,1:T(8,128)(2,1)} %get-tuple-element.91), channel_id=1, source_target_pairs={{0,2},{2,4},{4,6},{6,8},{8,10},{10,12},{12,14},{14,16},{16,18},{18... | collective-permute-start | bytes 1179656 | tf_op jit(solution)/shard_map/ppermute | solution.py:34
  147.4 35.3 %collective-permute-start.1 = (bf16[2,4,32,768]{3,2,0,1:T(8,128)(2,1)}, bf16[2,4,32,768]{3,2,0,1:T(8,128)(2,1)}, u32[]{:S(2)}, u32[]{:S(2)}) collective-permute-start(bf16[2,4,32,768]{3,2,0,1:T(8,128)(2,1)} %get-tuple-element.92), channel_id=1, source_target_pairs={{2,0},{4,2},{6,4},{8,6},{10,8},{12,10},{14,12},{16,14},{18,16},{20... | collective-permute-start | bytes 1179656 | tf_op jit(solution)/shard_map/ppermute | solution.py:37
  149.6 42.2 %collective-permute-start.2 = (bf16[2,4,32,768]{3,2,0,1:T(8,128)(2,1)}, bf16[2,4,32,768]{3,2,0,1:T(8,128)(2,1)}, u32[]{:S(2)}, u32[]{:S(2)}) collective-permute-start(bf16[2,4,32,768]{3,2,0,1:T(8,128)(2,1)} %get-tuple-element.93), channel_id=1, source_target_pairs={{0,2},{2,4},{4,6},{6,8},{8,10},{10,12},{12,14},{14,16},{16,18},{18... | collective-permute-start | bytes 1179656 | tf_op jit(solution)/shard_map/ppermute | solution.py:34
  163.3 22.3 %copy-start.49 = (bf16[4,64,12,64]{1,3,0,2:T(8,128)(2,1)}, bf16[4,64,12,64]{1,3,0,2:T(8,128)(2,1)S(1)}, u32[]{:S(2)}) copy-start(bf16[4,64,12,64]{1,3,0,2:T(8,128)(2,1)S(1)} %copy.193) | copy-start | bytes 1179652
  169.5 22.3 %collective-permute-start.3 = (bf16[2,4,32,768]{3,2,0,1:T(8,128)(2,1)}, bf16[2,4,32,768]{3,2,0,1:T(8,128)(2,1)}, u32[]{:S(2)}, u32[]{:S(2)}) collective-permute-start(bf16[2,4,32,768]{3,2,0,1:T(8,128)(2,1)} %get-tuple-element.94), channel_id=1, source_target_pairs={{2,0},{4,2},{6,4},{8,6},{10,8},{12,10},{14,12},{16,14},{18,16},{20... | collective-permute-start | bytes 1179656 | tf_op jit(solution)/shard_map/ppermute | solution.py:37
  205.5 34.7 %copy-start.22 = (f32[4,64,768]{2,1,0:T(8,128)}, f32[4,64,768]{2,1,0:T(8,128)S(1)}, u32[]{:S(2)}) copy-start(f32[4,64,768]{2,1,0:T(8,128)S(1)} %get-tuple-element.115) | copy-start | bytes 2359300
  242.2 59.0 %copy-start.5 = (f32[4,64,768]{2,1,0:T(8,128)}, f32[4,64,768]{2,1,0:T(8,128)S(1)}, u32[]{:S(2)}) copy-start(f32[4,64,768]{2,1,0:T(8,128)S(1)} %get-tuple-element.119) | copy-start | bytes 2359300
  242.3 59.0 %copy-start.110 = (f32[4,64]{1,0:T(4,128)}, f32[4,64]{1,0:T(4,128)S(1)}, u32[]{:S(2)}) copy-start(f32[4,64]{1,0:T(4,128)S(1)} %broadcast_multiply_fusion.12) | copy-start | bytes 3076
  242.5 58.8 %copy-start.122 = (f32[4,64]{1,0:T(4,128)}, f32[4,64]{1,0:T(4,128)S(1)}, u32[]{:S(2)}) copy-start(f32[4,64]{1,0:T(4,128)S(1)} %add_rsqrt_fusion) | copy-start | bytes 3076
  242.6 33.1 %slice-start = ((s8[18874368]{0:T(1024)(128)(4,1)}), s8[4194304]{0:T(1024)(128)(4,1)S(1)}, s32[]{:S(2)}) async-start(s8[18874368]{0:T(1024)(128)(4,1)} %bitcast.611), calls=%async_computation.3 | async-start | bytes 8388608
  242.6 33.1 %slice-start.1 = ((s8[18874368]{0:T(1024)(128)(4,1)}), s8[4194304]{0:T(1024)(128)(4,1)S(1)}, s32[]{:S(2)}) async-start(s8[18874368]{0:T(1024)(128)(4,1)} %bitcast.611), calls=%async_computation.4 | async-start | bytes 8388608
  247.2 28.5 %copy-start = (f32[4,64,3072]{2,1,0:T(8,128)}, f32[4,64,3072]{2,1,0:T(8,128)S(1)}, u32[]{:S(2)}) copy-start(f32[4,64,3072]{2,1,0:T(8,128)S(1)} %get-tuple-element.120) | copy-start | bytes 9437188
  247.2 28.5 %slice-start.2 = ((s8[18874368]{0:T(1024)(128)(4,1)}), s8[4194304]{0:T(1024)(128)(4,1)S(1)}, s32[]{:S(2)}) async-start(s8[18874368]{0:T(1024)(128)(4,1)} %bitcast.611), calls=%async_computation.5 | async-start | bytes 8388608
  247.2 28.5 %slice-start.3 = ((s8[18874368]{0:T(1024)(128)(4,1)}), s8[4194304]{0:T(1024)(128)(4,1)S(1)}, s32[]{:S(2)}) async-start(s8[18874368]{0:T(1024)(128)(4,1)} %bitcast.611), calls=%async_computation.6 | async-start | bytes 8388608
  261.4 14.3 %slice-start.4 = ((s8[18874368]{0:T(1024)(128)(4,1)}), s8[2097152]{0:T(1024)(128)(4,1)S(1)}, s32[]{:S(2)}) async-start(s8[18874368]{0:T(1024)(128)(4,1)} %bitcast.611), calls=%async_computation.7 | async-start | bytes 4194304
  464.1 11.4 %collective-permute-start.4 = (bf16[2,4,32,768]{3,2,0,1:T(8,128)(2,1)S(1)}, bf16[2,4,32,768]{3,2,0,1:T(8,128)(2,1)S(1)}, u32[]{:S(2)}, u32[]{:S(2)}) collective-permute-start(bf16[2,4,32,768]{3,2,0,1:T(8,128)(2,1)S(1)} %get-tuple-element.73), channel_id=1, source_target_pairs={{0,2},{2,4},{4,6},{6,8},{8,10},{10,12},{12,14},{14,16},{16,18},{18... | collective-permute-start | bytes 1179656 | tf_op jit(solution)/shard_map/ppermute | solution.py:34
  467.7 7.8 collective-permute-start.5
  469.4 6.5 collective-permute-start.6
  473.7 4.8 collective-permute-start.7
  479.7 17.9 %copy-start.45 = (bf16[2,4,64,768]{3,2,0,1:T(8,128)(2,1)}, bf16[2,4,64,768]{3,2,0,1:T(8,128)(2,1)S(1)}, u32[]{:S(2)}) copy-start(bf16[2,4,64,768]{3,2,0,1:T(8,128)(2,1)S(1)} %get-tuple-element.108) | copy-start | bytes 2359300
  575.9 56.5 %copy-start.18 = (f32[4,64,768]{2,1,0:T(8,128)S(1)}, f32[4,64,768]{2,1,0:T(8,128)}, u32[]{:S(2)}) copy-start(f32[4,64,768]{2,1,0:T(8,128)} %copy-done.16) | copy-start | bytes 2359300
  575.9 56.5 %copy-start.27 = (f32[4,64,768]{2,1,0:T(8,128)S(1)}, f32[4,64,768]{2,1,0:T(8,128)}, u32[]{:S(2)}) copy-start(f32[4,64,768]{2,1,0:T(8,128)} %get-tuple-element.98) | copy-start | bytes 2359300
  632.4 288.9 %copy-start.36 = (f32[384,768]{1,0:T(8,128)S(1)}, f32[384,768]{1,0:T(8,128)}, u32[]{:S(2)}) copy-start(f32[384,768]{1,0:T(8,128)} %param.14) | copy-start | bytes 3538948
  (138 other events, 523.9 us)
Sparse Core Ops, SparseCore 0:
  11.5 128.4 all-gather.1
  563.5 357.8 reduce-scatter.1
where the time goes:
time: 941 us; the launch traced here: 933 us
  waiting for transfers between devices  364 us (39%)
  matrix products  196 us (21%)
  local copies, waits for them, and re-layouts  136 us (14%)
  other arithmetic  104 us (11%)
  blocking collectives  94 us (10%)
  starting transfers between devices  20.6 us (2%)
  between operations  18.3 us (2%)
    reduce_scatter x1, waiting for transfers between devices, per_device(): lax.psum_scatter(weight_total, ('cols', 'fsdp'), scatter_dimension=0, til...  285 us
    unnamed x2, blocking collectives  94 us
    all_gather x1, waiting for transfers between devices, per_device(): lax.all_gather(weight_low, ('cols', 'fsdp'), axis=0, tiled=True)  77.2 us
    add x1, other arithmetic, per_device(): weight_total = weight_total + weight_grad  37.8 us
  transfers between devices with their start and end apart: 10, of which 3 were waited for; matrix products, arithmetic and copies ran while one was open for 7% of the time, Pallas kernels for 0%

commit v1 on v0

v1 whole, which is shorter than its diff:
```python
from functools import partial

import jax
import jax.numpy as jnp
from jax import lax
from jax.experimental import pallas as pl
from jax.experimental.pallas import tpu as pltpu
from jax.sharding import PartitionSpec as P

D = 768
H = 12
DH = 64
FF = 3072
NMAT = 16
ROWS = 4
CB = 64
HALO = 32
MB = 2
EXT = CB + 2 * HALO
SEQ = MB * ROWS
TOK = SEQ * CB
PAIRS = H // 2
LANES = 128
FOLD = FF // D

EPS = 1e-05
BETA_ONE = 0.9
BETA_TWO = 0.999
ADAM_EPS = 1e-08
DECAY = 0.01
RATE_GAIN = 0.3
STEP_NUMBER = 10.0
MASKED = -1e30
F32 = jnp.float32
LOW = jnp.bfloat16


def dot_nn(a, b):
    return lax.dot_general(a, b, (((1,), (0,)), ((), ())), preferred_element_type=F32)


def dot_nt(a, b):
    return lax.dot_general(a, b, (((1,), (1,)), ((), ())), preferred_element_type=F32)


def dot_tn(a, b):
    return lax.dot_general(a, b, (((0,), (0,)), ((), ())), preferred_element_type=F32)


def standardize(values):
    center = values - jnp.mean(values, axis=-1, keepdims=True)
    spread = lax.rsqrt(jnp.mean(center * center, axis=-1, keepdims=True) + EPS)
    return center * spread, spread


def norm_pull(upward, values, gain):
    scaled, spread = standardize(values)
    weighted = upward * gain
    result = spread * (
        weighted
        - jnp.mean(weighted, axis=-1, keepdims=True)
        - scaled * jnp.mean(weighted * scaled, axis=-1, keepdims=True)
    )
    return result, jnp.sum(upward * scaled, axis=0, keepdims=True)


def lane_window(pair):
    return pl.ds(pl.multiple_of(pair * LANES, LANES), LANES)


def side_by_side(ref, micro, window):
    return jnp.concatenate([ref[micro * ROWS + r, :, window] for r in range(ROWS)], axis=1)


def head_stack(packed):
    lane = lax.broadcasted_iota(jnp.int32, packed.shape, 1)
    first = (lane % LANES) < DH
    zero = jnp.zeros_like(packed)
    return jnp.concatenate([jnp.where(first, packed, zero), jnp.where(first, zero, packed)], axis=0)


def head_merge(stacked, r):
    block = stacked[:, r * LANES : (r + 1) * LANES]
    lane = lax.broadcasted_iota(jnp.int32, (CB, LANES), 1)
    return jnp.where(lane < DH, block[:CB], block[CB:])


def head_sums():
    feature = lax.broadcasted_iota(jnp.int32, (D, LANES), 0)
    head = lax.broadcasted_iota(jnp.int32, (D, LANES), 1)
    return (feature // DH == head).astype(F32).astype(LOW)


def head_spread():
    head = lax.broadcasted_iota(jnp.int32, (LANES, D), 0)
    feature = lax.broadcasted_iota(jnp.int32, (LANES, D), 1)
    return (feature // DH == head).astype(F32).astype(LOW)


def row_forward(scal, xe, allowed, gain, w, a1e, q, ke, ve, p1, o1, x1, a2):
    def norm_step(i, _):
        scaled, _s = standardize(xe[i].astype(F32))
        a1e[i] = (scaled * gain[0:1]).astype(LOW)
        return 0

    lax.fori_loop(0, SEQ, norm_step, 0)
    wide = a1e[...].reshape(SEQ * EXT, D)
    ke[...] = dot_nn(wide, w[1]).astype(LOW).reshape(SEQ, EXT, D)
    ve[...] = dot_nn(wide, w[2]).astype(LOW).reshape(SEQ, EXT, D)
    own = a1e[:, HALO : HALO + CB, :].reshape(TOK, D)
    q[...] = dot_nn(own, w[0]).astype(LOW).reshape(SEQ, CB, D)
    for i in range(SEQ):
        q[i] = (q[i].astype(F32) * scal[i // ROWS, 1 + i % ROWS]).astype(LOW)

    def attend(pair, _):
        window = lane_window(pair)
        for m in range(MB):
            query = head_stack(side_by_side(q, m, window))
            scores = dot_nt(query, side_by_side(ke, m, window)) * scal[m, 0]
            mask = allowed[m]
            mask = jnp.concatenate([mask, mask], axis=0)
            scores = jnp.where(mask > 0, scores, MASKED)
            weight = jnp.exp(scores - jnp.max(scores, axis=-1, keepdims=True))
            prob = weight / jnp.sum(weight, axis=-1, keepdims=True)
            p1[m, pair] = prob
            mixed = dot_nn(prob.astype(LOW), side_by_side(ve, m, window))
            for r in range(ROWS):
                o1[m * ROWS + r, :, window] = head_merge(mixed, r).astype(LOW)
        return 0

    lax.fori_loop(0, PAIRS, attend, 0)
    x1[...] = xe[:, HALO : HALO + CB, :].astype(F32) + dot_nn(
        o1[...].reshape(TOK, D), w[3]
    ).reshape(SEQ, CB, D)

    def next_norm(i, _):
        scaled, _s = standardize(x1[i])
        a2[i] = (scaled * gain[1:2]).astype(LOW)
        return 0

    lax.fori_loop(0, SEQ, next_norm, 0)


def col_forward(scal, x1, a2, gain, w, q2, k2, v2, p2, o2, x2, a3):
    flat = a2[...].reshape(TOK, D)
    q2[...] = dot_nn(flat, w[0]).astype(LOW).reshape(SEQ, CB, D)
    k2[...] = dot_nn(flat, w[1]).astype(LOW).reshape(SEQ, CB, D)
    v2[...] = dot_nn(flat, w[2]).astype(LOW).reshape(SEQ, CB, D)
    sums = head_sums()
    spread = head_spread()

    def attend(i, _):
        micro = i // ROWS
        query = q2[i].astype(F32)
        products = jnp.concatenate(
            [(query * k2[micro * ROWS + s].astype(F32)).astype(LOW) for s in range(ROWS)], axis=0
        )
        scores = dot_nn(products, sums) * (DH ** (-0.5))
        parts = [
            jnp.where(scal[micro, 1 + s] > 0, scores[s * CB : (s + 1) * CB], MASKED)
            for s in range(ROWS)
        ]
        top = jnp.maximum(jnp.maximum(parts[0], parts[1]), jnp.maximum(parts[2], parts[3]))
        parts = [jnp.exp(part - top) for part in parts]
        scale = 1.0 / (parts[0] + parts[1] + parts[2] + parts[3])
        prob = jnp.concatenate([part * scale for part in parts], axis=0)
        p2[i] = prob
        wide = dot_nn(prob.astype(LOW), spread)
        total = wide[:CB] * v2[micro * ROWS].astype(F32)
        for s in range(1, ROWS):
            total = total + wide[s * CB : (s + 1) * CB] * v2[micro * ROWS + s].astype(F32)
        o2[i] = total.astype(LOW)
        return 0

    lax.fori_loop(0, SEQ, attend, 0)
    x2[...] = x1[...] + dot_nn(o2[...].reshape(TOK, D), w[3]).reshape(SEQ, CB, D)

    def next_norm(i, _):
        scaled, _s = standardize(x2[i])
        a3[i] = (scaled * gain[2:3]).astype(LOW)
        return 0

    lax.fori_loop(0, SEQ, next_norm, 0)


CHUNK = 128


def feed_forward(
    scal, x2, a3, cot, gain, win, wout, out, e2, dwin, dwout, dgain, up, down, live_cot, gl, dhd, dgl
):
    step = pl.program_id(0)

    @pl.when(step == 0)
    def _():
        for i in range(SEQ):
            live_cot[i * CB : (i + 1) * CB] = (
                cot[i].astype(F32) * scal[i // ROWS, 1 + i % ROWS]
            ).astype(LOW)

    normed = a3[...].reshape(TOK, D)
    grad = live_cot[...]
    for base in range(0, TOK, CHUNK):
        rows = slice(base, base + CHUNK)
        hidden = dot_nn(normed[rows], win[0])
        pulled = dot_nt(grad[rows], wout[0])
        half = 0.5 * lax.erf(hidden * (0.5**0.5)) + 0.5
        gl[rows] = (hidden * half).astype(LOW)
        slope = half + hidden * (jnp.exp(-0.5 * hidden * hidden) * ((2.0 * jnp.pi) ** -0.5))
        dhd[rows] = (pulled * slope).astype(LOW)
    dwout[0] = dot_tn(gl[...], grad).astype(LOW)
    dwin[0] = dot_tn(normed, dhd[...]).astype(LOW)
    forward = dot_nn(gl[...], wout[0])
    backward = dot_nt(dhd[...], win[0])

    @pl.when(step == 0)
    def _():
        up[...] = forward
        down[...] = backward

    @pl.when(step > 0)
    def _():
        up[...] += forward
        down[...] += backward

    @pl.when(step == FOLD - 1)
    def _():
        total = jnp.zeros((1, D), F32)
        for i in range(SEQ):
            rows = slice(i * CB, (i + 1) * CB)
            value = x2[i]
            out[i] = ((value + up[rows]) * scal[i // ROWS, 1 + i % ROWS]).astype(LOW)
            part, gain_part = norm_pull(down[rows], value, gain[2:3])
            e2[i] = live_cot[rows].astype(F32) + part
            total = total + gain_part
        dgain[...] = total


def col_backward(
    scal, e2, o2, q2, k2, v2, p2, a2, x1, gain, w, dw, e1, dgain, do2, dq2, dk2, dv2, dka, dva
):
    low = e2[...].reshape(TOK, D).astype(LOW)
    dw[3] = dot_tn(o2[...].reshape(TOK, D), low).astype(LOW)
    do2[...] = dot_nt(low, w[3]).astype(LOW).reshape(SEQ, CB, D)
    sums = head_sums()
    spread = head_spread()
    dka[...] = jnp.zeros_like(dka)
    dva[...] = jnp.zeros_like(dva)

    def pull(i, _):
        micro = i // ROWS
        upward = do2[i].astype(F32)
        products = jnp.concatenate(
            [(upward * v2[micro * ROWS + s].astype(F32)).astype(LOW) for s in range(ROWS)], axis=0
        )
        dprob = dot_nn(products, sums)
        prob = p2[i]
        mixed = prob * dprob
        inner = mixed[:CB] + mixed[CB : 2 * CB] + mixed[2 * CB : 3 * CB] + mixed[3 * CB :]
        dscore = prob * (dprob - jnp.concatenate([inner] * ROWS, axis=0))
        wide = dot_nn(prob.astype(LOW), spread)
        dwide = dot_nn(dscore.astype(LOW), spread)
        query = q2[i].astype(F32)
        total = jnp.zeros((CB, D), F32)
        for s in range(ROWS):
            rows = slice(s * CB, (s + 1) * CB)
            total = total + dwide[rows] * k2[micro * ROWS + s].astype(F32)
            dka[micro * ROWS + s] += dwide[rows] * query
            dva[micro * ROWS + s] += wide[rows] * upward
        dq2[i] = (total * (DH ** (-0.5))).astype(LOW)
        return 0

    lax.fori_loop(0, SEQ, pull, 0)
    dk2[...] = (dka[...] * (DH ** (-0.5))).astype(LOW)
    dv2[...] = dva[...].astype(LOW)
    flat = a2[...].reshape(TOK, D)
    total = None
    for j, ref in enumerate((dq2, dk2, dv2)):
        grads = ref[...].reshape(TOK, D)
        dw[j] = dot_tn(flat, grads).astype(LOW)
        part = dot_nt(grads, w[j]).reshape(SEQ, CB, D)
        if j == 0:
            dka[...] = part
        else:
            dka[...] += part
    gain_total = jnp.zeros((1, D), F32)
    for i in range(SEQ):
        part, gain_part = norm_pull(dka[i], x1[i], gain[1:2])
        e1[i] = e2[i] + part
        gain_total = gain_total + gain_part
    dgain[...] = gain_total


def row_backward(scal, e1, o1, q, ke, ve, p1, a1e, w, dw, dq, dke, dve, do1):
    low = e1[...].reshape(TOK, D).astype(LOW)
    dw[3] = dot_tn(o1[...].reshape(TOK, D), low).astype(LOW)
    do1[...] = dot_nt(low, w[3]).astype(LOW).reshape(SEQ, CB, D)

    def pull(pair, _):
        window = lane_window(pair)
        for m in range(MB):
            query = head_stack(side_by_side(q, m, window))
            upward = head_stack(side_by_side(do1, m, window))
            prob = p1[m, pair]
            dprob = dot_nt(upward, side_by_side(ve, m, window))
            dscore = prob * (dprob - jnp.sum(prob * dprob, axis=-1, keepdims=True))
            dscore = dscore.astype(LOW)
            dvalue = dot_tn(prob.astype(LOW), upward)
            dkey = dot_tn(dscore, query) * scal[m, 0]
            dquery = dot_nn(dscore, side_by_side(ke, m, window)) * scal[m, 0]
            for r in range(ROWS):
                lanes = slice(r * LANES, (r + 1) * LANES)
                dve[m * ROWS + r, :, window] = dvalue[:, lanes].astype(LOW)
                dke[m * ROWS + r, :, window] = dkey[:, lanes].astype(LOW)
                dq[m * ROWS + r, :, window] = (head_merge(dquery, r) * scal[m, 1 + r]).astype(LOW)
        return 0

    lax.fori_loop(0, PAIRS, pull, 0)
    wide = a1e[...].reshape(SEQ * EXT, D)
    dw[0] = dot_tn(
        a1e[:, HALO : HALO + CB, :].reshape(TOK, D), dq[...].reshape(TOK, D)
    ).astype(LOW)
    dw[1] = dot_tn(wide, dke[...].reshape(SEQ * EXT, D)).astype(LOW)
    dw[2] = dot_tn(wide, dve[...].reshape(SEQ * EXT, D)).astype(LOW)


def input_backward(dq, dke, dve, from_low, from_high, w, e1, xe, gain, grad, dgain, own, acc):
    for j, ref in enumerate((dke, dve)):
        own[j, :, :HALO] = (
            ref[:, HALO:CB, :].astype(F32) + from_low[j].astype(F32)
        ).astype(LOW)
        own[j, :, HALO:] = (
            ref[:, CB : CB + HALO, :].astype(F32) + from_high[j].astype(F32)
        ).astype(LOW)
    acc[...] = dot_nt(dq[...].reshape(TOK, D), w[0]).reshape(SEQ, CB, D)
    for j in range(2):
        acc[...] += dot_nt(own[j].reshape(TOK, D), w[1 + j]).reshape(SEQ, CB, D)
    gain_total = jnp.zeros((1, D), F32)
    for i in range(SEQ):
        value = xe[i, HALO : HALO + CB, :].astype(F32)
        part, gain_part = norm_pull(acc[i], value, gain[0:1])
        grad[i] = (e1[i] + part).astype(LOW)
        gain_total = gain_total + gain_part
    dgain[...] = gain_total


def in_vmem(count):
    return [pl.BlockSpec(memory_space=pltpu.VMEM)] * count


def like(*shapes):
    return tuple(jax.ShapeDtypeStruct(shape, dtype) for shape, dtype in shapes)


SEQ_CB = (SEQ, CB, D)
SEQ_EXT = (SEQ, EXT, D)
SQUARE = (4, D, D)


def run_kernel(body, scal, args, outs, scratch=(), flops=0, megabytes=56):
    moved = sum(a.size * a.dtype.itemsize for a in args)
    moved += sum(o.size * jnp.dtype(o.dtype).itemsize for o in outs)
    ins = in_vmem(len(args))
    if scal is not None:
        args = (scal, *args)
        ins = [pl.BlockSpec(memory_space=pltpu.SMEM), *ins]
    return pl.pallas_call(
        body,
        name=body.__name__,
        out_shape=outs,
        in_specs=ins,
        out_specs=tuple(in_vmem(len(outs))),
        scratch_shapes=scratch,
        compiler_params=pltpu.CompilerParams(vmem_limit_bytes=megabytes << 20),
        cost_estimate=pl.CostEstimate(flops=flops, bytes_accessed=moved, transcendentals=0),
    )(*args)


UNIT = 2 * TOK * D * D


def call_row_forward(scal, xe, allowed, gain, w):
    outs = like(
        (SEQ_EXT, LOW),
        (SEQ_CB, LOW),
        (SEQ_EXT, LOW),
        (SEQ_EXT, LOW),
        ((MB, PAIRS, 2 * CB, EXT), F32),
        (SEQ_CB, LOW),
        (SEQ_CB, F32),
        (SEQ_CB, LOW),
    )
    return run_kernel(row_forward, scal, (xe, allowed, gain, w), outs, flops=8 * UNIT)


def call_col_forward(scal, x1, a2, gain, w):
    outs = like(
        (SEQ_CB, LOW),
        (SEQ_CB, LOW),
        (SEQ_CB, LOW),
        ((SEQ, ROWS * CB, LANES), F32),
        (SEQ_CB, LOW),
        (SEQ_CB, F32),
        (SEQ_CB, LOW),
    )
    return run_kernel(col_forward, scal, (x1, a2, gain, w), outs, flops=8 * UNIT)


def call_feed_forward(scal, x2, a3, cot, gain, win, wout):
    whole = lambda shape: pl.BlockSpec(shape, lambda f: (0,) * len(shape))
    block = pl.BlockSpec((1, D, D), lambda f: (f, 0, 0))
    outs = like((SEQ_CB, LOW), (SEQ_CB, F32), (SQUARE, LOW), (SQUARE, LOW), ((1, D), F32))
    return pl.pallas_call(
        feed_forward,
        name="feed_forward",
        grid=(FOLD,),
        out_shape=outs,
        in_specs=[
            pl.BlockSpec(memory_space=pltpu.SMEM),
            whole(SEQ_CB),
            whole(SEQ_CB),
            whole(SEQ_CB),
            whole((3, D)),
            block,
            block,
        ],
        out_specs=(whole(SEQ_CB), whole(SEQ_CB), block, block, whole((1, D))),
        scratch_shapes=[
            pltpu.VMEM((TOK, D), F32),
            pltpu.VMEM((TOK, D), F32),
            pltpu.VMEM((TOK, D), LOW),
            pltpu.VMEM((TOK, D), LOW),
            pltpu.VMEM((TOK, D), LOW),
            pltpu.VMEM((TOK, D), LOW),
        ],
        compiler_params=pltpu.CompilerParams(vmem_limit_bytes=56 << 20),
        cost_estimate=pl.CostEstimate(
            flops=24 * UNIT, bytes_accessed=2 * 8 * 2 * D * D + 12 * TOK * D, transcendentals=0
        ),
    )(scal, x2, a3, cot, gain, win, wout)


def call_col_backward(scal, e2, o2, q2, k2, v2, p2, a2, x1, gain, w):
    outs = like((SQUARE, LOW), (SEQ_CB, F32), ((1, D), F32))
    scratch = [pltpu.VMEM(SEQ_CB, LOW)] * 4 + [pltpu.VMEM(SEQ_CB, F32)] * 2
    return run_kernel(
        col_backward, scal, (e2, o2, q2, k2, v2, p2, a2, x1, gain, w), outs, scratch, 16 * UNIT
    )


def call_row_backward(scal, e1, o1, q, ke, ve, p1, a1e, w):
    outs = like((SQUARE, LOW), (SEQ_CB, LOW), (SEQ_EXT, LOW), (SEQ_EXT, LOW))
    scratch = [pltpu.VMEM(SEQ_CB, LOW)]
    return run_kernel(
        row_backward, scal, (e1, o1, q, ke, ve, p1, a1e, w), outs, scratch, 16 * UNIT
    )


def call_input_backward(dq, dke, dve, from_low, from_high, w, e1, xe, gain):
    outs = like((SEQ_CB, LOW), ((1, D), F32))
    scratch = [pltpu.VMEM((2, *SEQ_CB), LOW), pltpu.VMEM(SEQ_CB, F32)]
    return run_kernel(
        input_backward,
        None,
        (dq, dke, dve, from_low, from_high, w, e1, xe, gain),
        outs,
        scratch,
        4 * UNIT,
    )


def shifted(block, dim, width):
    count = lax.axis_size("cols")
    forward = [(i, i + 1) for i in range(count - 1)]
    backward = [(target, source) for source, target in forward]
    from_low = lax.ppermute(
        lax.slice_in_dim(block, block.shape[dim] - width, None, axis=dim), "cols", forward
    )
    from_high = lax.ppermute(lax.slice_in_dim(block, 0, width, axis=dim), "cols", backward)
    return from_low, from_high


def adamw(master, moment, square, grad_total, rate, decay, steps_done):
    moment_new = BETA_ONE * moment + (1.0 - BETA_ONE) * grad_total
    square_new = BETA_TWO * square + (1.0 - BETA_TWO) * grad_total * grad_total
    moment_fix = 1.0 - BETA_ONE**steps_done
    square_fix = 1.0 - BETA_TWO**steps_done
    update = moment_new / moment_fix / (jnp.sqrt(square_new / square_fix) + ADAM_EPS)
    return (master - rate * (update + decay * master), moment_new, square_new)


def band_mask(band_reach):
    first_col = lax.axis_index("cols") * CB
    col_total = CB * lax.axis_size("cols")
    query_pos = first_col + jnp.arange(CB, dtype=jnp.int32)
    key_pos = first_col - HALO + jnp.arange(EXT, dtype=jnp.int32)
    lowest = query_pos[None] - band_reach[:, 0]
    highest = query_pos[None] + band_reach[:, 1]
    key = key_pos[None, None]
    allowed = (key >= lowest[..., None]) & (key <= highest[..., None])
    allowed = allowed & (key >= 0) & (key < col_total)
    return allowed.astype(F32)


def layer(tokens, cot, counts, reach, weights, gain):
    present = (jnp.arange(ROWS, dtype=jnp.int32)[None] < counts[:, None]).astype(F32)
    row_scale = DH ** (-0.5) * lax.rsqrt(counts.astype(F32))
    scal = jnp.concatenate([row_scale[:, None], present], axis=1)
    allowed = band_mask(reach)
    from_low, from_high = shifted(tokens, 1, HALO)
    xe = jnp.concatenate([from_low, tokens, from_high], axis=1)
    a1e, q, ke, ve, p1, o1, x1, a2 = call_row_forward(scal, xe, allowed, gain, weights[0:4])
    q2, k2, v2, p2, o2, x2, a3 = call_col_forward(scal, x1, a2, gain, weights[4:8])
    out, e2, dwin, dwout, dg3 = call_feed_forward(
        scal, x2, a3, cot, gain, weights[8:12], weights[12:16]
    )
    dw_col, e1, dg2 = call_col_backward(scal, e2, o2, q2, k2, v2, p2, a2, x1, gain, weights[4:8])
    dw_row, dq, dke, dve = call_row_backward(scal, e1, o1, q, ke, ve, p1, a1e, weights[0:4])
    rims = jnp.stack([dke, dve])
    count = lax.axis_size("cols")
    forward = [(i, i + 1) for i in range(count - 1)]
    backward = [(target, source) for source, target in forward]
    to_high = lax.ppermute(rims[:, :, HALO + CB :], "cols", forward)
    to_low = lax.ppermute(rims[:, :, :HALO], "cols", backward)
    grad, dg1 = call_input_backward(dq, dke, dve, to_high, to_low, weights[0:3], e1, xe, gain)
    weight_grad = jnp.concatenate([dw_row, dw_col, dwin, dwout], axis=0)
    gain_grad = jnp.concatenate([dg1, dg2, dg3], axis=0)
    return out, grad, weight_grad, gain_grad


def per_device(
    alignment,
    cotangent,
    row_counts,
    band_reach,
    master_weights,
    weight_moment,
    weight_square,
    norm_gains,
    gain_moment,
    gain_square,
):
    axes = ("cols", "fsdp")
    weights = lax.all_gather(master_weights.astype(LOW), axes, axis=0, tiled=True)
    gain = lax.all_gather(norm_gains.astype(LOW), axes, axis=0, tiled=True)
    out, grad, weight_grad, gain_grad = layer(
        alignment.reshape(SEQ, CB, D),
        cotangent.reshape(SEQ, CB, D),
        row_counts[:, 0],
        band_reach[:, 0],
        weights.reshape(NMAT, D, D),
        gain.astype(F32).reshape(3, D),
    )
    weight_total = lax.psum_scatter(
        weight_grad.reshape(NMAT * D, D), axes, scatter_dimension=0, tiled=True
    ).astype(F32)
    gain_total = lax.psum_scatter(gain_grad.reshape(3 * D), axes, scatter_dimension=0, tiled=True)
    new_weights, new_moment, new_square = adamw(
        master_weights, weight_moment, weight_square, weight_total, D ** (-0.5), DECAY, STEP_NUMBER
    )
    new_gains, new_gain_moment, new_gain_square = adamw(
        norm_gains, gain_moment, gain_square, gain_total, RATE_GAIN, 0.0, STEP_NUMBER
    )
    shape = (MB, 1, ROWS, CB, D)
    return (
        out.reshape(shape),
        grad.reshape(shape),
        new_weights,
        new_moment,
        new_square,
        new_weights.astype(LOW),
        new_gains,
        new_gain_moment,
        new_gain_square,
    )


def solution(mesh):
    tokens = P(None, "fsdp", None, "cols", None)
    rows = P(("cols", "fsdp"), None)
    flat = P(("cols", "fsdp"))
    in_specs = (
        tokens,
        tokens,
        P(None, "fsdp"),
        P(None, "fsdp", None, "cols"),
        rows,
        rows,
        rows,
        flat,
        flat,
        flat,
    )
    out_specs = (tokens, tokens, rows, rows, rows, rows, flat, flat, flat)
    return jax.shard_map(
        per_device, mesh=mesh, in_specs=in_specs, out_specs=out_specs, check_vma=False
    )
```

time: 941 us -> 483 us (0.51)
  matrix products: 196 us -> 0 us
  waiting for transfers between devices: 364 us -> 202 us
  local copies, waits for them, and re-layouts: 136 us -> 22.7 us
  Pallas kernels: 0 us -> 104 us
  other arithmetic: 104 us -> 29.4 us
  starting transfers between devices: 20.6 us -> 8.11 us
    dot_general x62 -> x0, matrix products: 196 us -> none  [the longest x2 13.2 us: micro_pass(): jnp.einsum('hck,rkhd->rchd', score_grad, key_heads, preferred_element_typ...]
    reduce_scatter x1, waiting for transfers between devices: 285 us -> 127 us  [per_device(): lax.psum_scatter(weight_grad.reshape(NMAT * D, D), axes, scatter_dimensio...]
    pallas_call x0 -> x6, Pallas kernels: none -> 104 us  [the longest x5 77.6 us: run_kernel(): pl.pallas_call(body, name=body.__name__, out_shape=outs, in_specs=ins, ou...]
    add x9 -> x2, other arithmetic: 39.7 us -> 0.01 us  [the longest x1 0.01 us: band_mask(): query_pos = first_col + jnp.arange(CB, dtype=jnp.int32)]
    another operation x10 -> x0, local copies, waits for them, and re-layouts: 27.5 us -> none  [the longest x6 15.3 us: micro_pass(): jnp.stack([query_grad, key_grad, value_grad]).astype(low_type)]
    reshape x12 -> x2, local copies, waits for them, and re-layouts: 25.3 us -> 1.33 us  [the longest x1 0.72 us: per_device(): gain_grad.reshape(3 * D)]
    convert_element_type x14 -> x5, other arithmetic: 28.3 us -> 6.64 us  [the longest x1 3.63 us: per_device(): new_weights.astype(LOW)]
    mul x8 -> x1, local copies, waits for them, and re-layouts: 19.5 us -> 0.09 us  [layer(): row_scale = DH ** (-0.5) * lax.rsqrt(counts.astype(F32))]
  transfers between devices with their start and end apart: 10 -> 6, of which waited for: 3 -> 2; matrix products, arithmetic and copies ran while one was open for 7% -> 3% of each run, Pallas kernels for 0% -> 2%
where the time goes in v1:
time: 483 us; the launch traced here: 482 us
  waiting for transfers between devices  202 us (42%)
  Pallas kernels  104 us (22%)
  blocking collectives  102 us (21%)
  other arithmetic  29.4 us (6%)
  local copies, waits for them, and re-layouts  22.7 us (5%)
  between operations  14.2 us (3%)
  starting transfers between devices  8.11 us (2%)
    reduce_scatter x1, waiting for transfers between devices, per_device(): lax.psum_scatter(weight_grad.reshape(NMAT * D, D), axes, scatter_dimensio...  127 us
    unnamed x2, blocking collectives  102 us
    pallas_call x5, Pallas kernels, run_kernel(): pl.pallas_call(body, name=body.__name__, out_shape=outs, in_specs=ins, ou...  77.6 us
    all_gather x1, waiting for transfers between devices, per_device(): lax.all_gather(master_weights.astype(LOW), axes, axis=0, tiled=True)  75.2 us
    pallas_call x1, Pallas kernels, call_feed_forward(): pl.pallas_call(feed_forward, name='feed_forward', grid=(FOLD,), out_shape...  26.1 us
    concatenate x1, other arithmetic, layer(): weight_grad = jnp.concatenate([dw_row, dw_col, dwin, dwout], axis=0)  17 us
    slice x1, local copies, waits for them, and re-layouts, layer(): weights[12:16]  13.8 us
  transfers between devices with their start and end apart: 6, of which 2 were waited for; matrix products, arithmetic and copies ran while one was open for 3% of the time, Pallas kernels for 2%

profile of v1, /device:TPU:0, one launch (start us, length us, event | category | flops | bytes accessed | tf_op | source)
XLA Modules:
  0.0 482.0 jit_solution(4623319172992099991)
XLA Ops:
  7.3 2.2 convert_element_type.27
  9.6 2.4 collective-permute-start
  12.0 1.3 collective-permute-start.1
  13.6 0.2 dynamic-update-slice
  13.8 47.7 %all-reduce = bf16[2304]{0:T(1024)(128)(2,1)S(1)} all-reduce(bf16[2304]{0:T(1024)(128)(2,1)S(1)} %dynamic-update-slice), channel_id=1, replica_groups=mesh['cols'=16,'fsdp'=2] {'cols','fsdp'}, use_global_device_ids=true, to_apply=%add | all-reduce | flops 2304 | bytes 9216
  61.5 0.6 reshape.106.gain
  62.1 0.6 pad_maximum_fusion.5.scal
  62.7 0.7 and_convert_fusion.allowed
  63.4 1.2 pad_maximum_fusion.1.xe
  64.7 75.2 %all-gather.2.cloned.1.call-done = bf16[12288,768]{1,0:T(8,128)(2,1)} async-done(((bf16[384,768]{1,0:T(8,128)(2,1)}), bf16[12288,768]{1,0:T(8,128)(2,1)}) %all-gather.2.cloned.1.call-update) | async-done | bytes 18874384 | tf_op jit(solution)/shard_map/all_gather | solution.py:544
  139.9 13.8 %fusion.7 = (bf16[3072,768]{1,0:T(8,128)(2,1)}, bf16[3072,768]{1,0:T(8,128)(2,1)}, bf16[3072,768]{1,0:T(8,128)(2,1)}, bf16[3072,768]{1,0:T(8,128)(2,1)}) fusion(bf16[12288,768]{1,0:T(8,128)(2,1)} %all-gather.2.cloned.1.call-done), kind=kLoop, calls=%fused_computation.25 | loop fusion | bytes 37748736 | tf_op jit(solution)/shard_map/slice | solution.py:515
  153.7 19.4 %row_forward.1 = (bf16[8,128,768]{2,1,0:T(8,128)(2,1)}, bf16[8,64,768]{2,1,0:T(8,128)(2,1)}, bf16[8,128,768]{2,1,0:T(8,128)(2,1)}, bf16[8,128,768]{2,1,0:T(8,128...) custom-call(f32[2,5]{1,0:T(2,128)} %pad_maximum_fusion.5.scal, ...), custom_call_target="tpu_custom_call" | custom-call | flops 4831838208 | bytes 15803392 | tf_op jit(solution)/shard_map/row_forward/pallas_call | solution.py:367
  173.1 14.7 %col_forward.1 = (bf16[8,64,768]{2,1,0:T(8,128)(2,1)}, bf16[8,64,768]{2,1,0:T(8,128)(2,1)}, bf16[8,64,768]{2,1,0:T(8,128)(2,1)}, f32[8,256,128]{2,1,0:T(8,128)},...) custom-call(f32[2,5]{1,0:T(2,128)} %pad_maximum_fusion.5.scal, ...), custom_call_target="tpu_custom_call" | custom-call | flops 4831838208 | bytes 13640704 | tf_op jit(solution)/shard_map/col_forward/pallas_call | solution.py:367
  187.8 26.1 %feed_forward.1 = (bf16[8,64,768]{2,1,0:T(8,128)(2,1)}, f32[8,64,768]{2,1,0:T(8,128)}, bf16[4,768,768]{2,1,0:T(8,128)(2,1)}, bf16[4,768,768]{2,1,0:T(8,128)(2,1)}, f32[1,768]{1,0:T(1,128)}) custom-call(f32[2,5]{1,0:T(2,128)} %pad_maximum_fusion.5.scal, f32[8,64,768]{2,1,0:T(8,128)} %get-tuple-element.40.x2, bf16[8,64,768]{2,1,0:T(8,128)(2,1)} %get-tuple-element.41.a3, ...), custom_call_target="tpu_custom_call" | custom-call | flops 14495514624 | bytes 23592960 | tf_op jit(solution)/shard_map/feed_forward/pallas_call | solution.py:413
  214.0 17.0 %col_backward.1 = (bf16[4,768,768]{2,1,0:T(8,128)(2,1)}, f32[8,64,768]{2,1,0:T(8,128)}, f32[1,768]{1,0:T(1,128)}) custom-call(f32[2,5]{1,0:T(2,128)} %pad_maximum_fusion.5.scal, f32[8,64,768]{2,1,0:T(8,128)} %get-tuple-element.43.e2, bf16[8,64,768]{2,1,0:T(8,128)(2,1)} %get-tuple-element.44.o2, bf16[8,64,768]{2,1,0:T(8,128)(2,1)} %get-tuple-element.45.q2, ...), custom_call_target="tpu_custom_call" | custom-call | flops 9663676416 | bytes 19148800 | tf_op jit(solution)/shard_map/col_backward/pallas_call | solution.py:367
  231.0 17.3 %row_backward.1 = (bf16[4,768,768]{2,1,0:T(8,128)(2,1)}, bf16[8,64,768]{2,1,0:T(8,128)(2,1)}, bf16[8,128,768]{2,1,0:T(8,128)(2,1)}, bf16[8,128,768]{2,1,0:T(8,128)(2,1)}) custom-call(f32[2,5]{1,0:T(2,128)} %pad_maximum_fusion.5.scal, f32[8,64,768]{2,1,0:T(8,128)} %get-tuple-element.49.e1, bf16[8,64,768]{2,1,0:T(8,128)(2,1)} %get-tuple-element.50.o1, ...), custom_call_target="tpu_custom_call" | custom-call | flops 9663676416 | bytes 22020096 | tf_op jit(solution)/shard_map/row_backward/pallas_call | solution.py:367
  248.3 17.0 %pad_maximum_fusion = bf16[16,768,768]{2,1,0:T(8,128)(2,1)} fusion(bf16[4,768,768]{2,1,0:T(8,128)(2,1)} %get-tuple-element.63, bf16[4,768,768]{2,1,0:T(8,128)(2,1)} %get-tuple-element.62, bf16[4,768,768]{2,1,0:T(8,128)(2,1)} %get-tuple-element.61, bf16[4,768,768]{2,1,0:T(8,128)(2,1)} %get-tuple-element.60), kind=kLoop, calls=%fused_computation | loop fusion | flops 28311552 | bytes 37748736 | tf_op jit(solution)/shard_map/concatenate | solution.py:526
  265.3 1.4 copy-done
  266.7 0.5 copy-done.1
  267.2 1.3 pad_maximum_fusion.2
  268.5 1.3 collective-permute-start.3
  269.7 3.1 collective-permute-start.2
  272.8 4.1 slice.74
  277.0 0.9 copy-done.6
  277.8 0.3 copy-done.7
  278.1 9.1 %input_backward.1 = (bf16[8,64,768]{2,1,0:T(8,128)(2,1)}, f32[1,768]{1,0:T(1,128)}) custom-call(bf16[8,64,768]{2,1,0:T(8,128)(2,1)} %get-tuple-element.56.dq, bf16[8,128,768]{2,1,0:T(8,128)(2,1)} %get-tuple-element.57.dke, bf16[8,128,768]{2,1,0:T(8,128)(2,1)} %get-tuple-element.58.dve, bf16[2,8,32,768]{3,2,1,0:T(8,128)(2,1)} %copy-done.7, ...), custom_call_target="tpu_custom_call" | custom-call | flops 2415919104 | bytes 12988416 | tf_op jit(solution)/shard_map/input_backward/pallas_call | solution.py:367
  287.3 1.3 pad_maximum_fusion.4
  288.6 0.7 reshape.104
  289.3 53.9 %all-reduce.1 = f32[2304]{0:T(1024)} all-reduce(f32[2304]{0:T(1024)S(1)} %reshape.104), channel_id=3, replica_groups=mesh['cols'=16,'fsdp'=2] {'cols','fsdp'}, use_global_device_ids=true, to_apply=%region_1.0.clone | all-reduce | flops 2304 | bytes 18432
  343.2 1.3 multiply_subtract_fusion.1
  344.5 126.9 %reduce-scatter.2.cloned.1.call-done = bf16[384,768]{1,0:T(8,128)(2,1)} async-done(((bf16[12288,768]{1,0:T(8,128)(2,1)}), bf16[384,768]{1,0:T(8,128)(2,1)}) %reduce-scatter.2.cloned.1.call-update) | async-done | bytes 589840 | tf_op jit(solution)/shard_map/reduce_scatter | solution.py:554
  471.5 3.6 fusion.4
  (41 shorter events, 0.4 us)
Async XLA Ops:
  7.2 2.4 copy-start.3
  7.2 6.1 %copy-start.12 = (s32[2,1]{0,1:T(1,128)S(1)}, s32[2,1]{0,1:T(1,128)}, u32[]{:S(2)}) copy-start(s32[2,1]{0,1:T(1,128)} %param.12) | copy-start | bytes 28
  7.2 6.2 %copy-start.10 = (s32[2,1,2,64]{3,2,1,0:T(2,128)S(1)}, s32[2,1,2,64]{3,2,1,0:T(2,128)}, u32[]{:S(2)}) copy-start(s32[2,1,2,64]{3,2,1,0:T(2,128)} %param.13) | copy-start | bytes 3076
  7.2 6.3 %copy-start.11 = (f32[72]{0:T(128)S(1)}, f32[72]{0:T(128)}, u32[]{:S(2)}) copy-start(f32[72]{0:T(128)} %param.17) | copy-start | bytes 868
  7.2 132.7 %all-gather.2.cloned.1.call-start = ((), (), s32[]{:S(2)}) async-start(), calls=%async_computation.1 | async-start | bytes 19464192 | tf_op jit(solution)/shard_map/all_gather | solution.py:544
  9.5 462.0 %reduce-scatter.2.cloned.1.call-start = ((), (), s32[]{:S(2)}) async-start(), calls=%async_computation.2 | async-start | bytes 19464192 | tf_op jit(solution)/shard_map/reduce_scatter | solution.py:554
  9.6 53.8 %collective-permute-start = (bf16[8,32,768]{2,1,0:T(8,128)(2,1)S(1)}, bf16[8,32,768]{2,1,0:T(8,128)(2,1)S(1)}, u32[]{:S(2)}, u32[]{:S(2)}) collective-permute-start(bf16[8,32,768]{2,1,0:T(8,128)(2,1)S(1)} %get-tuple-element.98), channel_id=1, source_target_pairs={{0,2},{2,4},{4,6},{6,8},{8,10},{10,12},{12,14},{14,16},{16,18},{18... | collective-permute-start | bytes 1179656 | tf_op jit(solution)/shard_map/ppermute | solution.py:476
  12.0 51.4 %collective-permute-start.1 = (bf16[8,32,768]{2,1,0:T(8,128)(2,1)S(1)}, bf16[8,32,768]{2,1,0:T(8,128)(2,1)S(1)}, u32[]{:S(2)}, u32[]{:S(2)}) collective-permute-start(bf16[8,32,768]{2,1,0:T(8,128)(2,1)S(1)} %get-tuple-element.99), channel_id=1, source_target_pairs={{2,0},{4,2},{6,4},{8,6},{10,8},{12,10},{14,12},{16,14},{18,16},{20... | collective-permute-start | bytes 1179656 | tf_op jit(solution)/shard_map/ppermute | solution.py:479
  265.3 1.4 copy-start
  265.3 1.9 copy-start.1
  268.5 8.5 %collective-permute-start.3 = (bf16[2,8,32,768]{3,2,1,0:T(8,128)(2,1)}, bf16[2,8,32,768]{3,2,1,0:T(8,128)(2,1)S(1)}, u32[]{:S(2)}, u32[]{:S(2)}) collective-permute-start(bf16[2,8,32,768]{3,2,1,0:T(8,128)(2,1)} %get-tuple-element.96), channel_id=1, source_target_pairs={{2,0},{4,2},{6,4},{8,6},{10,8},{12,10},{14,12},{16,14},{18,16},{20... | collective-permute-start | bytes 2359304 | tf_op jit(solution)/shard_map/ppermute | solution.py:524
  269.7 7.2 %collective-permute-start.2 = (bf16[2,8,32,768]{3,2,1,0:T(8,128)(2,1)}, bf16[2,8,32,768]{3,2,1,0:T(8,128)(2,1)S(1)}, u32[]{:S(2)}, u32[]{:S(2)}) collective-permute-start(bf16[2,8,32,768]{3,2,1,0:T(8,128)(2,1)} %get-tuple-element.97), channel_id=1, source_target_pairs={{0,2},{2,4},{4,6},{6,8},{8,10},{10,12},{12,14},{14,16},{16,18},{18... | collective-permute-start | bytes 2359304 | tf_op jit(solution)/shard_map/ppermute | solution.py:523
  277.0 0.9 copy-start.6
  277.0 1.1 copy-start.7
  278.1 9.2 %copy-start.8 = (f32[1,768]{1,0:T(1,128)S(1)}, f32[1,768]{1,0:T(1,128)}, u32[]{:S(2)}) copy-start(f32[1,768]{1,0:T(1,128)} %get-tuple-element.66) | copy-start | bytes 9220
  278.1 9.2 %copy-start.9 = (f32[1,768]{1,0:T(1,128)S(1)}, f32[1,768]{1,0:T(1,128)}, u32[]{:S(2)}) copy-start(f32[1,768]{1,0:T(1,128)} %get-tuple-element.65) | copy-start | bytes 9220
  278.1 193.4 %copy-start.2 = (f32[384,768]{1,0:T(8,128)S(1)}, f32[384,768]{1,0:T(8,128)}, u32[]{:S(2)}) copy-start(f32[384,768]{1,0:T(8,128)} %param.14) | copy-start | bytes 3538948
  278.1 193.4 %copy-start.4 = (f32[384,768]{1,0:T(8,128)S(1)}, f32[384,768]{1,0:T(8,128)}, u32[]{:S(2)}) copy-start(f32[384,768]{1,0:T(8,128)} %param.15) | copy-start | bytes 3538948
  278.1 193.4 %copy-start.5 = (f32[384,768]{1,0:T(8,128)S(1)}, f32[384,768]{1,0:T(8,128)}, u32[]{:S(2)}) copy-start(f32[384,768]{1,0:T(8,128)} %param.16) | copy-start | bytes 3538948
Sparse Core Ops, SparseCore 0:
  11.5 128.3 all-gather.1
  265.5 205.9 reduce-scatter.1

commit v2 on v1

--- a/solution.py
+++ b/solution.py
@@ -22,6 +22,8 @@
 PAIRS = H // 2
 LANES = 128
 FOLD = FF // D
+PART = 192
+SPAN = 2 * PART
 
 EPS = 1e-05
 BETA_ONE = 0.9
@@ -97,18 +99,91 @@
     return (feature // DH == head).astype(F32).astype(LOW)
 
 
-def row_forward(scal, xe, allowed, gain, w, a1e, q, ke, ve, p1, o1, x1, a2):
+def flip(index, relative):
+    return index if relative == 0 else 1 - index
+
+
+def fetch_copies(place, own, other, w, sems):
+    copies = []
+    count = own.shape[3]
+    for n in range(count):
+        for core_rel, source in enumerate((own, other)):
+            for part in range(2):
+                for i in range(2):
+                    for j in range(2):
+                        y_rel, x_rel = (i, j) if part == 0 else (j, i)
+                        matrix = 2 * flip(place[1], y_rel) + flip(place[2], core_rel) + 4 * n
+                        row = pl.multiple_of(flip(place[0], x_rel) * SPAN + part * PART, PART)
+                        copies.append(
+                            pltpu.make_async_copy(
+                                source.at[part, i, j, n],
+                                w.at[matrix, pl.ds(row, PART)],
+                                sems.at[len(copies)],
+                            )
+                        )
+    return copies
+
+
+def emit_matrix(place, source, matrix, n, keep, send, sems, base):
+    core_same = place[2] == matrix % 2
+    y_rel = jnp.where(place[1] == matrix // 2, 0, 1)
+    waits = []
+    for x in range(2):
+        x_rel = jnp.where(place[0] == x, 0, 1)
+        for part in range(2):
+            i, j = (x_rel, y_rel) if part == 0 else (y_rel, x_rel)
+            block = source.at[pl.ds(x * SPAN + part * PART, PART)]
+            sem = sems.at[base + 2 * x + part]
+            kept = pltpu.make_async_copy(block, keep.at[part, i, j, n], sem)
+            sent = pltpu.make_async_copy(block, send.at[part, i, j, n], sem)
+            pl.when(core_same)(kept.start)
+            pl.when(jnp.logical_not(core_same))(sent.start)
+            waits.append(kept)
+    return waits
+
+
+def row_forward(
+    scal,
+    place,
+    tokens,
+    from_low,
+    from_high,
+    allowed,
+    gain,
+    own,
+    other,
+    a1e,
+    q,
+    ke,
+    ve,
+    p1,
+    o1,
+    x1,
+    a2,
+    w,
+    sems,
+):
+    copies = fetch_copies(place, own, other, w, sems)
+    for copy in copies:
+        copy.start()
     def norm_step(i, _):
-        scaled, _s = standardize(xe[i].astype(F32))
-        a1e[i] = (scaled * gain[0:1]).astype(LOW)
+        for source, start, size in (
+            (from_low, 0, HALO),
+            (tokens, HALO, CB),
+            (from_high, HALO + CB, HALO),
+        ):
+            scaled, _s = standardize(source[i].astype(F32))
+            a1e[i, start : start + size] = (scaled * gain[0:1]).astype(LOW)
         return 0
 
     lax.fori_loop(0, SEQ, norm_step, 0)
+    for copy in copies:
+        copy.wait()
     wide = a1e[...].reshape(SEQ * EXT, D)
     ke[...] = dot_nn(wide, w[1]).astype(LOW).reshape(SEQ, EXT, D)
     ve[...] = dot_nn(wide, w[2]).astype(LOW).reshape(SEQ, EXT, D)
-    own = a1e[:, HALO : HALO + CB, :].reshape(TOK, D)
-    q[...] = dot_nn(own, w[0]).astype(LOW).reshape(SEQ, CB, D)
+    inner = a1e[:, HALO : HALO + CB, :].reshape(TOK, D)
+    q[...] = dot_nn(inner, w[0]).astype(LOW).reshape(SEQ, CB, D)
     for i in range(SEQ):
         q[i] = (q[i].astype(F32) * scal[i // ROWS, 1 + i % ROWS]).astype(LOW)
 
@@ -129,7 +204,7 @@
         return 0
 
     lax.fori_loop(0, PAIRS, attend, 0)
-    x1[...] = xe[:, HALO : HALO + CB, :].astype(F32) + dot_nn(
+    x1[...] = tokens[...].astype(F32) + dot_nn(
         o1[...].reshape(TOK, D), w[3]
     ).reshape(SEQ, CB, D)
 
@@ -141,7 +216,14 @@
     lax.fori_loop(0, SEQ, next_norm, 0)
 
 
-def col_forward(scal, x1, a2, gain, w, q2, k2, v2, p2, o2, x2, a3):
+def col_forward(
+    scal, place, x1, a2, gain, own, other, q2, k2, v2, p2, o2, x2, a3, w, sems
+):
+    copies = fetch_copies(place, own, other, w, sems)
+    for copy in copies:
+        copy.start()
+    for copy in copies:
+        copy.wait()
     flat = a2[...].reshape(TOK, D)
     q2[...] = dot_nn(flat, w[0]).astype(LOW).reshape(SEQ, CB, D)
     k2[...] = dot_nn(flat, w[1]).astype(LOW).reshape(SEQ, CB, D)
@@ -187,60 +269,114 @@
 
 
 def feed_forward(
-    scal, x2, a3, cot, gain, win, wout, out, e2, dwin, dwout, dgain, up, down, live_cot, gl, dhd, dgl
+    scal,
+    place,
+    x2,
+    a3,
+    cot,
+    gain,
+    own,
+    other,
+    out,
+    e2,
+    dgain,
+    keep,
+    send,
+    up,
+    down,
+    live_cot,
+    gl,
+    dhd,
+    w,
+    dw,
+    in_sems,
+    out_sems,
 ):
-    step = pl.program_id(0)
-
-    @pl.when(step == 0)
-    def _():
-        for i in range(SEQ):
-            live_cot[i * CB : (i + 1) * CB] = (
-                cot[i].astype(F32) * scal[i // ROWS, 1 + i % ROWS]
-            ).astype(LOW)
-
+    copies = fetch_copies(place, own, other, w, in_sems)
+    for copy in copies:
+        copy.start()
+    for i in range(SEQ):
+        live_cot[i * CB : (i + 1) * CB] = (
+            cot[i].astype(F32) * scal[i // ROWS, 1 + i % ROWS]
+        ).astype(LOW)
     normed = a3[...].reshape(TOK, D)
     grad = live_cot[...]
-    for base in range(0, TOK, CHUNK):
-        rows = slice(base, base + CHUNK)
-        hidden = dot_nn(normed[rows], win[0])
-        pulled = dot_nt(grad[rows], wout[0])
-        half = 0.5 * lax.erf(hidden * (0.5**0.5)) + 0.5
-        gl[rows] = (hidden * half).astype(LOW)
-        slope = half + hidden * (jnp.exp(-0.5 * hidden * hidden) * ((2.0 * jnp.pi) ** -0.5))
-        dhd[rows] = (pulled * slope).astype(LOW)
-    dwout[0] = dot_tn(gl[...], grad).astype(LOW)
-    dwin[0] = dot_tn(normed, dhd[...]).astype(LOW)
-    forward = dot_nn(gl[...], wout[0])
-    backward = dot_nt(dhd[...], win[0])
-
-    @pl.when(step == 0)
-    def _():
-        up[...] = forward
-        down[...] = backward
-
-    @pl.when(step > 0)
-    def _():
-        up[...] += forward
-        down[...] += backward
-
-    @pl.when(step == FOLD - 1)
-    def _():
-        total = jnp.zeros((1, D), F32)
-        for i in range(SEQ):
-            rows = slice(i * CB, (i + 1) * CB)
-            value = x2[i]
-            out[i] = ((value + up[rows]) * scal[i // ROWS, 1 + i % ROWS]).astype(LOW)
-            part, gain_part = norm_pull(down[rows], value, gain[2:3])
-            e2[i] = live_cot[rows].astype(F32) + part
-            total = total + gain_part
-        dgain[...] = total
+    for copy in copies:
+        copy.wait()
+    waits = []
+    for step in range(FOLD):
+        win = w[step]
+        wout = w[FOLD + step]
+        for base in range(0, TOK, CHUNK):
+            rows = slice(base, base + CHUNK)
+            hidden = dot_nn(normed[rows], win)
+            pulled = dot_nt(grad[rows], wout)
+            half = 0.5 * lax.erf(hidden * (0.5**0.5)) + 0.5
+            gl[rows] = (hidden * half).astype(LOW)
+            slope = half + hidden * (jnp.exp(-0.5 * hidden * hidden) * ((2.0 * jnp.pi) ** -0.5))
+            dhd[rows] = (pulled * slope).astype(LOW)
+        for n, value in enumerate((dot_tn(normed, dhd[...]), dot_tn(gl[...], grad))):
+            slot = 4 * n + step
+            dw[slot] = value.astype(LOW)
+            waits += emit_matrix(place, dw.at[slot], step, n, keep, send, out_sems, 4 * slot)
+        forward = dot_nn(gl[...], wout)
+        backward = dot_nt(dhd[...], win)
+        if step == 0:
+            up[...] = forward
+            down[...] = backward
+        else:
+            up[...] += forward
+            down[...] += backward
+    total = jnp.zeros((1, D), F32)
+    for i in range(SEQ):
+        rows = slice(i * CB, (i + 1) * CB)
+        value = x2[i]
+        out[i] = ((value + up[rows]) * scal[i // ROWS, 1 + i % ROWS]).astype(LOW)
+        part, gain_part = norm_pull(down[rows], value, gain[2:3])
+        e2[i] = live_cot[rows].astype(F32) + part
+        total = total + gain_part
+    dgain[...] = total
+    for copy in waits:
+        copy.wait()
 
 
 def col_backward(
-    scal, e2, o2, q2, k2, v2, p2, a2, x1, gain, w, dw, e1, dgain, do2, dq2, dk2, dv2, dka, dva
+    scal,
+    place,
+    e2,
+    o2,
+    q2,
+    k2,
+    v2,
+    p2,
+    a2,
+    x1,
+    gain,
+    own,
+    other,
+    e1,
+    dgain,
+    keep,
+    send,
+    do2,
+    dq2,
+    dk2,
+    dv2,
+    dka,
+    dva,
+    w,
+    dw,
+    in_sems,
+    out_sems,
 ):
+    copies = fetch_copies(place, own, other, w, in_sems)
+    for copy in copies:
+        copy.start()
+    for copy in copies:
+        copy.wait()
     low = e2[...].reshape(TOK, D).astype(LOW)
     dw[3] = dot_tn(o2[...].reshape(TOK, D), low).astype(LOW)
+    waits = emit_matrix(place, dw.at[3], 3, 0, keep, send, out_sems, 12)
     do2[...] = dot_nt(low, w[3]).astype(LOW).reshape(SEQ, CB, D)
     sums = head_sums()
     spread = head_spread()
@@ -278,6 +414,7 @@
     for j, ref in enumerate((dq2, dk2, dv2)):
         grads = ref[...].reshape(TOK, D)
         dw[j] = dot_tn(flat, grads).astype(LOW)
+        waits += emit_matrix(place, dw.at[j], j, 0, keep, send, out_sems, 4 * j)
         part = dot_nt(grads, w[j]).reshape(SEQ, CB, D)
         if j == 0:
             dka[...] = part
@@ -289,11 +426,44 @@
         e1[i] = e2[i] + part
         gain_total = gain_total + gain_part
     dgain[...] = gain_total
-
-
-def row_backward(scal, e1, o1, q, ke, ve, p1, a1e, w, dw, dq, dke, dve, do1):
+    for copy in waits:
+        copy.wait()
+
+
+def row_backward(
+    scal,
+    place,
+    e1,
+    o1,
+    q,
+    ke,
+    ve,
+    p1,
+    a1e,
+    own,
+    other,
+    dq,
+    inner,
+    to_low,
+    to_high,
+    keep,
+    send,
+    do1,
+    dke,
+    dve,
+    w,
+    dw,
+    in_sems,
+    out_sems,
+):
+    copies = fetch_copies(place, own, other, w, in_sems)
+    for copy in copies:
+        copy.start()
+    for copy in copies:
+        copy.wait()
     low = e1[...].reshape(TOK, D).astype(LOW)
     dw[3] = dot_tn(o1[...].reshape(TOK, D), low).astype(LOW)
+    waits = emit_matrix(place, dw.at[3], 3, 0, keep, send, out_sems, 12)
     do1[...] = dot_nt(low, w[3]).astype(LOW).reshape(SEQ, CB, D)
 
     def pull(pair, _):
@@ -316,29 +486,44 @@
         return 0
 
     lax.fori_loop(0, PAIRS, pull, 0)
+    for j, ref in enumerate((dke, dve)):
+        inner[j] = ref[:, HALO : HALO + CB, :]
+        to_low[j] = ref[:, :HALO, :]
+        to_high[j] = ref[:, HALO + CB :, :]
     wide = a1e[...].reshape(SEQ * EXT, D)
     dw[0] = dot_tn(
         a1e[:, HALO : HALO + CB, :].reshape(TOK, D), dq[...].reshape(TOK, D)
     ).astype(LOW)
+    waits += emit_matrix(place, dw.at[0], 0, 0, keep, send, out_sems, 0)
     dw[1] = dot_tn(wide, dke[...].reshape(SEQ * EXT, D)).astype(LOW)
+    waits += emit_matrix(place, dw.at[1], 1, 0, keep, send, out_sems, 4)
     dw[2] = dot_tn(wide, dve[...].reshape(SEQ * EXT, D)).astype(LOW)
-
-
-def input_backward(dq, dke, dve, from_low, from_high, w, e1, xe, gain, grad, dgain, own, acc):
-    for j, ref in enumerate((dke, dve)):
-        own[j, :, :HALO] = (
-            ref[:, HALO:CB, :].astype(F32) + from_low[j].astype(F32)
+    waits += emit_matrix(place, dw.at[2], 2, 0, keep, send, out_sems, 8)
+    for copy in waits:
+        copy.wait()
+
+
+def input_backward(
+    place, dq, inner, from_low, from_high, own, other, e1, tokens, gain, grad, dgain, full, acc, w, sems
+):
+    copies = fetch_copies(place, own, other, w, sems)
+    for copy in copies:
+        copy.start()
+    for j in range(2):
+        full[j, :, :HALO] = (
+            inner[j, :, :HALO].astype(F32) + from_low[j].astype(F32)
         ).astype(LOW)
-        own[j, :, HALO:] = (
-            ref[:, CB : CB + HALO, :].astype(F32) + from_high[j].astype(F32)
+        full[j, :, HALO:] = (
+            inner[j, :, HALO:].astype(F32) + from_high[j].astype(F32)
         ).astype(LOW)
+    for copy in copies:
+        copy.wait()
     acc[...] = dot_nt(dq[...].reshape(TOK, D), w[0]).reshape(SEQ, CB, D)
     for j in range(2):
-        acc[...] += dot_nt(own[j].reshape(TOK, D), w[1 + j]).reshape(SEQ, CB, D)
+        acc[...] += dot_nt(full[j].reshape(TOK, D), w[1 + j]).reshape(SEQ, CB, D)
     gain_total = jnp.zeros((1, D), F32)
     for i in range(SEQ):
-        value = xe[i, HALO : HALO + CB, :].astype(F32)
-        part, gain_part = norm_pull(acc[i], value, gain[0:1])
+        part, gain_part = norm_pull(acc[i], tokens[i].astype(F32), gain[0:1])
         grad[i] = (e1[i] + part).astype(LOW)
         gain_total = gain_total + gain_part
     dgain[...] = gain_total
@@ -354,32 +539,35 @@
 
 SEQ_CB = (SEQ, CB, D)
 SEQ_EXT = (SEQ, EXT, D)
-SQUARE = (4, D, D)
-
-
-def run_kernel(body, scal, args, outs, scratch=(), flops=0, megabytes=56):
+RIM = (2, SEQ, HALO, D)
+UNIT = 2 * TOK * D * D
+VM = pltpu.VMEM
+DMA = pltpu.SemaphoreType.DMA
+
+
+def pieces(count):
+    return (2, 2, 2, count, PART, D)
+
+
+def run_kernel(body, scalars, args, outs, scratch, flops, raw_in=(), raw_out=()):
+    vmem = pl.BlockSpec(memory_space=pltpu.VMEM)
+    raw = pl.BlockSpec(memory_space=pl.ANY)
     moved = sum(a.size * a.dtype.itemsize for a in args)
     moved += sum(o.size * jnp.dtype(o.dtype).itemsize for o in outs)
-    ins = in_vmem(len(args))
-    if scal is not None:
-        args = (scal, *args)
-        ins = [pl.BlockSpec(memory_space=pltpu.SMEM), *ins]
     return pl.pallas_call(
         body,
         name=body.__name__,
         out_shape=outs,
-        in_specs=ins,
-        out_specs=tuple(in_vmem(len(outs))),
+        in_specs=[pl.BlockSpec(memory_space=pltpu.SMEM)] * len(scalars)
+        + [raw if i in raw_in else vmem for i in range(len(args))],
+        out_specs=tuple(raw if i in raw_out else vmem for i in range(len(outs))),
         scratch_shapes=scratch,
-        compiler_params=pltpu.CompilerParams(vmem_limit_bytes=megabytes << 20),
+        compiler_params=pltpu.CompilerParams(vmem_limit_bytes=60 << 20),
         cost_estimate=pl.CostEstimate(flops=flops, bytes_accessed=moved, transcendentals=0),
-    )(*args)
-
-
-UNIT = 2 * TOK * D * D
-
-
-def call_row_forward(scal, xe, allowed, gain, w):
+    )(*scalars, *args)
+
+
+def call_row_forward(scalars, tokens, from_low, from_high, allowed, gain, weights):
     outs = like(
         (SEQ_EXT, LOW),
         (SEQ_CB, LOW),
@@ -390,10 +578,12 @@
         (SEQ_CB, F32),
         (SEQ_CB, LOW),
     )
-    return run_kernel(row_forward, scal, (xe, allowed, gain, w), outs, flops=8 * UNIT)
-
-
-def call_col_forward(scal, x1, a2, gain, w):
+    args = (tokens, from_low, from_high, allowed, gain, *weights)
+    scratch = [VM((4, D, D), LOW), DMA((16,))]
+    return run_kernel(row_forward, scalars, args, outs, scratch, 8 * UNIT, (5, 6))
+
+
+def call_col_forward(scalars, x1, a2, gain, weights):
     outs = like(
         (SEQ_CB, LOW),
         (SEQ_CB, LOW),
@@ -403,81 +593,186 @@
         (SEQ_CB, F32),
         (SEQ_CB, LOW),
     )
-    return run_kernel(col_forward, scal, (x1, a2, gain, w), outs, flops=8 * UNIT)
-
-
-def call_feed_forward(scal, x2, a3, cot, gain, win, wout):
-    whole = lambda shape: pl.BlockSpec(shape, lambda f: (0,) * len(shape))
-    block = pl.BlockSpec((1, D, D), lambda f: (f, 0, 0))
-    outs = like((SEQ_CB, LOW), (SEQ_CB, F32), (SQUARE, LOW), (SQUARE, LOW), ((1, D), F32))
-    return pl.pallas_call(
-        feed_forward,
-        name="feed_forward",
-        grid=(FOLD,),
-        out_shape=outs,
-        in_specs=[
-            pl.BlockSpec(memory_space=pltpu.SMEM),
-            whole(SEQ_CB),
-            whole(SEQ_CB),
-            whole(SEQ_CB),
-            whole((3, D)),
-            block,
-            block,
-        ],
-        out_specs=(whole(SEQ_CB), whole(SEQ_CB), block, block, whole((1, D))),
-        scratch_shapes=[
-            pltpu.VMEM((TOK, D), F32),
-            pltpu.VMEM((TOK, D), F32),
-            pltpu.VMEM((TOK, D), LOW),
-            pltpu.VMEM((TOK, D), LOW),
-            pltpu.VMEM((TOK, D), LOW),
-            pltpu.VMEM((TOK, D), LOW),
-        ],
-        compiler_params=pltpu.CompilerParams(vmem_limit_bytes=56 << 20),
-        cost_estimate=pl.CostEstimate(
-            flops=24 * UNIT, bytes_accessed=2 * 8 * 2 * D * D + 12 * TOK * D, transcendentals=0
-        ),
-    )(scal, x2, a3, cot, gain, win, wout)
-
-
-def call_col_backward(scal, e2, o2, q2, k2, v2, p2, a2, x1, gain, w):
-    outs = like((SQUARE, LOW), (SEQ_CB, F32), ((1, D), F32))
-    scratch = [pltpu.VMEM(SEQ_CB, LOW)] * 4 + [pltpu.VMEM(SEQ_CB, F32)] * 2
+    scratch = [VM((4, D, D), LOW), DMA((16,))]
     return run_kernel(
-        col_backward, scal, (e2, o2, q2, k2, v2, p2, a2, x1, gain, w), outs, scratch, 16 * UNIT
-    )
-
-
-def call_row_backward(scal, e1, o1, q, ke, ve, p1, a1e, w):
-    outs = like((SQUARE, LOW), (SEQ_CB, LOW), (SEQ_EXT, LOW), (SEQ_EXT, LOW))
-    scratch = [pltpu.VMEM(SEQ_CB, LOW)]
-    return run_kernel(
-        row_backward, scal, (e1, o1, q, ke, ve, p1, a1e, w), outs, scratch, 16 * UNIT
-    )
-
-
-def call_input_backward(dq, dke, dve, from_low, from_high, w, e1, xe, gain):
+        col_forward, scalars, (x1, a2, gain, *weights), outs, scratch, 8 * UNIT, (3, 4)
+    )
+
+
+def call_feed_forward(scalars, x2, a3, cot, gain, weights):
+    outs = like(
+        (SEQ_CB, LOW), (SEQ_CB, F32), ((1, D), F32), (pieces(2), LOW), (pieces(2), LOW)
+    )
+    scratch = [
+        VM((TOK, D), F32),
+        VM((TOK, D), F32),
+        VM((TOK, D), LOW),
+        VM((TOK, D), LOW),
+        VM((TOK, D), LOW),
+        VM((8, D, D), LOW),
+        VM((8, D, D), LOW),
+        DMA((32,)),
+        DMA((32,)),
+    ]
+    args = (x2, a3, cot, gain, *weights)
+    return run_kernel(feed_forward, scalars, args, outs, scratch, 24 * UNIT, (4, 5), (3, 4))
+
+
+def call_col_backward(scalars, e2, o2, q2, k2, v2, p2, a2, x1, gain, weights):
+    outs = like((SEQ_CB, F32), ((1, D), F32), (pieces(1), LOW), (pieces(1), LOW))
+    scratch = [VM(SEQ_CB, LOW)] * 4 + [VM(SEQ_CB, F32)] * 2
+    scratch += [VM((4, D, D), LOW)] * 2 + [DMA((16,))] * 2
+    args = (e2, o2, q2, k2, v2, p2, a2, x1, gain, *weights)
+    return run_kernel(col_backward, scalars, args, outs, scratch, 16 * UNIT, (9, 10), (2, 3))
+
+
+def call_row_backward(scalars, e1, o1, q, ke, ve, p1, a1e, weights):
+    outs = like(
+        (SEQ_CB, LOW),
+        ((2, *SEQ_CB), LOW),
+        (RIM, LOW),
+        (RIM, LOW),
+        (pieces(1), LOW),
+        (pieces(1), LOW),
+    )
+    scratch = [VM(SEQ_CB, LOW)] + [VM(SEQ_EXT, LOW)] * 2
+    scratch += [VM((4, D, D), LOW)] * 2 + [DMA((16,))] * 2
+    args = (e1, o1, q, ke, ve, p1, a1e, *weights)
+    return run_kernel(row_backward, scalars, args, outs, scratch, 16 * UNIT, (7, 8), (4, 5))
+
+
+def call_input_backward(place, dq, inner, from_low, from_high, weights, e1, tokens, gain):
     outs = like((SEQ_CB, LOW), ((1, D), F32))
-    scratch = [pltpu.VMEM((2, *SEQ_CB), LOW), pltpu.VMEM(SEQ_CB, F32)]
-    return run_kernel(
-        input_backward,
-        None,
-        (dq, dke, dve, from_low, from_high, w, e1, xe, gain),
-        outs,
-        scratch,
-        4 * UNIT,
-    )
-
-
-def shifted(block, dim, width):
+    scratch = [VM((2, *SEQ_CB), LOW), VM(SEQ_CB, F32), VM((4, D, D), LOW), DMA((16,))]
+    args = (dq, inner, from_low, from_high, *weights, e1, tokens, gain)
+    return run_kernel(input_backward, (place,), args, outs, scratch, 4 * UNIT, (4, 5))
+
+
+def swap_pairs(count, bit):
+    return [(i, i ^ bit) for i in range(count)]
+
+
+class Staged:
+    planes = 4
+
+    def __init__(self):
+        count = NMAT
+        step = count // self.planes
+        self.step = step
+        self.count = count
+        cols = lax.axis_index("cols")
+        self.z = cols // step
+        self.place = jnp.stack([lax.axis_index("fsdp"), (cols // 2) % 2, cols % 2])
+
+    def over_x(self, value):
+        return lax.ppermute(value, "fsdp", [(0, 1), (1, 0)])
+
+    def over_y(self, value):
+        return lax.ppermute(value, "cols", swap_pairs(self.count, 2))
+
+    def over_core(self, value):
+        return lax.ppermute(value, "cols", swap_pairs(self.count, 1))
+
+    def over_z(self, value, pairs):
+        step = self.step
+        full = [(a * step + i, b * step + i) for a, b in pairs for i in range(step)]
+        return lax.ppermute(value, "cols", full)
+
+    def by_plane(self, options):
+        result = options[-1]
+        for index in range(len(options) - 2, -1, -1):
+            result = jnp.where(self.z == index, options[index], result)
+        return result
+
+    def spread_planes(self, shard):
+        last = self.planes - 1
+        up, down = [shard], [shard]
+        for k in range(last):
+            up.append(self.over_z(up[-1], [(i, i + 1) for i in range(k, last)]))
+            down.append(self.over_z(down[-1], [(i + 1, i) for i in range(last - k)]))
+        return [
+            self.by_plane([up[z - b] if z >= b else down[b - z] for z in range(self.planes)])
+            for b in range(self.planes)
+        ]
+
+    def gather_group(self, shards):
+        both = jnp.stack(shards)
+        first, second = both[:, :PART], both[:, PART:]
+        first = jnp.stack([first, self.over_x(first)])
+        second = jnp.stack([second, self.over_y(second)])
+        own = jnp.stack(
+            [
+                jnp.stack([first, self.over_y(first)]),
+                jnp.stack([second, self.over_x(second)]),
+            ]
+        )
+        return own, self.over_core(own)
+
+    def gather(self, shard):
+        planes = self.spread_planes(shard)
+        col = self.gather_group(planes[1:2])
+        row = self.gather_group(planes[0:1])
+        return row, col, self.gather_group(planes[2:4])
+
+    def reduce_group(self, keep, send, planes):
+        got = self.over_core(send)
+
+        def mine(*index):
+            return keep[index].astype(F32) + got[index].astype(F32)
+
+        from_x = self.over_x(mine(0, 1).astype(LOW)).astype(F32)
+        from_y = self.over_y(mine(1, 1).astype(LOW)).astype(F32)
+        first = mine(0, 0, 0) + from_x[0]
+        second = mine(1, 0, 0) + from_y[0]
+        first = first + self.over_y((mine(0, 0, 1) + from_x[1]).astype(LOW)).astype(F32)
+        second = second + self.over_x((mine(1, 0, 1) + from_y[1]).astype(LOW)).astype(F32)
+        partial_sum = jnp.concatenate([first, second], axis=1)
+        return [self.reduce_plane(partial_sum[i], b) for i, b in enumerate(planes)]
+
+    def reduce_plane(self, value, b):
+        hub = 2 if b < 2 else 1
+        near = self.over_z(value.astype(LOW), [(b ^ 1, b), (3 if hub == 2 else 0, hub)])
+        value = value + near.astype(F32)
+        return value + self.over_z(value.astype(LOW), [(hub, b)]).astype(F32)
+
+    def reduce(self, row, col, forward):
+        row = self.reduce_group(*row, (0,))
+        col = self.reduce_group(*col, (1,))
+        forward = self.reduce_group(*forward, (2, 3))
+        return self.by_plane(row + col + forward)
+
+
+class Native:
+    axes = ("cols", "fsdp")
+
+    def __init__(self):
+        self.place = jnp.zeros((3,), jnp.int32)
+
+    def gather(self, shard):
+        full = lax.all_gather(shard, self.axes, axis=0, tiled=True)
+        blocks = full.reshape(4, 2, 2, 2, 2, PART, D)
+        first = blocks[:, :, :, :, 0].transpose(2, 1, 3, 0, 4, 5)
+        second = blocks[:, :, :, :, 1].transpose(2, 3, 1, 0, 4, 5)
+        cores = jnp.stack([first, second], axis=1)
+        return [
+            (cores[0][:, :, :, a:b], cores[1][:, :, :, a:b]) for a, b in ((0, 1), (1, 2), (2, 4))
+        ]
+
+    def reduce(self, row, col, forward):
+        cores = jnp.stack(
+            [jnp.concatenate([g[c] for g in (row, col, forward)], axis=3) for c in range(2)]
+        )
+        first = cores[:, 0].transpose(3, 2, 0, 1, 4, 5)
+        second = cores[:, 1].transpose(3, 1, 0, 2, 4, 5)
+        full = jnp.stack([first, second], axis=4).reshape(NMAT * D, D)
+        return lax.psum_scatter(full, self.axes, scatter_dimension=0, tiled=True).astype(F32)
+
+
+def neighbours(upward, downward):
     count = lax.axis_size("cols")
     forward = [(i, i + 1) for i in range(count - 1)]
     backward = [(target, source) for source, target in forward]
-    from_low = lax.ppermute(
-        lax.slice_in_dim(block, block.shape[dim] - width, None, axis=dim), "cols", forward
-    )
-    from_high = lax.ppermute(lax.slice_in_dim(block, 0, width, axis=dim), "cols", backward)
-    return from_low, from_high
+    return lax.ppermute(upward, "cols", forward), lax.ppermute(downward, "cols", backward)
 
 
 def adamw(master, moment, square, grad_total, rate, decay, steps_done):
@@ -502,30 +797,28 @@
     return allowed.astype(F32)
 
 
-def layer(tokens, cot, counts, reach, weights, gain):
+def layer(tokens, cot, counts, reach, place, weights, gain):
+    row_w, col_w, forward_w = weights
     present = (jnp.arange(ROWS, dtype=jnp.int32)[None] < counts[:, None]).astype(F32)
     row_scale = DH ** (-0.5) * lax.rsqrt(counts.astype(F32))
-    scal = jnp.concatenate([row_scale[:, None], present], axis=1)
-    allowed = band_mask(reach)
-    from_low, from_high = shifted(tokens, 1, HALO)
-    xe = jnp.concatenate([from_low, tokens, from_high], axis=1)
-    a1e, q, ke, ve, p1, o1, x1, a2 = call_row_forward(scal, xe, allowed, gain, weights[0:4])
-    q2, k2, v2, p2, o2, x2, a3 = call_col_forward(scal, x1, a2, gain, weights[4:8])
-    out, e2, dwin, dwout, dg3 = call_feed_forward(
-        scal, x2, a3, cot, gain, weights[8:12], weights[12:16]
-    )
-    dw_col, e1, dg2 = call_col_backward(scal, e2, o2, q2, k2, v2, p2, a2, x1, gain, weights[4:8])
-    dw_row, dq, dke, dve = call_row_backward(scal, e1, o1, q, ke, ve, p1, a1e, weights[0:4])
-    rims = jnp.stack([dke, dve])
-    count = lax.axis_size("cols")
-    forward = [(i, i + 1) for i in range(count - 1)]
-    backward = [(target, source) for source, target in forward]
-    to_high = lax.ppermute(rims[:, :, HALO + CB :], "cols", forward)
-    to_low = lax.ppermute(rims[:, :, :HALO], "cols", backward)
-    grad, dg1 = call_input_backward(dq, dke, dve, to_high, to_low, weights[0:3], e1, xe, gain)
-    weight_grad = jnp.concatenate([dw_row, dw_col, dwin, dwout], axis=0)
-    gain_grad = jnp.concatenate([dg1, dg2, dg3], axis=0)
-    return out, grad, weight_grad, gain_grad
+    scalars = (jnp.concatenate([row_scale[:, None], present], axis=1), place)
+    from_low, from_high = neighbours(tokens[:, CB - HALO :], tokens[:, :HALO])
+    a1e, q, ke, ve, p1, o1, x1, a2 = call_row_forward(
+        scalars, tokens, from_low, from_high, band_mask(reach), gain, row_w
+    )
+    q2, k2, v2, p2, o2, x2, a3 = call_col_forward(scalars, x1, a2, gain, col_w)
+    out, e2, dg3, *forward_g = call_feed_forward(scalars, x2, a3, cot, gain, forward_w)
+    e1, dg2, *col_g = call_col_backward(
+        scalars, e2, o2, q2, k2, v2, p2, a2, x1, gain, col_w
+    )
+    dq, inner, to_low, to_high, *row_g = call_row_backward(
+        scalars, e1, o1, q, ke, ve, p1, a1e, row_w
+    )
+    from_low, from_high = neighbours(to_high, to_low)
+    grad, dg1 = call_input_backward(
+        place, dq, inner, from_low, from_high, row_w, e1, tokens, gain
+    )
+    return out, grad, (row_g, col_g, forward_g), jnp.concatenate([dg1, dg2, dg3], axis=0)
 
 
 def per_device(
@@ -541,22 +834,29 @@
     gain_square,
 ):
     axes = ("cols", "fsdp")
-    weights = lax.all_gather(master_weights.astype(LOW), axes, axis=0, tiled=True)
+    staged = lax.axis_size("cols") == NMAT and lax.axis_size("fsdp") == 2
+    mover = Staged() if staged else Native()
+    weights = mover.gather(master_weights.astype(LOW))
     gain = lax.all_gather(norm_gains.astype(LOW), axes, axis=0, tiled=True)
-    out, grad, weight_grad, gain_grad = layer(
+    out, grad, weight_grads, gain_grad = layer(
         alignment.reshape(SEQ, CB, D),
         cotangent.reshape(SEQ, CB, D),
         row_counts[:, 0],
         band_reach[:, 0],
-        weights.reshape(NMAT, D, D),
+        mover.place,
+        weights,
         gain.astype(F32).reshape(3, D),
     )
-    weight_total = lax.psum_scatter(
-        weight_grad.reshape(NMAT * D, D), axes, scatter_dimension=0, tiled=True
-    ).astype(F32)
+    weight_total = mover.reduce(*weight_grads)
     gain_total = lax.psum_scatter(gain_grad.reshape(3 * D), axes, scatter_dimension=0, tiled=True)
     new_weights, new_moment, new_square = adamw(
-        master_weights, weight_moment, weight_square, weight_total, D ** (-0.5), DECAY, STEP_NUMBER
+        master_weights,
+        weight_moment,
+        weight_square,
+        weight_total.reshape(master_weights.shape),
+        D ** (-0.5),
+        DECAY,
+        STEP_NUMBER,
     )
     new_gains, new_gain_moment, new_gain_square = adamw(
         norm_gains, gain_moment, gain_square, gain_total, RATE_GAIN, 0.0, STEP_NUMBER

time: 483 us -> 503 us (1.041)
  starting transfers between devices: 8.11 us -> 67.1 us
  local copies, waits for them, and re-layouts: 22.7 us -> 3.49 us
  waiting for transfers between devices: 202 us -> 189 us
  between operations: 14.2 us -> 1.56 us
  blocking collectives: 102 us -> 89.4 us
  other arithmetic: 29.4 us -> 40.1 us
    ppermute x4 -> x48, waiting for transfers between devices: 0.01 us -> 189 us  [the longest x12 66.8 us: over_y(): return lax.ppermute(value, 'cols', swap_pairs(self.count, 2))]
    reduce_scatter x1 -> x0, waiting for transfers between devices: 127 us -> none  [per_device(): lax.psum_scatter(weight_grad.reshape(NMAT * D, D), axes, scatter_dimensio...]
    all_gather x1 -> x0, waiting for transfers between devices: 75.2 us -> none  [per_device(): lax.all_gather(master_weights.astype(LOW), axes, axis=0, tiled=True)]
    ppermute x4 -> x48, starting transfers between devices: 8.03 us -> 67.1 us  [the longest x14 29 us: over_z(): return lax.ppermute(value, 'cols', full)]
    concatenate x4 -> x2, other arithmetic: 20.1 us -> 2.63 us  [the longest x1 1.34 us: layer(): scalars = (jnp.concatenate([row_scale[:, None], present], axis=1), place)]
    slice x3 -> x1, local copies, waits for them, and re-layouts: 18 us -> 0.93 us  [layer(): from_low, from_high = neighbours(tokens[:, CB - HALO:], tokens[:, :HALO])]
    unnamed x2, blocking collectives: 102 us -> 89.4 us
    convert_element_type x1 -> x21, other arithmetic: 2.2 us -> 12.3 us  [the longest x6 4.13 us: reduce_group(): from_x = self.over_x(mine(0, 1).astype(LOW)).astype(F32)]
  transfers between devices with their start and end apart: 6 -> 48, of which waited for: 2 -> 20; matrix products, arithmetic and copies ran while one was open for 3% -> 7% of each run, Pallas kernels for 2% -> 16%
where the time goes in v2:
time: 503 us; the launch traced here: 498 us
  waiting for transfers between devices  189 us (38%)
  Pallas kernels  107 us (21%)
  blocking collectives  89.4 us (18%)
  starting transfers between devices  67.1 us (13%)
  other arithmetic  40.1 us (8%)
    pallas_call x6, Pallas kernels, run_kernel(): pl.pallas_call(body, name=body.__name__, out_shape=outs, in_specs=[pl.Blo...  107 us
    unnamed x2, blocking collectives  89.4 us
    ppermute x12, waiting for transfers between devices, over_y(): return lax.ppermute(value, 'cols', swap_pairs(self.count, 2))  66.8 us
    ppermute x12, waiting for transfers between devices, over_x(): return lax.ppermute(value, 'fsdp', [(0, 1), (1, 0)])  64.1 us
    ppermute x14, waiting for transfers between devices, over_z(): return lax.ppermute(value, 'cols', full)  53.5 us
    ppermute x14, starting transfers between devices, over_z(): return lax.ppermute(value, 'cols', full)  29 us
    ppermute x12, starting transfers between devices, over_y(): return lax.ppermute(value, 'cols', swap_pairs(self.count, 2))  15.6 us
    ppermute x12, starting transfers between devices, over_x(): return lax.ppermute(value, 'fsdp', [(0, 1), (1, 0)])  13.7 us
  transfers between devices with their start and end apart: 48, of which 20 were waited for; matrix products, arithmetic and copies ran while one was open for 7% of the time, Pallas kernels for 16%

profile of v2, /device:TPU:0, one launch (start us, length us, event | category | flops | bytes accessed | tf_op | source)
XLA Modules:
  0.0 497.8 jit_solution(15943358430406468935)
XLA Ops:
  3.4 5.6 %collective-permute-start.2 = (bf16[384,768]{1,0:T(8,128)(2,1)S(1)}, bf16[384,768]{1,0:T(8,128)(2,1)S(1)}, u32[]{:S(2)}, u32[]{:S(2)}) collective-permute-start(bf16[384,768]{1,0:T(8,128)(2,1)S(1)} %convert_element_type.562), channel_id=1, source_target_pairs={{0,8},{2,10},{4,12},{6,14},{8,16},{10,18},{12,20},{14,22},{16,24},... | collective-permute-start | bytes 1769480 | tf_op jit(solution)/shard_map/ppermute | solution.py:679
  9.0 11.4 %collective-permute-done.10 = bf16[384,768]{1,0:T(8,128)(2,1)S(1)} collective-permute-done((bf16[384,768]{1,0:T(8,128)(2,1)S(1)}, bf16[384,768]{1,0:T(8,128)(2,1)S(1)}, u32[]{:S(2)}, u32[]{:S(2)}) %collective-permute-start.10) | collective-permute-done | bytes 589856 | tf_op jit(solution)/shard_map/ppermute | solution.py:679
  22.3 14.4 %collective-permute-done.16 = bf16[384,768]{1,0:T(8,128)(2,1)S(1)} collective-permute-done((bf16[384,768]{1,0:T(8,128)(2,1)S(1)}, bf16[384,768]{1,0:T(8,128)(2,1)S(1)}, u32[]{:S(2)}, u32[]{:S(2)}) %collective-permute-start.16) | collective-permute-done | bytes 589856 | tf_op jit(solution)/shard_map/ppermute | solution.py:679
  39.5 12.8 %collective-permute-done.17 = bf16[384,768]{1,0:T(8,128)(2,1)} collective-permute-done((bf16[384,768]{1,0:T(8,128)(2,1)S(1)}, bf16[384,768]{1,0:T(8,128)(2,1)}, u32[]{:S(2)}, u32[]{:S(2)}) %collective-permute-start.17) | collective-permute-done | bytes 589856 | tf_op jit(solution)/shard_map/ppermute | solution.py:679
  56.5 10.4 %collective-permute-done.18 = bf16[2,192,768]{2,1,0:T(8,128)(2,1)S(1)} collective-permute-done((bf16[2,192,768]{2,1,0:T(8,128)(2,1)S(1)}, bf16[2,192,768]{2,1,0:T(8,128)(2,1)S(1)}, u32[]{:S(2)}, u32[]{:S(2)}) %collective-permute-start.18) | collective-permute-done | bytes 589856 | tf_op jit(solution)/shard_map/ppermute | solution.py:668
  73.1 22.4 %collective-permute-done.19 = bf16[2,2,192,768]{3,2,1,0:T(8,128)(2,1)S(1)} collective-permute-done((bf16[2,2,192,768]{3,2,1,0:T(8,128)(2,1)S(1)}, bf16[2,2,192,768]{3,2,1,0:T(8,128)(2,1)S(1)}, u32[]{:S(2)}, u32[]{:S(2)}) %collective-permute-start.19) | collective-permute-done | bytes 1179680 | tf_op jit(solution)/shard_map/ppermute | solution.py:671
  96.0 2.6 pad_maximum_fusion.own
  103.1 6.6 %collective-permute-done.11 = bf16[1,192,768]{2,1,0:T(8,128)(2,1)S(1)} collective-permute-done((bf16[1,192,768]{2,1,0:T(8,128)(2,1)S(1)}, bf16[1,192,768]{2,1,0:T(8,128)(2,1)S(1)}, u32[]{:S(2)}, u32[]{:S(2)}) %collective-permute-start.11) | collective-permute-done | bytes 294944 | tf_op jit(solution)/shard_map/ppermute | solution.py:668
  110.9 10.3 %collective-permute-done.13 = bf16[1,192,768]{2,1,0:T(8,128)(2,1)S(1)} collective-permute-done((bf16[1,192,768]{2,1,0:T(8,128)(2,1)S(1)}, bf16[1,192,768]{2,1,0:T(8,128)(2,1)S(1)}, u32[]{:S(2)}, u32[]{:S(2)}) %collective-permute-start.13) | collective-permute-done | bytes 294944 | tf_op jit(solution)/shard_map/ppermute | solution.py:671
  122.9 10.6 %collective-permute-done.12 = bf16[2,1,192,768]{3,2,0,1:T(8,128)(2,1)S(1)} collective-permute-done((bf16[2,1,192,768]{3,2,0,1:T(8,128)(2,1)S(1)}, bf16[2,1,192,768]{3,2,0,1:T(8,128)(2,1)S(1)}, u32[]{:S(2)}, u32[]{:S(2)}) %collective-permute-start.12) | collective-permute-done | bytes 589856 | tf_op jit(solution)/shard_map/ppermute | solution.py:671
  136.0 2.5 pad_maximum_fusion.2
  139.5 3.2 collective-permute-start
  147.7 42.2 %all-reduce = bf16[2304]{0:T(1024)(128)(2,1)S(1)} all-reduce(bf16[2304]{0:T(1024)(128)(2,1)S(1)} %dynamic-update-slice), channel_id=1, replica_groups=mesh['cols'=16,'fsdp'=2] {'cols','fsdp'}, use_global_device_ids=true, to_apply=%add | all-reduce | flops 2304 | bytes 9216
  194.0 18.6 %row_forward.1 = (bf16[8,128,768]{2,1,0:T(8,128)(2,1)}, bf16[8,64,768]{2,1,0:T(8,128)(2,1)}, bf16[8,128,768]{2,1,0:T(8,128)(2,1)}, bf16[8,128,768]{2,1,0:T(8,128...) custom-call(f32[2,5]{1,0:T(2,128)} %pad_maximum_fusion.12.scal, ...), custom_call_target="tpu_custom_call" | custom-call | flops 4831838208 | bytes 15803392 | tf_op jit(solution)/shard_map/row_forward/pallas_call | solution.py:557
  212.6 15.8 %col_forward.1 = (bf16[8,64,768]{2,1,0:T(8,128)(2,1)}, bf16[8,64,768]{2,1,0:T(8,128)(2,1)}, bf16[8,64,768]{2,1,0:T(8,128)(2,1)}, f32[8,256,128]{2,1,0:T(8,128)},...) custom-call(f32[2,5]{1,0:T(2,128)} %pad_maximum_fusion.12.scal, ...), custom_call_target="tpu_custom_call" | custom-call | flops 4831838208 | bytes 13640704 | tf_op jit(solution)/shard_map/col_forward/pallas_call | solution.py:557
  228.4 26.7 %feed_forward.1 = (bf16[8,64,768]{2,1,0:T(8,128)(2,1)}, f32[8,64,768]{2,1,0:T(8,128)}, f32[1,768]{1,0:T(1,128)}, bf16[2,2,2,2,192,768]{5,4,3,2,1,0:T(8,128)(2,1)}, bf16[2,2,2,2,192,768]{5,4,3,2,1,0:T(8,128)(2,1)}) custom-call(f32[2,5]{1,0:T(2,128)} %pad_maximum_fusion.12.scal, s32[3]{0:T(128)} %pad_add_fusion.place, f32[8,64,768]{2,1,0:T(8,128)} %get-tuple-element.43.x2, ...), custom_call_target="tpu_custom_call" | custom-call | flops 14495514624 | bytes 24391680 | tf_op jit(solution)/shard_map/feed_forward/pallas_call | solution.py:557
  255.2 17.5 %col_backward.1 = (f32[8,64,768]{2,1,0:T(8,128)}, f32[1,768]{1,0:T(1,128)}, bf16[2,2,2,1,192,768]{5,4,3,2,1,0:T(8,128)(2,1)}, bf16[2,2,2,1,192,768]{5,4,3,2,1,0:T(8,128)(2,1)}) custom-call(f32[2,5]{1,0:T(2,128)} %pad_maximum_fusion.12.scal, s32[3]{0:T(128)} %pad_add_fusion.place, f32[8,64,768]{2,1,0:T(8,128)} %get-tuple-element.46.e2, ...), custom_call_target="tpu_custom_call" | custom-call | flops 9663676416 | bytes 19148800 | tf_op jit(solution)/shard_map/col_backward/pallas_call | solution.py:557
  272.7 20.1 %row_backward.1 = (bf16[8,64,768]{2,1,0:T(8,128)(2,1)}, bf16[2,8,64,768]{3,2,1,0:T(8,128)(2,1)}, bf16[2,8,32,768]{3,2,1,0:T(8,128)(2,1)}, bf16[2,8,32,768]{3,2,1...) custom-call(f32[2,5]{1,0:T(2,128)} %pad_maximum_fusion.12.scal, ...), custom_call_target="tpu_custom_call" | custom-call | flops 9663676416 | bytes 22020096 | tf_op jit(solution)/shard_map/row_backward/pallas_call | solution.py:557
  293.5 4.3 collective-permute-done.25
  309.6 6.0 %collective-permute-done.26 = bf16[2,1,192,768]{3,2,1,0:T(8,128)(2,1)S(1)} collective-permute-done((bf16[2,1,192,768]{3,2,1,0:T(8,128)(2,1)S(1)}, bf16[2,1,192,768]{3,2,1,0:T(8,128)(2,1)S(1)}, u32[]{:S(2)}, u32[]{:S(2)}) %collective-permute-start.26) | collective-permute-done | bytes 589856 | tf_op jit(solution)/shard_map/ppermute | solution.py:668
  317.9 10.5 %collective-permute-done.33 = bf16[2,1,192,768]{3,2,1,0:T(8,128)(2,1)S(1)} collective-permute-done((bf16[2,1,192,768]{3,2,1,0:T(8,128)(2,1)S(1)}, bf16[2,1,192,768]{3,2,1,0:T(8,128)(2,1)S(1)}, u32[]{:S(2)}, u32[]{:S(2)}) %collective-permute-start.33) | collective-permute-done | bytes 589856 | tf_op jit(solution)/shard_map/ppermute | solution.py:668
  331.7 21.6 %collective-permute-done.40 = bf16[2,2,192,768]{3,2,1,0:T(8,128)(2,1)S(1)} collective-permute-done((bf16[2,2,192,768]{3,2,1,0:T(8,128)(2,1)S(1)}, bf16[2,2,192,768]{3,2,1,0:T(8,128)(2,1)S(1)}, u32[]{:S(2)}, u32[]{:S(2)}) %collective-permute-start.40) | collective-permute-done | bytes 1179680 | tf_op jit(solution)/shard_map/ppermute | solution.py:668
  359.1 10.4 %collective-permute-done.42 = bf16[2,2,192,768]{3,2,1,0:T(8,128)(2,1)S(1)} collective-permute-done((bf16[2,2,192,768]{3,2,1,0:T(8,128)(2,1)S(1)}, bf16[2,2,192,768]{3,2,1,0:T(8,128)(2,1)S(1)}, u32[]{:S(2)}, u32[]{:S(2)}) %collective-permute-start.42) | collective-permute-done | bytes 1179680 | tf_op jit(solution)/shard_map/ppermute | solution.py:671
  369.7 11.6 %collective-permute-done.41 = bf16[2,192,768]{2,1,0:T(8,128)(2,1)S(1)} collective-permute-done((bf16[2,192,768]{2,1,0:T(8,128)(2,1)S(1)}, bf16[2,192,768]{2,1,0:T(8,128)(2,1)S(1)}, u32[]{:S(2)}, u32[]{:S(2)}) %collective-permute-start.41) | collective-permute-done | bytes 589856 | tf_op jit(solution)/shard_map/ppermute | solution.py:671
  386.3 4.6 collective-permute-start.37
  390.9 6.7 %collective-permute-done.43 = bf16[2,192,768]{2,1,0:T(8,128)(2,1)S(1)} collective-permute-done((bf16[2,192,768]{2,1,0:T(8,128)(2,1)S(1)}, bf16[2,192,768]{2,1,0:T(8,128)(2,1)S(1)}, u32[]{:S(2)}, u32[]{:S(2)}) %collective-permute-start.43) | collective-permute-done | bytes 589856 | tf_op jit(solution)/shard_map/ppermute | solution.py:668
  399.1 4.2 collective-permute-start.44
  411.4 5.6 %collective-permute-done.44 = bf16[384,768]{1,0:T(8,128)(2,1)S(1)} collective-permute-done((bf16[384,768]{1,0:T(8,128)(2,1)S(1)}, bf16[384,768]{1,0:T(8,128)(2,1)S(1)}, u32[]{:S(2)}, u32[]{:S(2)}) %collective-permute-start.44) | collective-permute-done | bytes 589856 | tf_op jit(solution)/shard_map/ppermute | solution.py:679
  418.5 9.4 %collective-permute-done.46 = bf16[384,768]{1,0:T(8,128)(2,1)S(1)} collective-permute-done((bf16[384,768]{1,0:T(8,128)(2,1)S(1)}, bf16[384,768]{1,0:T(8,128)(2,1)S(1)}, u32[]{:S(2)}, u32[]{:S(2)}) %collective-permute-start.46) | collective-permute-done | bytes 589856 | tf_op jit(solution)/shard_map/ppermute | solution.py:679
  432.4 8.8 %input_backward.1 = (bf16[8,64,768]{2,1,0:T(8,128)(2,1)}, f32[1,768]{1,0:T(1,128)}) custom-call(s32[3]{0:T(128)} %pad_add_fusion.place, bf16[8,64,768]{2,1,0:T(8,128)(2,1)} %get-tuple-element.59.dq, bf16[2,8,64,768]{3,2,1,0:T(8,128)(2,1)} %get-tuple-element.60.inner, bf16[2,8,32,768]{3,2,1,0:T(8,128)(2,1)} %collective-permute-done.23.from_low, ...), custom_call_target="tpu_custom_call" | custom-call | flops 2415919104 | bytes 11808768 | tf_op jit(solution)/shard_map/input_backward/pallas_call | solution.py:557
  443.3 47.2 %all-reduce.1 = f32[2304]{0:T(1024)} all-reduce(f32[2304]{0:T(1024)S(1)} %reshape.618), channel_id=2, replica_groups=mesh['cols'=16,'fsdp'=2] {'cols','fsdp'}, use_global_device_ids=true, to_apply=%region_0.1.clone | all-reduce | flops 2304 | bytes 18432
  491.9 5.7 %fusion.52 = (bf16[384,768]{1,0:T(8,128)(2,1)}, f32[384,768]{1,0:T(8,128)}, f32[384,768]{1,0:T(8,128)}, f32[384,768]{1,0:T(8,128)}) fusion(f32[384,768]{1,0:T(8,128)S(1)} %copy-done, f32[384,768]{1,0:T(8,128)} %param.15, f32[384,768]{1,0:T(8,128)} %param.16, bf16[384,768]{1,0:T(8,128)(2,1)} %collective-permute-done.47, bf16[384,768]{1,0:T(8,128)(2,1)} %copy-done.9, ...), kind=kLoop, calls=%fused_computation.125 | loop fusion | flops 11501568 | bytes 17104900 | tf_op jit(solution)/shard_map/convert_element_type | solution.py:871
  (180 shorter events, 86.2 us)
Async XLA Ops:
  67.1 28.4 %collective-permute-start.19 = (bf16[2,2,192,768]{3,2,1,0:T(8,128)(2,1)S(1)}, bf16[2,2,192,768]{3,2,1,0:T(8,128)(2,1)S(1)}, u32[]{:S(2)}, u32[]{:S(2)}) collective-permute-start(bf16[2,2,192,768]{3,2,1,0:T(8,128)(2,1)S(1)} %get-tuple-element.117), channel_id=1, source_target_pairs={{0,4},{2,6},{4,0},{6,2},{8,12},{10,14},{12,8},{14,10},{16,20},{18,... | collective-permute-start | bytes 3538952 | tf_op jit(solution)/shard_map/ppermute | solution.py:671
  68.4 27.3 %collective-permute-start.21 = (bf16[2,2,192,768]{3,2,1,0:T(8,128)(2,1)S(1)}, bf16[2,2,192,768]{3,2,1,0:T(8,128)(2,1)S(1)}, u32[]{:S(2)}, u32[]{:S(2)}) collective-permute-start(bf16[2,2,192,768]{3,2,1,0:T(8,128)(2,1)S(1)} %get-tuple-element.121), channel_id=1, source_target_pairs={{0,1},{1,0},{2,3},{3,2},{4,5},{5,4},{6,7},{7,6},{8,9},{9,8},{10,11... | collective-permute-start | bytes 3538952 | tf_op jit(solution)/shard_map/ppermute | solution.py:668
  70.7 27.9 %collective-permute-start.5 = (bf16[1,192,768]{2,1,0:T(8,128)(2,1)S(1)}, bf16[1,192,768]{2,1,0:T(8,128)(2,1)S(1)}, u32[]{:S(2)}, u32[]{:S(2)}) collective-permute-start(bf16[1,192,768]{2,1,0:T(8,128)(2,1)S(1)} %get-tuple-element.137), channel_id=1, source_target_pairs={{0,1},{1,0},{2,3},{3,2},{4,5},{5,4},{6,7},{7,6},{8,9},{9,8},{10,11... | collective-permute-start | bytes 884744 | tf_op jit(solution)/shard_map/ppermute | solution.py:668
  70.8 30.2 %collective-permute-start.7 = (bf16[1,192,768]{2,1,0:T(8,128)(2,1)S(1)}, bf16[1,192,768]{2,1,0:T(8,128)(2,1)S(1)}, u32[]{:S(2)}, u32[]{:S(2)}) collective-permute-start(bf16[1,192,768]{2,1,0:T(8,128)(2,1)S(1)} %get-tuple-element.136), channel_id=1, source_target_pairs={{0,4},{2,6},{4,0},{6,2},{8,12},{10,14},{12,8},{14,10},{16,20},{18,... | collective-permute-start | bytes 884744 | tf_op jit(solution)/shard_map/ppermute | solution.py:671
  98.6 129.9 %collective-permute-start.22 = (bf16[2,2,2,2,192,768]{5,4,3,2,1,0:T(8,128)(2,1)}, bf16[2,2,2,2,192,768]{5,4,3,2,1,0:T(8,128)(2,1)}, u32[]{:S(2)}, u32[]{:S(2)}) collective-permute-start(bf16[2,2,2,2,192,768]{5,4,3,2,1,0:T(8,128)(2,1)} %pad_maximum_fusion.own), channel_id=1, source_target_pairs={{0,2},{2,0},{4,6},{6,4},{8,10},{10,8},{12,14},{14,12},{16,18},{18,... | collective-permute-start | bytes 14155784 | tf_op jit(solution)/shard_map/ppermute | solution.py:674
  98.7 23.6 %collective-permute-start.6 = (bf16[2,1,192,768]{3,2,1,0:T(8,128)(2,1)S(1)}, bf16[2,1,192,768]{3,2,1,0:T(8,128)(2,1)S(1)}, u32[]{:S(2)}, u32[]{:S(2)}) collective-permute-start(bf16[2,1,192,768]{3,2,1,0:T(8,128)(2,1)S(1)} %get-tuple-element.133), channel_id=1, source_target_pairs={{0,4},{2,6},{4,0},{6,2},{8,12},{10,14},{12,8},{14,10},{16,20},{18,... | collective-permute-start | bytes 1769480 | tf_op jit(solution)/shard_map/ppermute | solution.py:671
  101.0 21.4 %collective-permute-start.8 = (bf16[2,1,192,768]{3,2,0,1:T(8,128)(2,1)S(1)}, bf16[2,1,192,768]{3,2,0,1:T(8,128)(2,1)S(1)}, u32[]{:S(2)}, u32[]{:S(2)}) collective-permute-start(bf16[2,1,192,768]{3,2,0,1:T(8,128)(2,1)S(1)} %get-tuple-element.139), channel_id=1, source_target_pairs={{0,1},{1,0},{2,3},{3,2},{4,5},{5,4},{6,7},{7,6},{8,9},{9,8},{10,11... | collective-permute-start | bytes 1769480 | tf_op jit(solution)/shard_map/ppermute | solution.py:668
  109.8 23.6 %collective-permute-start.12 = (bf16[2,1,192,768]{3,2,0,1:T(8,128)(2,1)S(1)}, bf16[2,1,192,768]{3,2,0,1:T(8,128)(2,1)S(1)}, u32[]{:S(2)}, u32[]{:S(2)}) collective-permute-start(bf16[2,1,192,768]{3,2,0,1:T(8,128)(2,1)S(1)} %get-tuple-element.125), channel_id=1, source_target_pairs={{0,4},{2,6},{4,0},{6,2},{8,12},{10,14},{12,8},{14,10},{16,20},{18,... | collective-permute-start | bytes 1769480 | tf_op jit(solution)/shard_map/ppermute | solution.py:671
  122.8 71.3 %collective-permute-start.9 = (bf16[2,2,2,1,192,768]{5,4,3,2,1,0:T(8,128)(2,1)S(1)}, bf16[2,2,2,1,192,768]{5,4,3,2,1,0:T(8,128)(2,1)}, u32[]{:S(2)}, u32[]{:S(2)}) collective-permute-start(bf16[2,2,2,1,192,768]{5,4,3,2,1,0:T(8,128)(2,1)S(1)} %pad_maximum_fusion.1.own), channel_id=1, source_target_pairs={{0,2},{2,0},{4,6},{6,4},{8,10},{10,8},{12,14},{14,12},{16,18},{18,... | collective-permute-start | bytes 7077896 | tf_op jit(solution)/shard_map/ppermute | solution.py:674
  138.5 74.1 %collective-permute-start.15 = (bf16[2,2,2,1,192,768]{5,4,2,1,3,0:T(8,128)(2,1)}, bf16[2,2,2,1,192,768]{5,4,2,1,3,0:T(8,128)(2,1)}, u32[]{:S(2)}, u32[]{:S(2)}) collective-permute-start(bf16[2,2,2,1,192,768]{5,4,2,1,3,0:T(8,128)(2,1)} %get-tuple-element.110), channel_id=1, source_target_pairs={{0,2},{2,0},{4,6},{6,4},{8,10},{10,8},{12,14},{14,12},{16,18},{18,... | collective-permute-start | bytes 7077896 | tf_op jit(solution)/shard_map/ppermute | solution.py:674
  139.5 54.6 %collective-permute-start = (bf16[8,32,768]{2,1,0:T(8,128)(2,1)}, bf16[8,32,768]{2,1,0:T(8,128)(2,1)}, u32[]{:S(2)}, u32[]{:S(2)}) collective-permute-start(bf16[8,32,768]{2,1,0:T(8,128)(2,1)} %get-tuple-element.123), channel_id=1, source_target_pairs={{0,2},{2,4},{4,6},{6,8},{8,10},{10,12},{12,14},{14,16},{16,18},{18... | collective-permute-start | bytes 1179656 | tf_op jit(solution)/shard_map/ppermute | solution.py:775
  142.6 51.4 %collective-permute-start.1 = (bf16[8,32,768]{2,1,0:T(8,128)(2,1)}, bf16[8,32,768]{2,1,0:T(8,128)(2,1)}, u32[]{:S(2)}, u32[]{:S(2)}) collective-permute-start(bf16[8,32,768]{2,1,0:T(8,128)(2,1)} %get-tuple-element.122), channel_id=1, source_target_pairs={{2,0},{4,2},{6,4},{8,6},{10,8},{12,10},{14,12},{16,14},{18,16},{20... | collective-permute-start | bytes 1179656 | tf_op jit(solution)/shard_map/ppermute | solution.py:775
  255.1 49.9 %collective-permute-start.39 = (bf16[2,2,2,2,192,768]{5,4,3,2,1,0:T(8,128)(2,1)}, bf16[2,2,2,2,192,768]{5,4,3,2,1,0:T(8,128)(2,1)}, u32[]{:S(2)}, u32[]{:S(2)}) collective-permute-start(bf16[2,2,2,2,192,768]{5,4,3,2,1,0:T(8,128)(2,1)} %get-tuple-element.69), channel_id=1, source_target_pairs={{0,2},{2,0},{4,6},{6,4},{8,10},{10,8},{12,14},{14,12},{16,18},{18,... | collective-permute-start | bytes 14155784 | tf_op jit(solution)/shard_map/ppermute | solution.py:674
  302.7 27.8 %collective-permute-start.28 = (bf16[2,1,192,768]{3,2,0,1:T(8,128)(2,1)S(1)}, bf16[2,1,192,768]{3,2,0,1:T(8,128)(2,1)S(1)}, u32[]{:S(2)}, u32[]{:S(2)}) collective-permute-start(bf16[2,1,192,768]{3,2,0,1:T(8,128)(2,1)S(1)} %fusion.21), channel_id=1, source_target_pairs={{0,4},{2,6},{4,0},{6,2},{8,12},{10,14},{12,8},{14,10},{16,20},{18,... | collective-permute-start | bytes 1769480 | tf_op jit(solution)/shard_map/ppermute | solution.py:671
  303.8 24.5 %collective-permute-start.33 = (bf16[2,1,192,768]{3,2,1,0:T(8,128)(2,1)S(1)}, bf16[2,1,192,768]{3,2,1,0:T(8,128)(2,1)S(1)}, u32[]{:S(2)}, u32[]{:S(2)}) collective-permute-start(bf16[2,1,192,768]{3,2,1,0:T(8,128)(2,1)S(1)} %fusion.22), channel_id=1, source_target_pairs={{0,1},{1,0},{2,3},{3,2},{4,5},{5,4},{6,7},{7,6},{8,9},{9,8},{10,11... | collective-permute-start | bytes 1769480 | tf_op jit(solution)/shard_map/ppermute | solution.py:668
  307.3 46.0 %collective-permute-start.40 = (bf16[2,2,192,768]{3,2,1,0:T(8,128)(2,1)S(1)}, bf16[2,2,192,768]{3,2,1,0:T(8,128)(2,1)S(1)}, u32[]{:S(2)}, u32[]{:S(2)}) collective-permute-start(bf16[2,2,192,768]{3,2,1,0:T(8,128)(2,1)S(1)} %get-tuple-element.100), channel_id=1, source_target_pairs={{0,1},{1,0},{2,3},{3,2},{4,5},{5,4},{6,7},{7,6},{8,9},{9,8},{10,11... | collective-permute-start | bytes 3538952 | tf_op jit(solution)/shard_map/ppermute | solution.py:668
  308.4 23.3 %collective-permute-start.35 = (bf16[2,1,192,768]{3,2,0,1:T(8,128)(2,1)S(1)}, bf16[2,1,192,768]{3,2,0,1:T(8,128)(2,1)S(1)}, u32[]{:S(2)}, u32[]{:S(2)}) collective-permute-start(bf16[2,1,192,768]{3,2,0,1:T(8,128)(2,1)S(1)} %fusion.23), channel_id=1, source_target_pairs={{0,4},{2,6},{4,0},{6,2},{8,12},{10,14},{12,8},{14,10},{16,20},{18,... | collective-permute-start | bytes 1769480 | tf_op jit(solution)/shard_map/ppermute | solution.py:671
  315.9 40.6 %collective-permute-start.27 = (bf16[1,192,768]{2,1,0:T(8,128)(2,1)S(1)}, bf16[1,192,768]{2,1,0:T(8,128)(2,1)S(1)}, u32[]{:S(2)}, u32[]{:S(2)}) collective-permute-start(bf16[1,192,768]{2,1,0:T(8,128)(2,1)S(1)} %fusion.38), channel_id=1, source_target_pairs={{0,4},{2,6},{4,0},{6,2},{8,12},{10,14},{12,8},{14,10},{16,20},{18,... | collective-permute-start | bytes 884744 | tf_op jit(solution)/shard_map/ppermute | solution.py:671
  328.5 29.2 %collective-permute-start.34 = (bf16[1,192,768]{2,1,0:T(8,128)(2,1)S(1)}, bf16[1,192,768]{2,1,0:T(8,128)(2,1)S(1)}, u32[]{:S(2)}, u32[]{:S(2)}) collective-permute-start(bf16[1,192,768]{2,1,0:T(8,128)(2,1)S(1)} %fusion.30), channel_id=1, source_target_pairs={{0,4},{2,6},{4,0},{6,2},{8,12},{10,14},{12,8},{14,10},{16,20},{18,... | collective-permute-start | bytes 884744 | tf_op jit(solution)/shard_map/ppermute | solution.py:671
  330.5 39.0 %collective-permute-start.42 = (bf16[2,2,192,768]{3,2,1,0:T(8,128)(2,1)S(1)}, bf16[2,2,192,768]{3,2,1,0:T(8,128)(2,1)S(1)}, u32[]{:S(2)}, u32[]{:S(2)}) collective-permute-start(bf16[2,2,192,768]{3,2,1,0:T(8,128)(2,1)S(1)} %get-tuple-element.101), channel_id=1, source_target_pairs={{0,4},{2,6},{4,0},{6,2},{8,12},{10,14},{12,8},{14,10},{16,20},{18,... | collective-permute-start | bytes 3538952 | tf_op jit(solution)/shard_map/ppermute | solution.py:671
  354.8 26.5 %collective-permute-start.41 = (bf16[2,192,768]{2,1,0:T(8,128)(2,1)S(1)}, bf16[2,192,768]{2,1,0:T(8,128)(2,1)S(1)}, u32[]{:S(2)}, u32[]{:S(2)}) collective-permute-start(bf16[2,192,768]{2,1,0:T(8,128)(2,1)S(1)} %fusion.11), channel_id=1, source_target_pairs={{0,4},{2,6},{4,0},{6,2},{8,12},{10,14},{12,8},{14,10},{16,20},{18,... | collective-permute-start | bytes 1769480 | tf_op jit(solution)/shard_map/ppermute | solution.py:671
  356.7 26.8 %collective-permute-start.29 = (bf16[1,192,768]{2,1,0:T(8,128)(2,1)S(1)}, bf16[1,192,768]{2,1,0:T(8,128)(2,1)S(1)}, u32[]{:S(2)}, u32[]{:S(2)}) collective-permute-start(bf16[1,192,768]{2,1,0:T(8,128)(2,1)S(1)} %get-tuple-element.103), channel_id=1, source_target_pairs={{0,1},{1,0},{2,3},{3,2},{4,5},{5,4},{6,7},{7,6},{8,9},{9,8},{10,11... | collective-permute-start | bytes 884744 | tf_op jit(solution)/shard_map/ppermute | solution.py:668
  357.9 27.1 %collective-permute-start.36 = (bf16[1,192,768]{2,1,0:T(8,128)(2,1)S(1)}, bf16[1,192,768]{2,1,0:T(8,128)(2,1)S(1)}, u32[]{:S(2)}, u32[]{:S(2)}) collective-permute-start(bf16[1,192,768]{2,1,0:T(8,128)(2,1)S(1)} %get-tuple-element.105), channel_id=1, source_target_pairs={{0,1},{1,0},{2,3},{3,2},{4,5},{5,4},{6,7},{7,6},{8,9},{9,8},{10,11... | collective-permute-start | bytes 884744 | tf_op jit(solution)/shard_map/ppermute | solution.py:668
  383.7 23.1 %collective-permute-start.30 = (bf16[384,768]{1,0:T(8,128)(2,1)S(1)}, bf16[384,768]{1,0:T(8,128)(2,1)S(1)}, u32[]{:S(2)}, u32[]{:S(2)}) collective-permute-start(bf16[384,768]{1,0:T(8,128)(2,1)S(1)} %fusion.15), channel_id=1, source_target_pairs={{8,0},{10,2},{12,4},{14,6},{24,16},{26,18},{28,20},{30,22},{9,1},{... | collective-permute-start | bytes 1769480 | tf_op jit(solution)/shard_map/ppermute | solution.py:679
  386.3 22.9 %collective-permute-start.37 = (bf16[384,768]{1,0:T(8,128)(2,1)S(1)}, bf16[384,768]{1,0:T(8,128)(2,1)S(1)}, u32[]{:S(2)}, u32[]{:S(2)}) collective-permute-start(bf16[384,768]{1,0:T(8,128)(2,1)S(1)} %fusion.14), channel_id=1, source_target_pairs={{0,8},{2,10},{4,12},{6,14},{24,16},{26,18},{28,20},{30,22},{1,9},{... | collective-permute-start | bytes 1769480 | tf_op jit(solution)/shard_map/ppermute | solution.py:679
  403.3 24.6 %collective-permute-start.46 = (bf16[384,768]{1,0:T(8,128)(2,1)S(1)}, bf16[384,768]{1,0:T(8,128)(2,1)S(1)}, u32[]{:S(2)}, u32[]{:S(2)}) collective-permute-start(bf16[384,768]{1,0:T(8,128)(2,1)S(1)} %get-tuple-element.109), channel_id=1, source_target_pairs={{16,24},{18,26},{20,28},{22,30},{0,8},{2,10},{4,12},{6,14},{17,25}... | collective-permute-start | bytes 1769480 | tf_op jit(solution)/shard_map/ppermute | solution.py:679
  404.6 26.1 %collective-permute-start.23 = (bf16[2,8,32,768]{3,2,1,0:T(8,128)(2,1)S(1)}, bf16[2,8,32,768]{3,2,1,0:T(8,128)(2,1)}, u32[]{:S(2)}, u32[]{:S(2)}) collective-permute-start(bf16[2,8,32,768]{3,2,1,0:T(8,128)(2,1)S(1)} %copy-done.19), channel_id=1, source_target_pairs={{0,2},{2,4},{4,6},{6,8},{8,10},{10,12},{12,14},{14,16},{16,18},{18... | collective-permute-start | bytes 2359304 | tf_op jit(solution)/shard_map/ppermute | solution.py:775
  406.9 25.5 %collective-permute-start.24 = (bf16[2,8,32,768]{3,2,1,0:T(8,128)(2,1)}, bf16[2,8,32,768]{3,2,1,0:T(8,128)(2,1)}, u32[]{:S(2)}, u32[]{:S(2)}) collective-permute-start(bf16[2,8,32,768]{3,2,1,0:T(8,128)(2,1)} %get-tuple-element.62), channel_id=1, source_target_pairs={{2,0},{4,2},{6,4},{8,6},{10,8},{12,10},{14,12},{16,14},{18,16},{20... | collective-permute-start | bytes 2359304 | tf_op jit(solution)/shard_map/ppermute | solution.py:775
  409.2 82.7 %collective-permute-start.31 = (bf16[384,768]{1,0:T(8,128)(2,1)}, bf16[384,768]{1,0:T(8,128)(2,1)}, u32[]{:S(2)}, u32[]{:S(2)}) collective-permute-start(bf16[384,768]{1,0:T(8,128)(2,1)} %fusion.18), channel_id=1, source_target_pairs={{16,0},{18,2},{20,4},{22,6},{17,1},{19,3},{21,5},{23,7}} | collective-permute-start | bytes 1769480 | tf_op jit(solution)/shard_map/ppermute | solution.py:679
  417.0 74.8 %collective-permute-start.38 = (bf16[384,768]{1,0:T(8,128)(2,1)}, bf16[384,768]{1,0:T(8,128)(2,1)}, u32[]{:S(2)}, u32[]{:S(2)}) collective-permute-start(bf16[384,768]{1,0:T(8,128)(2,1)} %fusion.19), channel_id=1, source_target_pairs={{16,8},{18,10},{20,12},{22,14},{17,9},{19,11},{21,13},{23,15}} | collective-permute-start | bytes 1769480 | tf_op jit(solution)/shard_map/ppermute | solution.py:679
  429.2 62.6 %collective-permute-start.45 = (bf16[384,768]{1,0:T(8,128)(2,1)}, bf16[384,768]{1,0:T(8,128)(2,1)}, u32[]{:S(2)}, u32[]{:S(2)}) collective-permute-start(bf16[384,768]{1,0:T(8,128)(2,1)} %get-tuple-element.106), channel_id=1, source_target_pairs={{8,16},{10,18},{12,20},{14,22},{9,17},{11,19},{13,21},{15,23}} | collective-permute-start | bytes 1769480 | tf_op jit(solution)/shard_map/ppermute | solution.py:679
  430.7 61.1 %collective-permute-start.47 = (bf16[384,768]{1,0:T(8,128)(2,1)}, bf16[384,768]{1,0:T(8,128)(2,1)}, u32[]{:S(2)}, u32[]{:S(2)}) collective-permute-start(bf16[384,768]{1,0:T(8,128)(2,1)} %get-tuple-element.107), channel_id=1, source_target_pairs={{8,24},{10,26},{12,28},{14,30},{9,25},{11,27},{13,29},{15,31}} | collective-permute-start | bytes 1769480 | tf_op jit(solution)/shard_map/ppermute | solution.py:679
  (37 other events, 625.2 us)

commit v3 on v1

v3 whole, which is shorter than its diff:
```python
from functools import partial

import jax
import jax.numpy as jnp
from jax import lax
from jax.experimental import pallas as pl
from jax.experimental.pallas import tpu as pltpu
from jax.sharding import PartitionSpec as P

D = 768
H = 12
DH = 64
FF = 3072
NMAT = 16
ROWS = 4
CB = 64
HALO = 32
MB = 2
EXT = CB + 2 * HALO
SEQ = MB * ROWS
TOK = SEQ * CB
PAIRS = H // 2
LANES = 128
FOLD = FF // D
SPAN = D // 2
PART = SPAN // 2

EPS = 1e-05
BETA_ONE = 0.9
BETA_TWO = 0.999
ADAM_EPS = 1e-08
DECAY = 0.01
RATE_GAIN = 0.3
STEP_NUMBER = 10.0
MASKED = -1e30
F32 = jnp.float32
LOW = jnp.bfloat16


def dot_nn(a, b):
    return lax.dot_general(a, b, (((1,), (0,)), ((), ())), preferred_element_type=F32)


def dot_nt(a, b):
    return lax.dot_general(a, b, (((1,), (1,)), ((), ())), preferred_element_type=F32)


def dot_tn(a, b):
    return lax.dot_general(a, b, (((0,), (0,)), ((), ())), preferred_element_type=F32)


def standardize(values):
    center = values - jnp.mean(values, axis=-1, keepdims=True)
    spread = lax.rsqrt(jnp.mean(center * center, axis=-1, keepdims=True) + EPS)
    return center * spread, spread


def norm_pull(upward, values, gain):
    scaled, spread = standardize(values)
    weighted = upward * gain
    result = spread * (
        weighted
        - jnp.mean(weighted, axis=-1, keepdims=True)
        - scaled * jnp.mean(weighted * scaled, axis=-1, keepdims=True)
    )
    return result, jnp.sum(upward * scaled, axis=0, keepdims=True)


def lane_window(pair):
    return pl.ds(pl.multiple_of(pair * LANES, LANES), LANES)


def side_by_side(ref, micro, window):
    return jnp.concatenate([ref[micro * ROWS + r, :, window] for r in range(ROWS)], axis=1)


def head_stack(packed):
    lane = lax.broadcasted_iota(jnp.int32, packed.shape, 1)
    first = (lane % LANES) < DH
    zero = jnp.zeros_like(packed)
    return jnp.concatenate([jnp.where(first, packed, zero), jnp.where(first, zero, packed)], axis=0)


def head_merge(stacked, r):
    block = stacked[:, r * LANES : (r + 1) * LANES]
    lane = lax.broadcasted_iota(jnp.int32, (CB, LANES), 1)
    return jnp.where(lane < DH, block[:CB], block[CB:])


def head_sums():
    feature = lax.broadcasted_iota(jnp.int32, (D, LANES), 0)
    head = lax.broadcasted_iota(jnp.int32, (D, LANES), 1)
    return (feature // DH == head).astype(F32).astype(LOW)


def head_spread():
    head = lax.broadcasted_iota(jnp.int32, (LANES, D), 0)
    feature = lax.broadcasted_iota(jnp.int32, (LANES, D), 1)
    return (feature // DH == head).astype(F32).astype(LOW)


def fetch_matrix(place, sources, table, matrix, target, sems, base):
    y_rel = jnp.where(place[1] == matrix // 2, 0, 1)
    waits = []
    for x in range(2):
        x_rel = jnp.where(place[0] == x, 0, 1)
        block = 2 * y_rel + x_rel
        rows = target.at[pl.ds(x * SPAN, SPAN)]
        for index in sorted(set(table)):
            here = None
            for plane, chosen in enumerate(table):
                if chosen == index:
                    hit = place[3] == plane
                    here = hit if here is None else jnp.logical_or(here, hit)
            for core_rel in range(2):
                held = jnp.logical_and(here, place[2] == (matrix % 2) ^ core_rel)
                sides, corner = sources[4 * index + 2 * core_rel : 4 * index + 2 * core_rel + 2]
                side = jnp.minimum(block, 2)
                near = pltpu.make_async_copy(sides.at[side], rows, sems.at[base + x])
                far = pltpu.make_async_copy(corner, rows, sems.at[base + x])
                pl.when(jnp.logical_and(held, block < 3))(near.start)
                pl.when(jnp.logical_and(held, block == 3))(far.start)
        waits.append(far)
    return waits


def fetch(place, sources, table, matrices, w, sems, first=0):
    waits = []
    for slot, matrix in enumerate(matrices):
        slot += first
        waits.append(
            fetch_matrix(place, sources, table, matrix, w.at[slot], sems, 2 * slot)
        )
    return waits


def settle(waits):
    for copy in waits:
        copy.wait()


def emit_matrix(place, source, matrix, n, keep, send, sems, base):
    core_same = place[2] == matrix % 2
    y_rel = jnp.where(place[1] == matrix // 2, 0, 1)
    waits = []
    for x in range(2):
        x_rel = jnp.where(place[0] == x, 0, 1)
        block = source.at[pl.ds(x * SPAN, SPAN)]
        kept = pltpu.make_async_copy(block, keep.at[y_rel, x_rel, n], sems.at[base + x])
        sent = pltpu.make_async_copy(block, send.at[y_rel, x_rel, n], sems.at[base + x])
        pl.when(core_same)(kept.start)
        pl.when(jnp.logical_not(core_same))(sent.start)
        waits.append(kept)
    return waits


def row_project(
    table, count, scal, place, tokens, from_low, from_high, gain, *refs
):
    sources, (a1e, q, ke, ve, w, sems) = refs[:count], refs[count:]
    copies = fetch(place, sources, table, range(3), w, sems)

    def norm_step(i, _):
        for source, start, size in (
            (from_low, 0, HALO),
            (tokens, HALO, CB),
            (from_high, HALO + CB, HALO),
        ):
            scaled, _s = standardize(source[i].astype(F32))
            a1e[i, start : start + size] = (scaled * gain[0:1]).astype(LOW)
        return 0

    lax.fori_loop(0, SEQ, norm_step, 0)
    wide = a1e[...].reshape(SEQ * EXT, D)
    settle(copies[1])
    ke[...] = dot_nn(wide, w[1]).astype(LOW).reshape(SEQ, EXT, D)
    settle(copies[2])
    ve[...] = dot_nn(wide, w[2]).astype(LOW).reshape(SEQ, EXT, D)
    inner = a1e[:, HALO : HALO + CB, :].reshape(TOK, D)
    settle(copies[0])
    q[...] = dot_nn(inner, w[0]).astype(LOW).reshape(SEQ, CB, D)
    for i in range(SEQ):
        q[i] = (q[i].astype(F32) * scal[i // ROWS, 1 + i % ROWS]).astype(LOW)


def row_attend(
    table, count, scal, place, tokens, q, ke, ve, allowed, gain, *refs
):
    sources, (p1, o1, x1, a2, w, sems) = refs[:count], refs[count:]
    copies = fetch(place, sources, table, (3,), w, sems)

    def attend(pair, _):
        window = lane_window(pair)
        for m in range(MB):
            query = head_stack(side_by_side(q, m, window))
            scores = dot_nt(query, side_by_side(ke, m, window)) * scal[m, 0]
            mask = allowed[m]
            mask = jnp.concatenate([mask, mask], axis=0)
            scores = jnp.where(mask > 0, scores, MASKED)
            weight = jnp.exp(scores - jnp.max(scores, axis=-1, keepdims=True))
            prob = weight / jnp.sum(weight, axis=-1, keepdims=True)
            p1[m, pair] = prob
            mixed = dot_nn(prob.astype(LOW), side_by_side(ve, m, window))
            for r in range(ROWS):
                o1[m * ROWS + r, :, window] = head_merge(mixed, r).astype(LOW)
        return 0

    lax.fori_loop(0, PAIRS, attend, 0)
    settle(copies[0])
    x1[...] = tokens[...].astype(F32) + dot_nn(o1[...].reshape(TOK, D), w[0]).reshape(SEQ, CB, D)

    def next_norm(i, _):
        scaled, _s = standardize(x1[i])
        a2[i] = (scaled * gain[1:2]).astype(LOW)
        return 0

    lax.fori_loop(0, SEQ, next_norm, 0)


def col_forward(table, count, scal, place, x1, a2, gain, *refs):
    sources, (q2, k2, v2, p2, o2, x2, a3, w, sems) = refs[:count], refs[count:]
    copies = fetch(place, sources, table, range(4), w, sems)
    for j in range(3):
        settle(copies[j])
    flat = a2[...].reshape(TOK, D)
    q2[...] = dot_nn(flat, w[0]).astype(LOW).reshape(SEQ, CB, D)
    k2[...] = dot_nn(flat, w[1]).astype(LOW).reshape(SEQ, CB, D)
    v2[...] = dot_nn(flat, w[2]).astype(LOW).reshape(SEQ, CB, D)
    sums = head_sums()
    spread = head_spread()

    def attend(i, _):
        micro = i // ROWS
        query = q2[i].astype(F32)
        products = jnp.concatenate(
            [(query * k2[micro * ROWS + s].astype(F32)).astype(LOW) for s in range(ROWS)], axis=0
        )
        scores = dot_nn(products, sums) * (DH ** (-0.5))
        parts = [
            jnp.where(scal[micro, 1 + s] > 0, scores[s * CB : (s + 1) * CB], MASKED)
            for s in range(ROWS)
        ]
        top = jnp.maximum(jnp.maximum(parts[0], parts[1]), jnp.maximum(parts[2], parts[3]))
        parts = [jnp.exp(part - top) for part in parts]
        scale = 1.0 / (parts[0] + parts[1] + parts[2] + parts[3])
        prob = jnp.concatenate([part * scale for part in parts], axis=0)
        p2[i] = prob
        wide = dot_nn(prob.astype(LOW), spread)
        total = wide[:CB] * v2[micro * ROWS].astype(F32)
        for s in range(1, ROWS):
            total = total + wide[s * CB : (s + 1) * CB] * v2[micro * ROWS + s].astype(F32)
        o2[i] = total.astype(LOW)
        return 0

    lax.fori_loop(0, SEQ, attend, 0)
    settle(copies[3])
    x2[...] = x1[...] + dot_nn(o2[...].reshape(TOK, D), w[3]).reshape(SEQ, CB, D)

    def next_norm(i, _):
        scaled, _s = standardize(x2[i])
        a3[i] = (scaled * gain[2:3]).astype(LOW)
        return 0

    lax.fori_loop(0, SEQ, next_norm, 0)


CHUNK = 128


def feed_forward(tables, count, scal, place, x2, a3, cot, gain, *refs):
    sources, refs = refs[:count], refs[count:]
    out, e2, dgain, keep, send, up, down, live_cot, gl, dhd, w, dw, in_sems, out_sems = refs
    copies = []
    for n in range(2):
        copies += fetch(place, sources, tables[n], range(4), w, in_sems, 4 * n)
    for i in range(SEQ):
        live_cot[i * CB : (i + 1) * CB] = (
            cot[i].astype(F32) * scal[i // ROWS, 1 + i % ROWS]
        ).astype(LOW)
    normed = a3[...].reshape(TOK, D)
    grad = live_cot[...]
    waits = []
    for step in range(FOLD):
        settle(copies[step])
        settle(copies[FOLD + step])
        win = w[step]
        wout = w[FOLD + step]
        for base in range(0, TOK, CHUNK):
            rows = slice(base, base + CHUNK)
            hidden = dot_nn(normed[rows], win)
            pulled = dot_nt(grad[rows], wout)
            half = 0.5 * lax.erf(hidden * (0.5**0.5)) + 0.5
            gl[rows] = (hidden * half).astype(LOW)
            slope = half + hidden * (jnp.exp(-0.5 * hidden * hidden) * ((2.0 * jnp.pi) ** -0.5))
            dhd[rows] = (pulled * slope).astype(LOW)
        for n, value in enumerate((dot_tn(normed, dhd[...]), dot_tn(gl[...], grad))):
            slot = 4 * n + step
            dw[slot] = value.astype(LOW)
            waits += emit_matrix(place, dw.at[slot], step, n, keep, send, out_sems, 2 * slot)
        forward = dot_nn(gl[...], wout)
        backward = dot_nt(dhd[...], win)
        if step == 0:
            up[...] = forward
            down[...] = backward
        else:
            up[...] += forward
            down[...] += backward
    total = jnp.zeros((1, D), F32)
    for i in range(SEQ):
        rows = slice(i * CB, (i + 1) * CB)
        value = x2[i]
        out[i] = ((value + up[rows]) * scal[i // ROWS, 1 + i % ROWS]).astype(LOW)
        part, gain_part = norm_pull(down[rows], value, gain[2:3])
        e2[i] = live_cot[rows].astype(F32) + part
        total = total + gain_part
    dgain[...] = total
    settle(waits)


def col_attend_back(table, count, scal, place, e2, q2, k2, v2, p2, *refs):
    sources, refs = refs[:count], refs[count:]
    dq2, dk2, dv2, do2, dka, dva, w, in_sems = refs
    copies = fetch(place, sources, table, (3,), w, in_sems)
    low = e2[...].reshape(TOK, D).astype(LOW)
    settle(copies[0])
    do2[...] = dot_nt(low, w[0]).astype(LOW).reshape(SEQ, CB, D)
    sums = head_sums()
    spread = head_spread()
    dka[...] = jnp.zeros_like(dka)
    dva[...] = jnp.zeros_like(dva)

    def pull(i, _):
        micro = i // ROWS
        upward = do2[i].astype(F32)
        products = jnp.concatenate(
            [(upward * v2[micro * ROWS + s].astype(F32)).astype(LOW) for s in range(ROWS)], axis=0
        )
        dprob = dot_nn(products, sums)
        prob = p2[i]
        mixed = prob * dprob
        inner = mixed[:CB] + mixed[CB : 2 * CB] + mixed[2 * CB : 3 * CB] + mixed[3 * CB :]
        dscore = prob * (dprob - jnp.concatenate([inner] * ROWS, axis=0))
        wide = dot_nn(prob.astype(LOW), spread)
        dwide = dot_nn(dscore.astype(LOW), spread)
        query = q2[i].astype(F32)
        total = jnp.zeros((CB, D), F32)
        for s in range(ROWS):
            rows = slice(s * CB, (s + 1) * CB)
            total = total + dwide[rows] * k2[micro * ROWS + s].astype(F32)
            dka[micro * ROWS + s] += dwide[rows] * query
            dva[micro * ROWS + s] += wide[rows] * upward
        dq2[i] = (total * (DH ** (-0.5))).astype(LOW)
        return 0

    lax.fori_loop(0, SEQ, pull, 0)
    dk2[...] = (dka[...] * (DH ** (-0.5))).astype(LOW)
    dv2[...] = dva[...].astype(LOW)


def col_project_back(table, count, scal, place, e2, o2, dq2, dk2, dv2, a2, x1, gain, *refs):
    sources, refs = refs[:count], refs[count:]
    e1, dgain, keep, send, acc, w, dw, in_sems, out_sems = refs
    copies = fetch(place, sources, table, range(3), w, in_sems)
    flat = a2[...].reshape(TOK, D)
    low = e2[...].reshape(TOK, D).astype(LOW)
    dw[3] = dot_tn(o2[...].reshape(TOK, D), low).astype(LOW)
    waits = emit_matrix(place, dw.at[3], 3, 0, keep, send, out_sems, 6)
    for j, ref in enumerate((dq2, dk2, dv2)):
        grads = ref[...].reshape(TOK, D)
        dw[j] = dot_tn(flat, grads).astype(LOW)
        waits += emit_matrix(place, dw.at[j], j, 0, keep, send, out_sems, 2 * j)
        settle(copies[j])
        part = dot_nt(grads, w[j]).reshape(SEQ, CB, D)
        if j == 0:
            acc[...] = part
        else:
            acc[...] += part
    gain_total = jnp.zeros((1, D), F32)
    for i in range(SEQ):
        part, gain_part = norm_pull(acc[i], x1[i], gain[1:2])
        e1[i] = e2[i] + part
        gain_total = gain_total + gain_part
    dgain[...] = gain_total
    settle(waits)


def row_backward(table, count, scal, place, e1, o1, q, ke, ve, p1, a1e, *refs):
    sources, refs = refs[:count], refs[count:]
    dq, inner, to_low, to_high, keep, send, do1, dke, dve, w, dw, in_sems, out_sems = refs
    copies = fetch(place, sources, table, (3,), w, in_sems)
    low = e1[...].reshape(TOK, D).astype(LOW)
    settle(copies[0])
    do1[...] = dot_nt(low, w[0]).astype(LOW).reshape(SEQ, CB, D)

    def pull(pair, _):
        window = lane_window(pair)
        for m in range(MB):
            query = head_stack(side_by_side(q, m, window))
            upward = head_stack(side_by_side(do1, m, window))
            prob = p1[m, pair]
            dprob = dot_nt(upward, side_by_side(ve, m, window))
            dscore = prob * (dprob - jnp.sum(prob * dprob, axis=-1, keepdims=True))
            dscore = dscore.astype(LOW)
            dvalue = dot_tn(prob.astype(LOW), upward)
            dkey = dot_tn(dscore, query) * scal[m, 0]
            dquery = dot_nn(dscore, side_by_side(ke, m, window)) * scal[m, 0]
            for r in range(ROWS):
                lanes = slice(r * LANES, (r + 1) * LANES)
                dve[m * ROWS + r, :, window] = dvalue[:, lanes].astype(LOW)
                dke[m * ROWS + r, :, window] = dkey[:, lanes].astype(LOW)
                dq[m * ROWS + r, :, window] = (head_merge(dquery, r) * scal[m, 1 + r]).astype(LOW)
        return 0

    lax.fori_loop(0, PAIRS, pull, 0)
    for j, ref in enumerate((dke, dve)):
        inner[j] = ref[:, HALO : HALO + CB, :]
        to_low[j] = ref[:, :HALO, :]
        to_high[j] = ref[:, HALO + CB :, :]
    wide = a1e[...].reshape(SEQ * EXT, D)
    own = a1e[:, HALO : HALO + CB, :].reshape(TOK, D)
    waits = []
    for j, (left, right) in enumerate(
        (
            (own, dq[...].reshape(TOK, D)),
            (wide, dke[...].reshape(SEQ * EXT, D)),
            (wide, dve[...].reshape(SEQ * EXT, D)),
            (o1[...].reshape(TOK, D), low),
        )
    ):
        dw[j] = dot_tn(left, right).astype(LOW)
        waits += emit_matrix(place, dw.at[j], j, 0, keep, send, out_sems, 2 * j)
    settle(waits)


def input_backward(
    table, count, scal, place, dq, inner, from_low, from_high, e1, tokens, gain, *refs
):
    sources, (grad, dgain, full, acc, w, sems) = refs[:count], refs[count:]
    copies = fetch(place, sources, table, range(3), w, sems)
    for j in range(2):
        full[j, :, :HALO] = (
            inner[j, :, :HALO].astype(F32) + from_low[j].astype(F32)
        ).astype(LOW)
        full[j, :, HALO:] = (
            inner[j, :, HALO:].astype(F32) + from_high[j].astype(F32)
        ).astype(LOW)
    for j in range(3):
        settle(copies[j])
    acc[...] = dot_nt(dq[...].reshape(TOK, D), w[0]).reshape(SEQ, CB, D)
    for j in range(2):
        acc[...] += dot_nt(full[j].reshape(TOK, D), w[1 + j]).reshape(SEQ, CB, D)
    gain_total = jnp.zeros((1, D), F32)
    for i in range(SEQ):
        part, gain_part = norm_pull(acc[i], tokens[i].astype(F32), gain[0:1])
        grad[i] = (e1[i] + part).astype(LOW)
        gain_total = gain_total + gain_part
    dgain[...] = gain_total


def in_vmem(count):
    return [pl.BlockSpec(memory_space=pltpu.VMEM)] * count


def like(*shapes):
    return tuple(jax.ShapeDtypeStruct(shape, dtype) for shape, dtype in shapes)


SEQ_CB = (SEQ, CB, D)
SEQ_EXT = (SEQ, EXT, D)
RIM = (2, SEQ, HALO, D)
PER_MICRO = 1.15e9
VM = pltpu.VMEM
DMA = pltpu.SemaphoreType.DMA


def pieces(count):
    return (2, 2, count, SPAN, D)


def run_kernel(body, scalars, args, weights, outs, raw_out, scratch, micros):
    vmem = pl.BlockSpec(memory_space=pltpu.VMEM)
    raw = pl.BlockSpec(memory_space=pltpu.HBM)
    moved = sum(a.size * a.dtype.itemsize for a in args)
    moved += sum(o.size * jnp.dtype(o.dtype).itemsize for o in outs)
    call = body
    sources = ()
    if weights is not None:
        table, sources = weights
        call = partial(body, table, len(sources))
    return pl.pallas_call(
        call,
        name=body.__name__,
        out_shape=outs,
        in_specs=[pl.BlockSpec(memory_space=pltpu.SMEM)] * len(scalars)
        + [vmem] * len(args)
        + [raw] * len(sources),
        out_specs=tuple(raw if i in raw_out else vmem for i in range(len(outs))),
        scratch_shapes=scratch,
        compiler_params=pltpu.CompilerParams(vmem_limit_bytes=60 << 20),
        cost_estimate=pl.CostEstimate(
            flops=int(micros * PER_MICRO), bytes_accessed=moved, transcendentals=0
        ),
    )(*scalars, *args, *sources)


def held(count):
    return [VM((count, D, D), LOW), DMA((2 * count,))]


def terms(count):
    return [VM((count, D, D), LOW), DMA((2 * count,))]


def swap_pairs(count, bit):
    return [(i, i ^ bit) for i in range(count)]


def after(value, *before):
    return lax.optimization_barrier((value, *before))[0]


def add(*parts):
    total = parts[0].astype(F32)
    for part in parts[1:]:
        total = total + part.astype(F32)
    return total


def add_half(block, half, arrived):
    first, second = block[:, :PART], block[:, PART:]
    if half == 0:
        first = first + arrived.astype(F32)
    else:
        second = second + arrived.astype(F32)
    return jnp.concatenate([first, second], axis=1)


def together(*values):
    return lax.optimization_barrier(values)


def held_by(side, corner):
    return (side[0], corner[0], side[1], corner[1])


class Staged:
    planes = 4
    tables = ((0, 1, 2, 2), (1, 0, 1, 3), (2, 2, 0, 1), (3, 3, 3, 0))

    def __init__(self):
        self.count = NMAT
        self.step = NMAT // self.planes
        cols = lax.axis_index("cols")
        self.z = cols // self.step
        self.place = jnp.stack(
            [lax.axis_index("fsdp"), (cols // 2) % 2, cols % 2, self.z]
        ).astype(jnp.int32)

    def over_x(self, value):
        return lax.ppermute(value, "fsdp", [(0, 1), (1, 0)])

    def over_y(self, value):
        return lax.ppermute(value, "cols", swap_pairs(self.count, 2))

    def over_core(self, value):
        return lax.ppermute(value, "cols", swap_pairs(self.count, 1))

    def over_z(self, value, pairs):
        step = self.step
        full = [(a * step + i, b * step + i) for a, b in pairs for i in range(step)]
        return lax.ppermute(value, "cols", full)

    def by_plane(self, options):
        result = options[-1]
        for index in range(len(options) - 2, -1, -1):
            result = jnp.where(self.z == index, options[index], result)
        return result

    def own_place(self, gains):
        index = lax.axis_index("cols") * 2 + lax.axis_index("fsdp")
        spread = jnp.zeros((3 * D,), F32)
        spread = lax.dynamic_update_slice(spread, gains, (index * gains.shape[0],))
        return spread.reshape(18, LANES)

    def sum_step(self, value, index):
        swaps = (
            self.over_core,
            self.over_x,
            self.over_y,
            lambda v: self.over_z(v, [(0, 1), (1, 0), (2, 3), (3, 2)]),
            lambda v: self.over_z(v, [(0, 2), (2, 0), (1, 3), (3, 1)]),
        )
        return value + swaps[index](value)

    def sum_gains(self, value):
        value = value.reshape(18, LANES)
        for index in range(5):
            value = self.sum_step(value, index)
        return value.reshape(3 * D)

    def own_gains(self, value, size):
        index = lax.axis_index("cols") * 2 + lax.axis_index("fsdp")
        return lax.dynamic_slice(self.sum_gains(value), (index * size,), (size,))

    def collect(self, *blocks):
        own = jnp.stack(blocks)
        return own, self.over_core(own)

    def corner(self, corner_a, corner_b):
        own = jnp.concatenate([corner_a, corner_b], axis=0)
        return own, self.over_core(own)

    def gather(self, shard, gains, tokens):
        z = self.z
        gains = self.own_place(gains)
        up1 = self.over_z(shard, [(0, 1), (1, 2), (2, 3)])
        down1 = self.over_z(shard, [(3, 2), (2, 1), (1, 0)])
        x1, y1 = self.over_x(shard), self.over_y(shard)
        gains = self.sum_step(gains, 0)
        up1, down1, x1, y1, gains = together(up1, down1, x1, y1, gains)
        second = jnp.where(z == 0, down1, up1)
        x2, y2 = self.over_x(second), self.over_y(second)
        a1, b1 = self.over_y(x1[:PART]), self.over_x(y1[PART:])
        up2 = self.over_z(up1, [(1, 2), (2, 3)])
        down2 = self.over_z(down1, [(2, 1), (1, 0)])
        gains = self.sum_step(gains, 1)
        up2, down2, a1, b1, x2, y2, gains = together(up2, down2, a1, b1, x2, y2, gains)
        side1 = self.collect(shard, x1, y1)
        up3 = self.over_z(up2, [(2, 3)])
        down3 = self.over_z(down2, [(1, 0)])
        a2, b2 = self.over_y(x2[:PART]), self.over_x(y2[PART:])
        rims = neighbours(*after((tokens[:, CB - HALO :], tokens[:, :HALO]), x2))
        gains = self.sum_step(gains, 2)
        up3, down3, a2, b2, gains, *rims = together(up3, down3, a2, b2, gains, *rims)
        third = self.by_plane([down2, down1, up2, up3])
        x3, y3 = self.over_x(third), self.over_y(third)
        gains = self.sum_step(gains, 3)
        corner1 = self.corner(a1, b1)
        side2 = self.collect(second, x2, y2)
        x3, y3, gains = together(x3, y3, gains)
        a3, b3 = self.over_y(x3[:PART]), self.over_x(y3[PART:])
        gains = self.sum_step(gains, 4)
        corner2 = self.corner(a2, b2)
        side3 = self.collect(third, x3, y3)
        fourth = self.by_plane([down3, down2, down1, up2])
        a3, b3, fourth, gains = together(a3, b3, fourth, gains)
        x4, y4 = self.over_x(fourth), self.over_y(fourth)
        corner3 = self.corner(a3, b3)
        self.row_gate = (fourth,)
        self.fourth = fourth, x4, y4
        first3 = (
            *held_by(side1, corner1),
            *held_by(side2, corner2),
            *held_by(side3, corner3),
        )
        self.first3 = first3
        return (self.tables[0], first3), gains.reshape(3 * D), rims

    def gather_last(self, seen):
        fourth, x4, y4 = self.fourth
        x4, y4, seen = together(x4, y4, seen)
        xa, yb = x4[:PART], y4[PART:]
        self.attend_gate = (xa, yb)
        a4, b4 = self.over_y(xa), self.over_x(yb)
        side4 = self.collect(fourth, x4, y4)
        corner4 = self.corner(a4, b4)
        every = (*self.first3, *held_by(side4, corner4))
        return (self.tables[1], every), (self.tables[2:], every)

    def corner_swap(self, keep, got):
        mixed = add(keep[1, 1], got[1, 1]).astype(LOW)
        return mixed[:, :PART], mixed[:, PART:]

    def side_blocks(self, keep, got, corner_a, corner_b):
        over_x = add_half(add(keep[0, 1], got[0, 1]), 0, corner_a).astype(LOW)
        over_y = add_half(add(keep[1, 0], got[1, 0]), 1, corner_b).astype(LOW)
        return over_x, over_y

    def plane_sum(self, value, b):
        hub = 2 if b < 2 else 1
        near = self.over_z(value.astype(LOW), [(b ^ 1, b), (3 if hub == 2 else 0, hub)])
        value = add(value, near)
        return add(value, self.over_z(value.astype(LOW), [(hub, b)]))

    def reduce_forward(self, keep, send):
        self.fwd_keep = keep
        self.fwd_got = self.over_core(send)
        self.fwd_corner = self.corner_swap(keep, self.fwd_got)
        return self.fwd_corner

    def reduce_forward_sides(self):
        a, b = self.fwd_corner
        self.fwd_sides = self.side_blocks(
            self.fwd_keep, self.fwd_got, self.over_y(a), self.over_x(b)
        )
        return self.fwd_sides

    def reduce_col(self, keep, send):
        self.col_keep = keep
        self.col_got = self.over_core(send)

    def reduce_col_corner(self, *before):
        got = after(self.col_got, *before)
        self.col_corner = self.corner_swap(self.col_keep, got)
        return self.col_corner

    def reduce_rest(self, keep, send):
        fx, fy = self.fwd_sides
        fx, fy = self.over_x(fx), self.over_y(fy)
        got = self.over_core(send)
        a, b = self.col_corner
        cx, cy = self.side_blocks(self.col_keep, self.col_got, self.over_y(a), self.over_x(b))
        cx, cy = self.over_x(cx), self.over_y(cy)
        a, b = self.corner_swap(keep, got)
        self.rim_gate = (a, b)
        rx, ry = self.side_blocks(keep, got, self.over_y(a), self.over_x(b))
        forward = add(self.fwd_keep[0, 0], self.fwd_got[0, 0], fx, fy)
        col = add(self.col_keep[0, 0], self.col_got[0, 0], cx, cy)
        rx, ry = self.over_x(rx), self.over_y(ry)
        row = add(keep[0, 0], got[0, 0], rx, ry)
        return self.by_plane(
            [
                self.plane_sum(row[0], 0),
                self.plane_sum(col[0], 1),
                self.plane_sum(forward[0], 2),
                self.plane_sum(forward[1], 3),
            ]
        )


class Native:
    axes = ("cols", "fsdp")
    row_gate = ()
    attend_gate = ()
    rim_gate = ()
    last_gate = ()

    def __init__(self):
        self.place = jnp.zeros((4,), jnp.int32)
        self.parts = []

    def own_gains(self, value, size):
        return lax.psum_scatter(value, self.axes, scatter_dimension=0, tiled=True)

    def gather(self, shard, gains, tokens):
        full = lax.all_gather(shard, self.axes, axis=0, tiled=True)
        gains = lax.all_gather(gains, self.axes, axis=0, tiled=True)
        rims = neighbours(tokens[:, CB - HALO :], tokens[:, :HALO])
        row, *self.rest = self.arranged(full)
        return row, gains, rims

    def gather_last(self, seen):
        return self.rest

    def arranged(self, full):
        blocks = full.reshape(4, 2, 2, 2 * SPAN, D).transpose(0, 2, 1, 3, 4)
        blocks = blocks.reshape(4, 2, 4, SPAN, D)
        row, col, low, high = [
            (blocks[b, 0, :3], blocks[b, 0, 3], blocks[b, 1, :3], blocks[b, 1, 3])
            for b in range(4)
        ]
        flat = (0, 0, 0, 0)
        return (flat, row), (flat, col), ((flat, (1, 1, 1, 1)), (*low, *high))

    def reduce_forward(self, keep, send):
        self.parts = [jnp.stack([keep, send], axis=1).transpose(3, 0, 1, 2, 4, 5)]
        return ()

    def reduce_forward_sides(self):
        return ()

    def reduce_col(self, keep, send):
        self.parts.insert(0, jnp.stack([keep, send], axis=1).transpose(3, 0, 1, 2, 4, 5))

    def reduce_col_corner(self, *before):
        return ()

    def reduce_rest(self, keep, send):
        self.parts.insert(0, jnp.stack([keep, send], axis=1).transpose(3, 0, 1, 2, 4, 5))
        full = jnp.concatenate(self.parts, axis=0).reshape(NMAT * D, D)
        return lax.psum_scatter(full, self.axes, scatter_dimension=0, tiled=True).astype(F32)


def neighbours(upward, downward):
    count = lax.axis_size("cols")
    forward = [(i, i + 1) for i in range(count - 1)]
    backward = [(target, source) for source, target in forward]
    return lax.ppermute(upward, "cols", forward), lax.ppermute(downward, "cols", backward)


def adamw(master, moment, square, grad_total, rate, decay, steps_done):
    moment_new = BETA_ONE * moment + (1.0 - BETA_ONE) * grad_total
    square_new = BETA_TWO * square + (1.0 - BETA_TWO) * grad_total * grad_total
    moment_fix = 1.0 - BETA_ONE**steps_done
    square_fix = 1.0 - BETA_TWO**steps_done
    update = moment_new / moment_fix / (jnp.sqrt(square_new / square_fix) + ADAM_EPS)
    return (master - rate * (update + decay * master), moment_new, square_new)


def band_mask(band_reach):
    first_col = lax.axis_index("cols") * CB
    col_total = CB * lax.axis_size("cols")
    query_pos = first_col + jnp.arange(CB, dtype=jnp.int32)
    key_pos = first_col - HALO + jnp.arange(EXT, dtype=jnp.int32)
    lowest = query_pos[None] - band_reach[:, 0]
    highest = query_pos[None] + band_reach[:, 1]
    key = key_pos[None, None]
    allowed = (key >= lowest[..., None]) & (key <= highest[..., None])
    allowed = allowed & (key >= 0) & (key < col_total)
    return allowed.astype(F32)


def layer(tokens, cot, counts, reach, mover, shard, gains):
    row_w, gain, rims = mover.gather(shard, gains, tokens)
    gain = gain.reshape(3, D)
    from_low, from_high = rims
    present = (jnp.arange(ROWS, dtype=jnp.int32)[None] < counts[:, None]).astype(F32)
    row_scale = DH ** (-0.5) * lax.rsqrt(counts.astype(F32))
    scalars = (jnp.concatenate([row_scale[:, None], present], axis=1), mover.place)
    run = partial(run_kernel, scalars=scalars)
    low, wide = (SEQ_CB, LOW), (SEQ_EXT, LOW)
    term = (pieces(1), LOW)
    row_gain = ((1, D), F32)
    probs = ((MB, PAIRS, 2 * CB, EXT), F32)
    col_probs = ((SEQ, ROWS * CB, LANES), F32)

    a1e, q, ke, ve = run(
        row_project,
        args=(after(tokens, *mover.row_gate), from_low, from_high, gain),
        weights=row_w,
        outs=like(wide, low, wide, wide),
        raw_out=(),
        scratch=held(3),
        micros=9.5,
    )
    col_w, forward_w = mover.gather_last(q)
    p1, o1, x1, a2 = run(
        row_attend,
        args=(tokens, after(q, *mover.attend_gate), ke, ve, band_mask(reach), gain),
        weights=row_w,
        outs=like(probs, low, (SEQ_CB, F32), low),
        raw_out=(),
        scratch=held(1),
        micros=12.5,
    )
    q2, k2, v2, p2, o2, x2, a3 = run(
        col_forward,
        args=(x1, a2, gain),
        weights=col_w,
        outs=like(low, low, low, col_probs, low, (SEQ_CB, F32), low),
        raw_out=(),
        scratch=held(4),
        micros=15.5,
    )
    token = (TOK, D)
    out, e2, dg3, *forward_g = run(
        feed_forward,
        args=(x2, a3, cot, gain),
        weights=forward_w,
        outs=like(low, (SEQ_CB, F32), row_gain, (pieces(2), LOW), (pieces(2), LOW)),
        raw_out=(3, 4),
        scratch=[VM(token, F32)] * 2 + [VM(token, LOW)] * 3 + [held(8)[0], terms(8)[0]]
        + [DMA((16,))] * 2,
        micros=26,
    )
    gate = mover.reduce_forward(*forward_g)
    dq2, dk2, dv2 = run(
        col_attend_back,
        args=(e2, q2, k2, v2, p2),
        weights=col_w,
        outs=like(low, low, low),
        raw_out=(),
        scratch=[VM(SEQ_CB, LOW)] + [VM(SEQ_CB, F32)] * 2 + held(1),
        micros=10.5,
    )
    dq2 = after(dq2, *gate)
    e1, dg2, *col_g = run(
        col_project_back,
        args=(e2, o2, dq2, dk2, dv2, a2, x1, gain),
        weights=col_w,
        outs=like((SEQ_CB, F32), row_gain, term, term),
        raw_out=(2, 3),
        scratch=[VM(SEQ_CB, F32), held(3)[0], terms(4)[0], DMA((6,)), DMA((8,))],
        micros=11.5,
    )
    mover.reduce_col(*col_g)
    gate = mover.reduce_forward_sides()
    gate = (*gate, *mover.reduce_col_corner())
    dq, inner, to_low, to_high, *row_g = run(
        row_backward,
        args=(after(e1, *gate), o1, q, ke, ve, p1, a1e),
        weights=row_w,
        outs=like(low, ((2, *SEQ_CB), LOW), (RIM, LOW), (RIM, LOW), term, term),
        raw_out=(4, 5),
        scratch=[VM(SEQ_CB, LOW)] + [VM(SEQ_EXT, LOW)] * 2
        + [held(1)[0], terms(4)[0], DMA((2,)), DMA((8,))],
        micros=20,
    )
    weight_grad = mover.reduce_rest(*row_g)
    to_high = after(to_high, *mover.rim_gate)
    to_low = after(to_low, *mover.rim_gate)
    from_low, from_high = neighbours(to_high, to_low)
    grad, dg1 = run(
        input_backward,
        args=(dq, inner, from_low, from_high, e1, tokens, gain),
        weights=row_w,
        outs=like(low, row_gain),
        raw_out=(),
        scratch=[VM((2, *SEQ_CB), LOW), VM(SEQ_CB, F32)] + held(3),
        micros=8.5,
    )
    return out, grad, weight_grad, jnp.concatenate([dg1, dg2, dg3], axis=0)


def per_device(
    alignment,
    cotangent,
    row_counts,
    band_reach,
    master_weights,
    weight_moment,
    weight_square,
    norm_gains,
    gain_moment,
    gain_square,
):
    staged = lax.axis_size("cols") == NMAT and lax.axis_size("fsdp") == 2
    mover = Staged() if staged else Native()
    out, grad, weight_total, gain_grad = layer(
        alignment.reshape(SEQ, CB, D),
        cotangent.reshape(SEQ, CB, D),
        row_counts[:, 0],
        band_reach[:, 0],
        mover,
        master_weights.astype(LOW),
        norm_gains.astype(LOW).astype(F32),
    )
    gain_total = mover.own_gains(gain_grad.reshape(3 * D), norm_gains.shape[0])
    new_weights, new_moment, new_square = adamw(
        master_weights,
        weight_moment,
        weight_square,
        weight_total.reshape(master_weights.shape),
        D ** (-0.5),
        DECAY,
        STEP_NUMBER,
    )
    new_gains, new_gain_moment, new_gain_square = adamw(
        norm_gains, gain_moment, gain_square, gain_total, RATE_GAIN, 0.0, STEP_NUMBER
    )
    shape = (MB, 1, ROWS, CB, D)
    return (
        out.reshape(shape),
        grad.reshape(shape),
        new_weights,
        new_moment,
        new_square,
        new_weights.astype(LOW),
        new_gains,
        new_gain_moment,
        new_gain_square,
    )


def solution(mesh):
    tokens = P(None, "fsdp", None, "cols", None)
    rows = P(("cols", "fsdp"), None)
    flat = P(("cols", "fsdp"))
    in_specs = (
        tokens,
        tokens,
        P(None, "fsdp"),
        P(None, "fsdp", None, "cols"),
        rows,
        rows,
        rows,
        flat,
        flat,
        flat,
    )
    out_specs = (tokens, tokens, rows, rows, rows, rows, flat, flat, flat)
    return jax.shard_map(
        per_device, mesh=mesh, in_specs=in_specs, out_specs=out_specs, check_vma=False
    )
```

time: 483 us -> 389 us (0.81)
  blocking collectives: 102 us -> 0 us
  starting transfers between devices: 8.11 us -> 90 us
  waiting for transfers between devices: 202 us -> 123 us
  between operations: 14.2 us -> 2.03 us
  other arithmetic: 29.4 us -> 40.2 us
  Pallas kernels: 104 us -> 112 us
  local copies, waits for them, and re-layouts: 22.7 us -> 17.5 us
    reduce_scatter x1 -> x0, waiting for transfers between devices: 127 us -> none  [per_device(): lax.psum_scatter(weight_grad.reshape(NMAT * D, D), axes, scatter_dimensio...]
    ppermute x4 -> x67, waiting for transfers between devices: 0.01 us -> 123 us  [the longest x16 57.4 us: over_y(): return lax.ppermute(value, 'cols', swap_pairs(self.count, 2))]
    unnamed x2 -> x0, blocking collectives: 102 us -> none
    ppermute x4 -> x67, starting transfers between devices: 8.03 us -> 90 us  [the longest x18 35.3 us: over_z(): return lax.ppermute(value, 'cols', full)]
    all_gather x1 -> x0, waiting for transfers between devices: 75.2 us -> none  [per_device(): lax.all_gather(master_weights.astype(LOW), axes, axis=0, tiled=True)]
    concatenate x4 -> x8, other arithmetic: 20.1 us -> 2.55 us  [the longest x6 1.33 us: add_half(): return jnp.concatenate([first, second], axis=1)]
    slice x3 -> x18, local copies, waits for them, and re-layouts: 18 us -> 5.48 us  [the longest x6 1.67 us: add_half(): first, second = (block[:, :PART], block[:, PART:])]
    add x0 -> x13, other arithmetic: none -> 11 us  [the longest x4 10.2 us: add(): total = total + part.astype(F32)]
  transfers between devices with their start and end apart: 6 -> 67, of which waited for: 2 -> 31; matrix products, arithmetic and copies ran while one was open for 3% -> 10% of each run, Pallas kernels for 2% -> 15%
where the time goes in v3:
time: 389 us; the launch traced here: 384 us
  waiting for transfers between devices  123 us (32%)
  Pallas kernels  112 us (29%)
  starting transfers between devices  90 us (23%)
  other arithmetic  40.2 us (10%)
  local copies, waits for them, and re-layouts  17.5 us (4%)
    pallas_call x8, Pallas kernels, run_kernel(): pl.pallas_call(call, name=body.__name__, out_shape=outs, in_specs=[pl.Blo...  112 us
    ppermute x16, waiting for transfers between devices, over_y(): return lax.ppermute(value, 'cols', swap_pairs(self.count, 2))  57.4 us
    ppermute x18, starting transfers between devices, over_z(): return lax.ppermute(value, 'cols', full)  35.3 us
    ppermute x18, waiting for transfers between devices, over_z(): return lax.ppermute(value, 'cols', full)  32.9 us
    ppermute x16, waiting for transfers between devices, over_x(): return lax.ppermute(value, 'fsdp', [(0, 1), (1, 0)])  29.9 us
    ppermute x16, starting transfers between devices, over_y(): return lax.ppermute(value, 'cols', swap_pairs(self.count, 2))  25.8 us
    ppermute x16, starting transfers between devices, over_x(): return lax.ppermute(value, 'fsdp', [(0, 1), (1, 0)])  21 us
    add x4, other arithmetic, add(): total = total + part.astype(F32)  10.2 us
  transfers between devices with their start and end apart: 67, of which 31 were waited for; matrix products, arithmetic and copies ran while one was open for 10% of the time, Pallas kernels for 15%

profile of v3, /device:TPU:0, one launch (start us, length us, event | category | flops | bytes accessed | tf_op | source)
XLA Modules:
  0.0 384.1 jit_solution(8553938113983142224)
XLA Ops:
  2.0 3.0 collective-permute-start.3
  7.8 4.6 %collective-permute-start = (bf16[384,768]{1,0:T(8,128)(2,1)S(1)}, bf16[384,768]{1,0:T(8,128)(2,1)S(1)}, u32[]{:S(2)}, u32[]{:S(2)}) collective-permute-start(bf16[384,768]{1,0:T(8,128)(2,1)S(1)} %convert_element_type.404), channel_id=1, source_target_pairs={{0,8},{2,10},{4,12},{6,14},{8,16},{10,18},{12,20},{14,22},{16,24},... | collective-permute-start | bytes 1769480 | tf_op jit(solution)/shard_map/ppermute | solution.py:571
  13.8 4.6 %collective-permute-done.3 = bf16[384,768]{1,0:T(8,128)(2,1)S(1)} collective-permute-done((bf16[384,768]{1,0:T(8,128)(2,1)S(1)}, bf16[384,768]{1,0:T(8,128)(2,1)S(1)}, u32[]{:S(2)}, u32[]{:S(2)}) %collective-permute-start.3) | collective-permute-done | bytes 589856 | tf_op jit(solution)/shard_map/ppermute | solution.py:563
  19.8 3.1 collective-permute-done.1
  29.3 5.4 %collective-permute-done.8 = bf16[192,768]{1,0:T(8,128)(2,1)S(1)} collective-permute-done((bf16[192,768]{1,0:T(8,128)(2,1)S(1)}, bf16[192,768]{1,0:T(8,128)(2,1)S(1)}, u32[]{:S(2)}, u32[]{:S(2)}) %collective-permute-start.8) | collective-permute-done | bytes 294944 | tf_op jit(solution)/shard_map/ppermute | solution.py:560
  35.0 10.6 %collective-permute-done.7 = bf16[192,768]{1,0:T(8,128)(2,1)S(1)} collective-permute-done((bf16[192,768]{1,0:T(8,128)(2,1)S(1)}, bf16[192,768]{1,0:T(8,128)(2,1)S(1)}, u32[]{:S(2)}, u32[]{:S(2)}) %collective-permute-start.7) | collective-permute-done | bytes 294944 | tf_op jit(solution)/shard_map/ppermute | solution.py:563
  58.6 7.3 %collective-permute-done.15 = bf16[192,768]{1,0:T(8,128)(2,1)S(1)} collective-permute-done((bf16[192,768]{1,0:T(8,128)(2,1)}, bf16[192,768]{1,0:T(8,128)(2,1)S(1)}, u32[]{:S(2)}, u32[]{:S(2)}) %collective-permute-start.15) | collective-permute-done | bytes 294944 | tf_op jit(solution)/shard_map/ppermute | solution.py:560
  67.4 4.1 %collective-permute-start.20 = (bf16[384,768]{1,0:T(8,128)(2,1)S(1)}, bf16[384,768]{1,0:T(8,128)(2,1)S(1)}, u32[]{:S(2)}, u32[]{:S(2)}) collective-permute-start(bf16[384,768]{1,0:T(8,128)(2,1)S(1)} %get-tuple-element.181), channel_id=1, source_target_pairs={{0,4},{2,6},{4,0},{6,2},{8,12},{10,14},{12,8},{14,10},{16,20},{18,... | collective-permute-start | bytes 1769480 | tf_op jit(solution)/shard_map/ppermute | solution.py:563
  78.4 6.7 %collective-permute-done.20 = bf16[384,768]{1,0:T(8,128)(2,1)S(1)} collective-permute-done((bf16[384,768]{1,0:T(8,128)(2,1)S(1)}, bf16[384,768]{1,0:T(8,128)(2,1)S(1)}, u32[]{:S(2)}, u32[]{:S(2)}) %collective-permute-start.20) | collective-permute-done | bytes 589856 | tf_op jit(solution)/shard_map/ppermute | solution.py:563
  103.4 5.1 %collective-permute-done.22 = bf16[192,768]{1,0:T(8,128)(2,1)S(1)} collective-permute-done((bf16[192,768]{1,0:T(8,128)(2,1)S(1)}, bf16[192,768]{1,0:T(8,128)(2,1)S(1)}, u32[]{:S(2)}, u32[]{:S(2)}) %collective-permute-start.22) | collective-permute-done | bytes 294944 | tf_op jit(solution)/shard_map/ppermute | solution.py:563
  116.2 9.4 %row_project.1 = (bf16[8,128,768]{2,1,0:T(8,128)(2,1)}, bf16[8,64,768]{2,1,0:T(8,128)(2,1)}, bf16[8,128,768]{2,1,0:T(8,128)(2,1)}, bf16[8,128,768]{2,1,0:T(8,128)(2,1)}) custom-call(f32[2,5]{1,0:T(2,128)} %pad_maximum_fusion.11.scal, s32[4]{0:T(128)} %pad_add_fusion.place, bf16[8,64,768]{2,1,0:T(8,128)(2,1)} %bitcast.120, ...), custom_call_target="tpu_custom_call" | custom-call | flops 10924999680 | bytes 7087104 | tf_op jit(solution)/shard_map/row_project/pallas_call | solution.py:490
  125.6 3.6 collective-permute-done.32
  134.2 4.6 %collective-permute-done.33 = bf16[192,768]{1,0:T(8,128)(2,1)S(1)} collective-permute-done((bf16[192,768]{1,0:T(8,128)(2,1)S(1)}, bf16[192,768]{1,0:T(8,128)(2,1)S(1)}, u32[]{:S(2)}, u32[]{:S(2)}) %collective-permute-start.33) | collective-permute-done | bytes 294944 | tf_op jit(solution)/shard_map/ppermute | solution.py:563
  139.0 12.3 %row_attend.1 = (f32[2,6,128,128]{3,2,1,0:T(8,128)}, bf16[8,64,768]{2,1,0:T(8,128)(2,1)}, f32[8,64,768]{2,1,0:T(8,128)}, bf16[8,64,768]{2,1,0:T(8,128)(2,1)}) custom-call(f32[2,5]{1,0:T(2,128)} %pad_maximum_fusion.11.scal, s32[4]{0:T(128)} %pad_add_fusion.place, bf16[8,64,768]{2,1,0:T(8,128)(2,1)} %bitcast.121, bf16[8,64,768]{2,1,0:T(8,128)(2,1)} %get-tuple-element.112.q, ...), custom_call_target="tpu_custom_call" | custom-call | flops 14375000064 | bytes 8725504 | tf_op jit(solution)/shard_map/row_attend/pallas_call | solution.py:490
  152.1 15.4 %col_forward.1 = (bf16[8,64,768]{2,1,0:T(8,128)(2,1)}, bf16[8,64,768]{2,1,0:T(8,128)(2,1)}, bf16[8,64,768]{2,1,0:T(8,128)(2,1)}, f32[8,256,128]{2,1,0:T(8,128)},...) custom-call(f32[2,5]{1,0:T(2,128)} %pad_maximum_fusion.11.scal, ...), custom_call_target="tpu_custom_call" | custom-call | flops 17824999424 | bytes 8922112 | tf_op jit(solution)/shard_map/col_forward/pallas_call | solution.py:490
  167.5 25.9 %feed_forward.1 = (bf16[8,64,768]{2,1,0:T(8,128)(2,1)}, f32[8,64,768]{2,1,0:T(8,128)}, f32[1,768]{1,0:T(1,128)}, bf16[2,2,2,384,768]{4,3,2,1,0:T(8,128)(2,1)}, bf16[2,2,2,384,768]{4,3,2,1,0:T(8,128)(2,1)}) custom-call(f32[2,5]{1,0:T(2,128)} %pad_maximum_fusion.11.scal, s32[4]{0:T(128)} %pad_add_fusion.place, f32[8,64,768]{2,1,0:T(8,128)} %get-tuple-element.117.x2, ...), custom_call_target="tpu_custom_call" | custom-call | flops 29899999232 | bytes 14954496 | tf_op jit(solution)/shard_map/feed_forward/pallas_call | solution.py:490
  193.9 10.4 %col_attend_back.1 = (bf16[8,64,768]{2,1,0:T(8,128)(2,1)}, bf16[8,64,768]{2,1,0:T(8,128)(2,1)}, bf16[8,64,768]{2,1,0:T(8,128)(2,1)}) custom-call(f32[2,5]{1,0:T(2,128)} %pad_maximum_fusion.11.scal, s32[4]{0:T(128)} %pad_add_fusion.place, f32[8,64,768]{2,1,0:T(8,128)} %get-tuple-element.120.e2, bf16[8,64,768]{2,1,0:T(8,128)(2,1)} %get-tuple-element.122.q2, ...), custom_call_target="tpu_custom_call" | custom-call | flops 12074999808 | bytes 7340032 | tf_op jit(solution)/shard_map/col_attend_back/pallas_call | solution.py:490
  204.3 5.3 %add_bitcast_fusion = (f32[2,384,768]{2,1,0:T(8,128)S(1)}, f32[2,384,768]{2,1,0:T(8,128)}, bf16[2,384,768]{2,1,0:T(8,128)(2,1)S(1)}) fusion(bf16[2,2,2,384,768]{4,3,2,1,0:T(8,128)(2,1)} %collective-permute-done.37, bf16[2,2,2,384,768]{4,3,2,1,0:T(8,128)(2,1)} %get-tuple-element.127), kind=kLoop, calls=%fused_computation.2 | loop fusion | flops 5898240 | bytes 12976128 | tf_op jit(solution)/shard_map/add | solution.py:525
  209.7 11.4 %col_project_back.1 = (f32[8,64,768]{2,1,0:T(8,128)}, f32[1,768]{1,0:T(1,128)}, bf16[2,2,1,384,768]{4,3,2,1,0:T(8,128)(2,1)}, bf16[2,2,1,384,768]{4,3,2,1,0:T(8,128)(2,1)}) custom-call(f32[2,5]{1,0:T(2,128)} %pad_maximum_fusion.11.scal, s32[4]{0:T(128)} %pad_add_fusion.place, f32[8,64,768]{2,1,0:T(8,128)} %get-tuple-element.120.e2, ...), custom_call_target="tpu_custom_call" | custom-call | flops 13224999936 | bytes 13381632 | tf_op jit(solution)/shard_map/col_project_back/pallas_call | solution.py:490
  224.7 12.2 %collective-permute-done.38 = bf16[2,192,768]{2,1,0:T(8,128)(2,1)S(1)} collective-permute-done((bf16[2,192,768]{2,1,0:T(8,128)(2,1)S(1)}, bf16[2,192,768]{2,1,0:T(8,128)(2,1)S(1)}, u32[]{:S(2)}, u32[]{:S(2)}) %collective-permute-start.38) | collective-permute-done | bytes 589856 | tf_op jit(solution)/shard_map/ppermute | solution.py:563
  243.0 18.5 %row_backward.1 = (bf16[8,64,768]{2,1,0:T(8,128)(2,1)}, bf16[2,8,64,768]{3,2,1,0:T(8,128)(2,1)}, bf16[2,8,32,768]{3,2,1,0:T(8,128)(2,1)}, bf16[2,8,32,768]{3,2,1...) custom-call(f32[2,5]{1,0:T(2,128)} %pad_maximum_fusion.11.scal, ...), custom_call_target="tpu_custom_call" | custom-call | flops 23000000512 | bytes 17301504 | tf_op jit(solution)/shard_map/row_backward/pallas_call | solution.py:490
  262.6 3.2 collective-permute-done.56
  274.1 5.4 %collective-permute-done.52 = bf16[1,192,768]{2,1,0:T(8,128)(2,1)S(1)} collective-permute-done((bf16[1,192,768]{2,1,0:T(8,128)(2,1)S(1)}, bf16[1,192,768]{2,1,0:T(8,128)(2,1)S(1)}, u32[]{:S(2)}, u32[]{:S(2)}) %collective-permute-start.52) | collective-permute-done | bytes 294944 | tf_op jit(solution)/shard_map/ppermute | solution.py:560
  282.1 4.5 %collective-permute-start.58 = (bf16[384,768]{1,0:T(8,128)(2,1)S(1)}, bf16[384,768]{1,0:T(8,128)(2,1)S(1)}, u32[]{:S(2)}, u32[]{:S(2)}) collective-permute-start(bf16[384,768]{1,0:T(8,128)(2,1)S(1)} %get-tuple-element.178), channel_id=1, source_target_pairs={{24,16},{26,18},{28,20},{30,22},{0,8},{2,10},{4,12},{6,14},{25,17}... | collective-permute-start | bytes 1769480 | tf_op jit(solution)/shard_map/ppermute | solution.py:571
  294.4 4.6 %collective-permute-start.54 = (bf16[384,768]{1,0:T(8,128)(2,1)S(1)}, bf16[384,768]{1,0:T(8,128)(2,1)S(1)}, u32[]{:S(2)}, u32[]{:S(2)}) collective-permute-start(bf16[384,768]{1,0:T(8,128)(2,1)S(1)} %bitcast_convert_fusion), channel_id=1, source_target_pairs={{0,8},{2,10},{4,12},{6,14},{24,16},{26,18},{28,20},{30,22},{1,9},{... | collective-permute-start | bytes 1769480 | tf_op jit(solution)/shard_map/ppermute | solution.py:571
  303.8 6.9 %collective-permute-done.60 = bf16[384,768]{1,0:T(8,128)(2,1)S(1)} collective-permute-done((bf16[384,768]{1,0:T(8,128)(2,1)S(1)}, bf16[384,768]{1,0:T(8,128)(2,1)S(1)}, u32[]{:S(2)}, u32[]{:S(2)}) %collective-permute-start.60) | collective-permute-done | bytes 589856 | tf_op jit(solution)/shard_map/ppermute | solution.py:571
  321.2 6.6 %collective-permute-done.47 = bf16[1,384,768]{2,1,0:T(8,128)(2,1)S(1)} collective-permute-done((bf16[1,384,768]{2,1,0:T(8,128)(2,1)S(1)}, bf16[1,384,768]{2,1,0:T(8,128)(2,1)S(1)}, u32[]{:S(2)}, u32[]{:S(2)}) %collective-permute-start.47) | collective-permute-done | bytes 589856 | tf_op jit(solution)/shard_map/ppermute | solution.py:563
  332.7 8.4 %input_backward.1 = (bf16[8,64,768]{2,1,0:T(8,128)(2,1)}, f32[1,768]{1,0:T(1,128)}) custom-call(f32[2,5]{1,0:T(2,128)} %pad_maximum_fusion.11.scal, s32[4]{0:T(128)} %pad_add_fusion.place, bf16[8,64,768]{2,1,0:T(8,128)(2,1)} %get-tuple-element.139.dq, bf16[2,8,64,768]{3,2,1,0:T(8,128)(2,1)} %get-tuple-element.140.inner, bf16[2,8,32,768]{3,2,1,0:T(8,128)(2,1)} %copy-done.60, ...), custom_call_target="tpu_custom_call" | custom-call | flops 9774999552 | bytes 7090176 | tf_op jit(solution)/shard_map/input_backward/pallas_call | solution.py:490
  341.2 10.5 %collective-permute-done.48 = bf16[384,768]{1,0:T(8,128)(2,1)} collective-permute-done((bf16[384,768]{1,0:T(8,128)(2,1)}, bf16[384,768]{1,0:T(8,128)(2,1)}, u32[]{:S(2)}, u32[]{:S(2)}) %collective-permute-start.48) | collective-permute-done | bytes 589856 | tf_op jit(solution)/shard_map/ppermute | solution.py:571
  366.1 4.1 %collective-permute-done.65 = f32[18,128]{1,0:T(8,128)S(1)} collective-permute-done((f32[18,128]{1,0:T(8,128)S(1)}, f32[18,128]{1,0:T(8,128)S(1)}, u32[]{:S(2)}, u32[]{:S(2)}) %collective-permute-start.65) | collective-permute-done | bytes 9248 | tf_op jit(solution)/shard_map/ppermute | solution.py:571
  370.2 3.9 %collective-permute-start.66 = (f32[18,128]{1,0:T(8,128)S(1)}, f32[18,128]{1,0:T(8,128)S(1)}, u32[]{:S(2)}, u32[]{:S(2)}) collective-permute-start(f32[18,128]{1,0:T(8,128)S(1)} %add.367), channel_id=1, source_target_pairs={{0,16},{2,18},{4,20},{6,22},{16,0},{18,2},{20,4},{22,6},{8,24},{10... | collective-permute-start | bytes 27656 | tf_op jit(solution)/shard_map/ppermute | solution.py:571
  377.1 6.7 %fusion.21 = (bf16[384,768]{1,0:T(8,128)(2,1)}, f32[384,768]{1,0:T(8,128)}, f32[384,768]{1,0:T(8,128)}, f32[384,768]{1,0:T(8,128)}) fusion(f32[384,768]{1,0:T(8,128)S(1)} %copy-done.1, f32[384,768]{1,0:T(8,128)} %param.15, f32[384,768]{1,0:T(8,128)} %param.16, bf16[384,768]{1,0:T(8,128)(2,1)} %collective-permute-done.61, bf16[384,768]{1,0:T(8,128)(2,1)} %copy-done.15, ...), kind=kLoop, calls=%fused_computation.95 | loop fusion | flops 14450688 | bytes 19464196 | tf_op jit(solution)/shard_map/convert_element_type | solution.py:958
  (324 shorter events, 133.6 us)
Async XLA Ops:
  2.0 16.4 %collective-permute-start.3 = (bf16[384,768]{1,0:T(8,128)(2,1)S(1)}, bf16[384,768]{1,0:T(8,128)(2,1)S(1)}, u32[]{:S(2)}, u32[]{:S(2)}) collective-permute-start(bf16[384,768]{1,0:T(8,128)(2,1)S(1)} %convert_element_type.404), channel_id=1, source_target_pairs={{0,4},{2,6},{4,0},{6,2},{8,12},{10,14},{12,8},{14,10},{16,20},{18,... | collective-permute-start | bytes 1769480 | tf_op jit(solution)/shard_map/ppermute | solution.py:563
  6.5 16.4 %collective-permute-start.1 = (bf16[384,768]{1,0:T(8,128)(2,1)S(1)}, bf16[384,768]{1,0:T(8,128)(2,1)S(1)}, u32[]{:S(2)}, u32[]{:S(2)}) collective-permute-start(bf16[384,768]{1,0:T(8,128)(2,1)S(1)} %convert_element_type.404), channel_id=1, source_target_pairs={{24,16},{26,18},{28,20},{30,22},{16,8},{18,10},{20,12},{22,14},{8,... | collective-permute-start | bytes 1769480 | tf_op jit(solution)/shard_map/ppermute | solution.py:571
  7.8 16.3 %collective-permute-start = (bf16[384,768]{1,0:T(8,128)(2,1)S(1)}, bf16[384,768]{1,0:T(8,128)(2,1)S(1)}, u32[]{:S(2)}, u32[]{:S(2)}) collective-permute-start(bf16[384,768]{1,0:T(8,128)(2,1)S(1)} %convert_element_type.404), channel_id=1, source_target_pairs={{0,8},{2,10},{4,12},{6,14},{8,16},{10,18},{12,20},{14,22},{16,24},... | collective-permute-start | bytes 1769480 | tf_op jit(solution)/shard_map/ppermute | solution.py:571
  26.3 19.3 %collective-permute-start.10 = (bf16[384,768]{1,0:T(8,128)(2,1)S(1)}, bf16[384,768]{1,0:T(8,128)(2,1)S(1)}, u32[]{:S(2)}, u32[]{:S(2)}) collective-permute-start(bf16[384,768]{1,0:T(8,128)(2,1)S(1)} %broadcast_select_fusion), channel_id=1, source_target_pairs={{0,4},{2,6},{4,0},{6,2},{8,12},{10,14},{12,8},{14,10},{16,20},{18,... | collective-permute-start | bytes 1769480 | tf_op jit(solution)/shard_map/ppermute | solution.py:563
  26.9 18.7 %collective-permute-start.9 = (bf16[384,768]{1,0:T(8,128)(2,1)S(1)}, bf16[384,768]{1,0:T(8,128)(2,1)S(1)}, u32[]{:S(2)}, u32[]{:S(2)}) collective-permute-start(bf16[384,768]{1,0:T(8,128)(2,1)S(1)} %broadcast_select_fusion), channel_id=1, source_target_pairs={{0,1},{1,0},{2,3},{3,2},{4,5},{5,4},{6,7},{7,6},{8,9},{9,8},{10,11... | collective-permute-start | bytes 1769480 | tf_op jit(solution)/shard_map/ppermute | solution.py:560
  27.3 18.4 %collective-permute-start.5 = (bf16[384,768]{1,0:T(8,128)(2,1)}, bf16[384,768]{1,0:T(8,128)(2,1)S(1)}, u32[]{:S(2)}, u32[]{:S(2)}) collective-permute-start(bf16[384,768]{1,0:T(8,128)(2,1)} %copy-done.32), channel_id=1, source_target_pairs={{8,16},{10,18},{12,20},{14,22},{16,24},{18,26},{20,28},{22,30},{9,... | collective-permute-start | bytes 1769480 | tf_op jit(solution)/shard_map/ppermute | solution.py:571
  28.0 17.7 %collective-permute-start.6 = (bf16[384,768]{1,0:T(8,128)(2,1)S(1)}, bf16[384,768]{1,0:T(8,128)(2,1)S(1)}, u32[]{:S(2)}, u32[]{:S(2)}) collective-permute-start(bf16[384,768]{1,0:T(8,128)(2,1)S(1)} %collective-permute-done.1), channel_id=1, source_target_pairs={{16,8},{18,10},{20,12},{22,14},{8,0},{10,2},{12,4},{14,6},{17,9},{... | collective-permute-start | bytes 1769480 | tf_op jit(solution)/shard_map/ppermute | solution.py:571
  47.9 18.0 %collective-permute-start.13 = (bf16[384,768]{1,0:T(8,128)(2,1)S(1)}, bf16[384,768]{1,0:T(8,128)(2,1)S(1)}, u32[]{:S(2)}, u32[]{:S(2)}) collective-permute-start(bf16[384,768]{1,0:T(8,128)(2,1)S(1)} %collective-permute-done.6), channel_id=1, source_target_pairs={{8,0},{10,2},{12,4},{14,6},{9,1},{11,3},{13,5},{15,7}} | collective-permute-start | bytes 1769480 | tf_op jit(solution)/shard_map/ppermute | solution.py:571
  49.2 16.7 %collective-permute-start.12 = (bf16[384,768]{1,0:T(8,128)(2,1)S(1)}, bf16[384,768]{1,0:T(8,128)(2,1)}, u32[]{:S(2)}, u32[]{:S(2)}) collective-permute-start(bf16[384,768]{1,0:T(8,128)(2,1)S(1)} %collective-permute-done.5), channel_id=1, source_target_pairs={{16,24},{18,26},{20,28},{22,30},{17,25},{19,27},{21,29},{23,31}} | collective-permute-start | bytes 1769480 | tf_op jit(solution)/shard_map/ppermute | solution.py:571
  67.4 17.7 %collective-permute-start.20 = (bf16[384,768]{1,0:T(8,128)(2,1)S(1)}, bf16[384,768]{1,0:T(8,128)(2,1)S(1)}, u32[]{:S(2)}, u32[]{:S(2)}) collective-permute-start(bf16[384,768]{1,0:T(8,128)(2,1)S(1)} %get-tuple-element.181), channel_id=1, source_target_pairs={{0,4},{2,6},{4,0},{6,2},{8,12},{10,14},{12,8},{14,10},{16,20},{18,... | collective-permute-start | bytes 1769480 | tf_op jit(solution)/shard_map/ppermute | solution.py:563
  74.2 40.2 %collective-permute-start.25 = (bf16[3,384,768]{2,1,0:T(8,128)(2,1)S(1)}, bf16[3,384,768]{2,1,0:T(8,128)(2,1)}, u32[]{:S(2)}, u32[]{:S(2)}) collective-permute-start(bf16[3,384,768]{2,1,0:T(8,128)(2,1)S(1)} %pad_maximum_fusion.refs_0_), channel_id=1, source_target_pairs={{0,2},{2,0},{4,6},{6,4},{8,10},{10,8},{12,14},{14,12},{16,18},{18,... | collective-permute-start | bytes 5308424 | tf_op jit(solution)/shard_map/ppermute | solution.py:566
  78.3 37.9 %collective-permute-start.27 = (bf16[3,384,768]{2,1,0:T(8,128)(2,1)}, bf16[3,384,768]{2,1,0:T(8,128)(2,1)}, u32[]{:S(2)}, u32[]{:S(2)}) collective-permute-start(bf16[3,384,768]{2,1,0:T(8,128)(2,1)} %pad_maximum_fusion.1.refs_4_), channel_id=1, source_target_pairs={{0,2},{2,0},{4,6},{6,4},{8,10},{10,8},{12,14},{14,12},{16,18},{18,... | collective-permute-start | bytes 5308424 | tf_op jit(solution)/shard_map/ppermute | solution.py:566
  88.1 28.0 %collective-permute-start.29 = (bf16[3,384,768]{2,1,0:T(8,128)(2,1)}, bf16[3,384,768]{2,1,0:T(8,128)(2,1)}, u32[]{:S(2)}, u32[]{:S(2)}) collective-permute-start(bf16[3,384,768]{2,1,0:T(8,128)(2,1)} %pad_maximum_fusion.2.refs_8_), channel_id=1, source_target_pairs={{0,2},{2,0},{4,6},{6,4},{8,10},{10,8},{12,14},{14,12},{16,18},{18,... | collective-permute-start | bytes 5308424 | tf_op jit(solution)/shard_map/ppermute | solution.py:566
  133.0 18.4 %collective-permute-start.35 = (bf16[3,384,768]{2,1,0:T(8,128)(2,1)S(1)}, bf16[3,384,768]{2,1,0:T(8,128)(2,1)}, u32[]{:S(2)}, u32[]{:S(2)}) collective-permute-start(bf16[3,384,768]{2,1,0:T(8,128)(2,1)S(1)} %pad_maximum_fusion.3.refs_12_), channel_id=1, source_target_pairs={{0,2},{2,0},{4,6},{6,4},{8,10},{10,8},{12,14},{14,12},{16,18},{18,... | collective-permute-start | bytes 5308424 | tf_op jit(solution)/shard_map/ppermute | solution.py:566
  221.1 19.1 %collective-permute-start.40 = (bf16[2,2,1,384,768]{4,3,2,1,0:T(8,128)(2,1)}, bf16[2,2,1,384,768]{4,3,2,1,0:T(8,128)(2,1)S(1)}, u32[]{:S(2)}, u32[]{:S(2)}) collective-permute-start(bf16[2,2,1,384,768]{4,3,2,1,0:T(8,128)(2,1)} %get-tuple-element.134), channel_id=1, source_target_pairs={{0,2},{2,0},{4,6},{6,4},{8,10},{10,8},{12,14},{14,12},{16,18},{18,... | collective-permute-start | bytes 7077896 | tf_op jit(solution)/shard_map/ppermute | solution.py:566
  222.8 15.7 %collective-permute-start.39 = (bf16[2,192,768]{2,1,0:T(8,128)(2,1)S(1)}, bf16[2,192,768]{2,1,0:T(8,128)(2,1)S(1)}, u32[]{:S(2)}, u32[]{:S(2)}) collective-permute-start(bf16[2,192,768]{2,1,0:T(8,128)(2,1)S(1)} %get-tuple-element.182), channel_id=1, source_target_pairs={{0,1},{1,0},{2,3},{3,2},{4,5},{5,4},{6,7},{7,6},{8,9},{9,8},{10,11... | collective-permute-start | bytes 1769480 | tf_op jit(solution)/shard_map/ppermute | solution.py:560
  238.1 27.8 %collective-permute-start.56 = (bf16[2,384,768]{2,1,0:T(8,128)(2,1)}, bf16[2,384,768]{2,1,0:T(8,128)(2,1)}, u32[]{:S(2)}, u32[]{:S(2)}) collective-permute-start(bf16[2,384,768]{2,1,0:T(8,128)(2,1)} %pad_maximum_fusion.4), channel_id=1, source_target_pairs={{0,1},{1,0},{2,3},{3,2},{4,5},{5,4},{6,7},{7,6},{8,9},{9,8},{10,11... | collective-permute-start | bytes 3538952 | tf_op jit(solution)/shard_map/ppermute | solution.py:560
  238.7 28.4 %collective-permute-start.57 = (bf16[2,384,768]{2,1,0:T(8,128)(2,1)S(1)}, bf16[2,384,768]{2,1,0:T(8,128)(2,1)}, u32[]{:S(2)}, u32[]{:S(2)}) collective-permute-start(bf16[2,384,768]{2,1,0:T(8,128)(2,1)S(1)} %pad_maximum_fusion.5), channel_id=1, source_target_pairs={{0,4},{2,6},{4,0},{6,2},{8,12},{10,14},{12,8},{14,10},{16,20},{18,... | collective-permute-start | bytes 3538952 | tf_op jit(solution)/shard_map/ppermute | solution.py:563
  261.5 26.4 %collective-permute-start.41 = (bf16[2,2,1,384,768]{4,3,2,1,0:T(8,128)(2,1)}, bf16[2,2,1,384,768]{4,3,2,1,0:T(8,128)(2,1)S(1)}, u32[]{:S(2)}, u32[]{:S(2)}) collective-permute-start(bf16[2,2,1,384,768]{4,3,2,1,0:T(8,128)(2,1)} %get-tuple-element.143), channel_id=1, source_target_pairs={{0,2},{2,0},{4,6},{6,4},{8,10},{10,8},{12,14},{14,12},{16,18},{18,... | collective-permute-start | bytes 7077896 | tf_op jit(solution)/shard_map/ppermute | solution.py:566
  272.4 19.7 %collective-permute-start.51 = (bf16[1,384,768]{2,1,0:T(8,128)(2,1)S(1)}, bf16[1,384,768]{2,1,0:T(8,128)(2,1)S(1)}, u32[]{:S(2)}, u32[]{:S(2)}) collective-permute-start(bf16[1,384,768]{2,1,0:T(8,128)(2,1)S(1)} %pad_maximum_fusion.8), channel_id=1, source_target_pairs={{0,1},{1,0},{2,3},{3,2},{4,5},{5,4},{6,7},{7,6},{8,9},{9,8},{10,11... | collective-permute-start | bytes 1769480 | tf_op jit(solution)/shard_map/ppermute | solution.py:560
  282.1 20.1 %collective-permute-start.58 = (bf16[384,768]{1,0:T(8,128)(2,1)S(1)}, bf16[384,768]{1,0:T(8,128)(2,1)S(1)}, u32[]{:S(2)}, u32[]{:S(2)}) collective-permute-start(bf16[384,768]{1,0:T(8,128)(2,1)S(1)} %get-tuple-element.178), channel_id=1, source_target_pairs={{24,16},{26,18},{28,20},{30,22},{0,8},{2,10},{4,12},{6,14},{25,17}... | collective-permute-start | bytes 1769480 | tf_op jit(solution)/shard_map/ppermute | solution.py:571
  286.6 24.1 %collective-permute-start.60 = (bf16[384,768]{1,0:T(8,128)(2,1)S(1)}, bf16[384,768]{1,0:T(8,128)(2,1)S(1)}, u32[]{:S(2)}, u32[]{:S(2)}) collective-permute-start(bf16[384,768]{1,0:T(8,128)(2,1)S(1)} %get-tuple-element.179), channel_id=1, source_target_pairs={{16,24},{18,26},{20,28},{22,30},{0,8},{2,10},{4,12},{6,14},{17,25}... | collective-permute-start | bytes 1769480 | tf_op jit(solution)/shard_map/ppermute | solution.py:571
  294.4 22.6 %collective-permute-start.54 = (bf16[384,768]{1,0:T(8,128)(2,1)S(1)}, bf16[384,768]{1,0:T(8,128)(2,1)S(1)}, u32[]{:S(2)}, u32[]{:S(2)}) collective-permute-start(bf16[384,768]{1,0:T(8,128)(2,1)S(1)} %bitcast_convert_fusion), channel_id=1, source_target_pairs={{0,8},{2,10},{4,12},{6,14},{24,16},{26,18},{28,20},{30,22},{1,9},{... | collective-permute-start | bytes 1769480 | tf_op jit(solution)/shard_map/ppermute | solution.py:571
  299.2 31.3 %collective-permute-start.42 = (bf16[2,8,32,768]{3,2,1,0:T(8,128)(2,1)S(1)}, bf16[2,8,32,768]{3,2,1,0:T(8,128)(2,1)S(1)}, u32[]{:S(2)}, u32[]{:S(2)}) collective-permute-start(bf16[2,8,32,768]{3,2,1,0:T(8,128)(2,1)S(1)} %copy-done.59), channel_id=1, source_target_pairs={{0,2},{2,4},{4,6},{6,8},{8,10},{10,12},{12,14},{14,16},{16,18},{18... | collective-permute-start | bytes 2359304 | tf_op jit(solution)/shard_map/ppermute | solution.py:788
  300.7 31.1 %collective-permute-start.43 = (bf16[2,8,32,768]{3,2,1,0:T(8,128)(2,1)S(1)}, bf16[2,8,32,768]{3,2,1,0:T(8,128)(2,1)S(1)}, u32[]{:S(2)}, u32[]{:S(2)}) collective-permute-start(bf16[2,8,32,768]{3,2,1,0:T(8,128)(2,1)S(1)} %copy-done.58), channel_id=1, source_target_pairs={{2,0},{4,2},{6,4},{8,6},{10,8},{12,10},{14,12},{16,14},{18,16},{20... | collective-permute-start | bytes 2359304 | tf_op jit(solution)/shard_map/ppermute | solution.py:788
  302.2 17.5 %collective-permute-start.45 = (bf16[1,384,768]{2,1,0:T(8,128)(2,1)S(1)}, bf16[1,384,768]{2,1,0:T(8,128)(2,1)S(1)}, u32[]{:S(2)}, u32[]{:S(2)}) collective-permute-start(bf16[1,384,768]{2,1,0:T(8,128)(2,1)S(1)} %pad_maximum_fusion.6), channel_id=1, source_target_pairs={{0,1},{1,0},{2,3},{3,2},{4,5},{5,4},{6,7},{7,6},{8,9},{9,8},{10,11... | collective-permute-start | bytes 1769480 | tf_op jit(solution)/shard_map/ppermute | solution.py:560
  310.7 17.2 %collective-permute-start.47 = (bf16[1,384,768]{2,1,0:T(8,128)(2,1)S(1)}, bf16[1,384,768]{2,1,0:T(8,128)(2,1)S(1)}, u32[]{:S(2)}, u32[]{:S(2)}) collective-permute-start(bf16[1,384,768]{2,1,0:T(8,128)(2,1)S(1)} %pad_maximum_fusion.7), channel_id=1, source_target_pairs={{0,4},{2,6},{4,0},{6,2},{8,12},{10,14},{12,8},{14,10},{16,20},{18,... | collective-permute-start | bytes 1769480 | tf_op jit(solution)/shard_map/ppermute | solution.py:563
  317.0 60.1 %collective-permute-start.59 = (bf16[384,768]{1,0:T(8,128)(2,1)}, bf16[384,768]{1,0:T(8,128)(2,1)}, u32[]{:S(2)}, u32[]{:S(2)}) collective-permute-start(bf16[384,768]{1,0:T(8,128)(2,1)} %get-tuple-element.176), channel_id=1, source_target_pairs={{8,16},{10,18},{12,20},{14,22},{9,17},{11,19},{13,21},{15,23}} | collective-permute-start | bytes 1769480 | tf_op jit(solution)/shard_map/ppermute | solution.py:571
  319.8 57.3 %collective-permute-start.61 = (bf16[384,768]{1,0:T(8,128)(2,1)}, bf16[384,768]{1,0:T(8,128)(2,1)}, u32[]{:S(2)}, u32[]{:S(2)}) collective-permute-start(bf16[384,768]{1,0:T(8,128)(2,1)} %get-tuple-element.177), channel_id=1, source_target_pairs={{8,24},{10,26},{12,28},{14,30},{9,25},{11,27},{13,29},{15,31}} | collective-permute-start | bytes 1769480 | tf_op jit(solution)/shard_map/ppermute | solution.py:571
  327.9 49.2 %collective-permute-start.55 = (bf16[384,768]{1,0:T(8,128)(2,1)}, bf16[384,768]{1,0:T(8,128)(2,1)}, u32[]{:S(2)}, u32[]{:S(2)}) collective-permute-start(bf16[384,768]{1,0:T(8,128)(2,1)} %fusion.10), channel_id=1, source_target_pairs={{16,8},{18,10},{20,12},{22,14},{17,9},{19,11},{21,13},{23,15}} | collective-permute-start | bytes 1769480 | tf_op jit(solution)/shard_map/ppermute | solution.py:571
  330.5 21.2 %collective-permute-start.48 = (bf16[384,768]{1,0:T(8,128)(2,1)}, bf16[384,768]{1,0:T(8,128)(2,1)}, u32[]{:S(2)}, u32[]{:S(2)}) collective-permute-start(bf16[384,768]{1,0:T(8,128)(2,1)} %bitcast_convert_fusion.1), channel_id=1, source_target_pairs={{8,0},{10,2},{12,4},{14,6},{24,16},{26,18},{28,20},{30,22},{9,1},{... | collective-permute-start | bytes 1769480 | tf_op jit(solution)/shard_map/ppermute | solution.py:571
  354.7 22.4 %collective-permute-start.49 = (bf16[384,768]{1,0:T(8,128)(2,1)}, bf16[384,768]{1,0:T(8,128)(2,1)}, u32[]{:S(2)}, u32[]{:S(2)}) collective-permute-start(bf16[384,768]{1,0:T(8,128)(2,1)} %fusion.9), channel_id=1, source_target_pairs={{16,0},{18,2},{20,4},{22,6},{17,1},{19,3},{21,5},{23,7}} | collective-permute-start | bytes 1769480 | tf_op jit(solution)/shard_map/ppermute | solution.py:571
  (100 other events, 920.3 us)
